TPU v7x, 256 devices: a whole 4x4x8 slice. The times are simulated.
256 devices in a mesh: ctx: 16 (over z, core), exp: 16 (over y, x).
Axes of the slice: x: 4, y: 4, z: 8, core: 2. Of those that a mesh axis runs over, the one named last changes fastest.
Arguments:
- u_in: bfloat16 [2048, 16384], P('ctx', 'exp'), may hold values from -6 to 6
- z_in: bfloat16 [2048, 16384], P('ctx', 'exp'), may hold values from -6 to 6
- delta: float32 [2048, 16384], P('ctx', 'exp'), may hold values from 0.25 to 2
- bc_proj: float32 [32, 2048], P(None, 'ctx'), may hold values from -0.6 to 0.6
- a_rate: float32 [16, 16384], P(None, 'exp'), may hold values from 9.765625e-07 to 0.2
- d_skip: float32 [16384], P('exp'), may hold values from 0.5 to 1.5
- w_out: bfloat16 [16384, 8192], P('exp', 'ctx'), may hold values from -0.046875 to 0.046875
Outputs:
- mixer_out: bfloat16 [2048, 8192], P('exp', 'ctx')
All inputs are finite; a program needn't handle non-finite values.
Results may differ from a plain program's by a relative error of at most 0.0048.
Values may be sent and summed in bfloat16 or wider, within the bound.
No kernel may reach another device: no remote copies, remote signals or barrier semaphores. Data moves between devices by JAX's collectives and lax.ppermute only.
A program may use at most 128 MiB of HBM per device.

v0:
```python
import functools
import math

import jax
import jax.numpy as jnp
from jax import lax
from jax.experimental import pallas as pl
from jax.experimental.pallas import tpu as pltpu
from jax.sharding import PartitionSpec as P

LANES = 128
SUB = 8
NEG_LOG2E = -math.log2(math.e)


def fill_transposed(dst, rows, groups, make):
    for g in range(groups):
        dst[pl.ds(g, rows, stride=groups), :] = make(g)


def fill_coefficients(dst, bc, rows, count):
    turned = bc.T
    for n in range(count):
        dst[pl.ds(n, rows, stride=count), :] = jnp.broadcast_to(
            turned[:, n : n + 1], (rows, LANES)
        )


def end_state_kernel(delta_ref, u_ref, bc_ref, a_ref, out_ref, d_t, w_t, b_t):
    rows, channels = delta_ref.shape
    groups = channels // LANES
    states = a_ref.shape[0] // groups

    def lanes(g):
        return slice(g * LANES, (g + 1) * LANES)

    fill_transposed(d_t, rows, groups, lambda g: delta_ref[:, lanes(g)])
    fill_transposed(
        w_t,
        rows,
        groups,
        lambda g: delta_ref[:, lanes(g)] * u_ref[:, lanes(g)].astype(jnp.float32),
    )
    fill_coefficients(b_t, bc_ref[:states, :], rows, states)
    rate = [a_ref[n * groups : (n + 1) * groups, :] * NEG_LOG2E for n in range(states)]

    def step(t, carry):
        total, state = carry
        d = d_t[pl.ds(pl.multiple_of(t * groups, groups), groups), :]
        w = w_t[pl.ds(pl.multiple_of(t * groups, groups), groups), :]
        new = []
        for n in range(states):
            b = b_t[pl.ds(t * states + n, groups, stride=0), :]
            new.append(jnp.exp2(d * rate[n]) * state[n] + w * b)
        return total + d, tuple(new)

    zero = jnp.zeros((groups, LANES), jnp.float32)
    total, state = lax.fori_loop(0, rows, step, (zero, (zero,) * states), unroll=4)
    for n in range(states):
        out_ref[n * groups : (n + 1) * groups, :] = state[n]
    out_ref[states * groups : (states + 1) * groups, :] = total


def gated_kernel(
    index_ref, delta_ref, u_ref, z_ref, bc_ref, a_ref, skip_ref, ends_ref, out_ref,
    d_t, w_t, bc_t, y_t,
):
    rows, channels = delta_ref.shape
    groups = channels // LANES
    states = a_ref.shape[0] // groups
    block = (states + 1) * groups

    def lanes(g):
        return slice(g * LANES, (g + 1) * LANES)

    fill_transposed(d_t, rows, groups, lambda g: delta_ref[:, lanes(g)])
    fill_transposed(
        w_t,
        rows,
        groups,
        lambda g: delta_ref[:, lanes(g)] * u_ref[:, lanes(g)].astype(jnp.float32),
    )
    fill_coefficients(bc_t, bc_ref[...], rows, 2 * states)
    rate = [a_ref[n * groups : (n + 1) * groups, :] * NEG_LOG2E for n in range(states)]

    def carry_in(k, state):
        base = pl.multiple_of(k * block, groups)
        total = ends_ref[pl.ds(base + states * groups, groups), :]
        return tuple(
            jnp.exp2(total * rate[n]) * state[n] + ends_ref[pl.ds(base + n * groups, groups), :]
            for n in range(states)
        )

    zero = jnp.zeros((groups, LANES), jnp.float32)
    start = lax.fori_loop(0, index_ref[0], carry_in, (zero,) * states)

    def step(t, state):
        d = d_t[pl.ds(pl.multiple_of(t * groups, groups), groups), :]
        w = w_t[pl.ds(pl.multiple_of(t * groups, groups), groups), :]
        new = []
        parts = [None] * 4
        for n in range(states):
            b = bc_t[pl.ds(t * 2 * states + n, groups, stride=0), :]
            c = bc_t[pl.ds(t * 2 * states + states + n, groups, stride=0), :]
            s = jnp.exp2(d * rate[n]) * state[n] + w * b
            new.append(s)
            term = s * c
            parts[n % 4] = term if parts[n % 4] is None else parts[n % 4] + term
        y_t[pl.ds(pl.multiple_of(t * groups, groups), groups), :] = (parts[0] + parts[1]) + (
            parts[2] + parts[3]
        )
        return tuple(new)

    lax.fori_loop(0, rows, step, start, unroll=4)

    for g in range(groups):
        y = y_t[pl.ds(g, rows, stride=groups), :]
        u = u_ref[:, lanes(g)].astype(jnp.float32)
        z = z_ref[:, lanes(g)].astype(jnp.float32)
        mixed = y + skip_ref[:, lanes(g)] * u
        out_ref[:, lanes(g)] = (mixed * (z / (1.0 + jnp.exp(-z)))).astype(jnp.bfloat16)


def whole():
    return pl.BlockSpec(memory_space=pltpu.VMEM)


def body(u_in, z_in, delta, bc_proj, a_rate, d_skip, w_out):
    rows, channels = u_in.shape
    states = a_rate.shape[0]
    groups = channels // LANES
    a_flat = a_rate.reshape(states * groups, LANES)
    flat = pltpu.VMEM((rows * groups, LANES), jnp.float32)

    ends = pl.pallas_call(
        end_state_kernel,
        out_shape=jax.ShapeDtypeStruct(((states + 1) * groups, LANES), jnp.float32),
        in_specs=[whole()] * 4,
        out_specs=whole(),
        scratch_shapes=[flat, flat, pltpu.VMEM((rows * states, LANES), jnp.float32)],
        name="end_state",
    )(delta, u_in, bc_proj, a_flat)
    all_ends = lax.all_gather(ends, "ctx", axis=0, tiled=True)
    index = lax.axis_index("ctx").astype(jnp.int32).reshape(1)
    gated = pl.pallas_call(
        gated_kernel,
        out_shape=jax.ShapeDtypeStruct((rows, channels), jnp.bfloat16),
        in_specs=[pl.BlockSpec(memory_space=pltpu.SMEM)] + [whole()] * 7,
        out_specs=whole(),
        scratch_shapes=[flat, flat, pltpu.VMEM((rows * 2 * states, LANES), jnp.float32), flat],
        name="gated",
    )(index, delta, u_in, z_in, bc_proj, a_flat, d_skip.reshape(1, channels), all_ends)

    terms = jnp.dot(
        lax.all_gather(gated, "ctx", axis=0, tiled=True), w_out, preferred_element_type=jnp.float32
    ).astype(jnp.bfloat16)
    count = lax.axis_size("exp")
    terms = terms.reshape(count, terms.shape[0] // count, terms.shape[1])
    received = lax.all_to_all(terms, "exp", split_axis=0, concat_axis=0)
    return jnp.sum(received.astype(jnp.float32), axis=0).astype(jnp.bfloat16)


def solution(mesh):
    return jax.shard_map(
        body,
        mesh=mesh,
        in_specs=(
            P("ctx", "exp"),
            P("ctx", "exp"),
            P("ctx", "exp"),
            P(None, "ctx"),
            P(None, "exp"),
            P("exp"),
            P("exp", "ctx"),
        ),
        out_specs=P("exp", "ctx"),
        check_vma=False,
    )
```

profile of v0, /device:TPU:1, one launch (start us, length us, event | category | flops | bytes accessed | tf_op | source)
XLA Modules:
  0.0 150.1 jit_solution(15042662819552126392)
XLA Ops:
  6.5 0.0 copy-start
  6.5 0.0 all-gather.3.cloned.1.call-start
  6.5 1.6 %reshape.13.a_ref = f32[128,128]{1,0:T(8,128)} reshape(f32[16,1024]{1,0:T(8,128)} %param.11) | data formatting | bytes 131072 | tf_op jit(solution)/shard_map/reshape | solution.py:132
  8.1 4.3 %end_state.1 = f32[136,128]{1,0:T(8,128)} custom-call(f32[128,1024]{1,0:T(8,128)} %delta_ref.3, bf16[128,1024]{1,0:T(8,128)(2,1)} %u_ref.3, f32[32,128]{1,0:T(8,128)} %bc_ref.3, f32[128,128]{1,0:T(8,128)} %reshape.13.a_ref), custom_call_target="tpu_custom_call" | custom-call | tf_op jit(solution)/shard_map/end_state/pallas_call | solution.py:135
  12.4 0.0 all-gather.3.cloned.1.call-update
  12.5 0.0 all-gather.5.cloned.1.call-start
  12.5 43.1 %all-gather.3.cloned.1.call-done.ends_ref = f32[2176,128]{1,0:T(8,128)} async-done(((f32[136,128]{1,0:T(8,128)}), f32[2176,128]{1,0:T(8,128)}) %all-gather.3.cloned.1.call-update) | async-done | bytes 1114128 | tf_op jit(solution)/shard_map/all_gather | solution.py:143
  55.6 7.0 %gated.1 = bf16[128,1024]{1,0:T(8,128)(2,1)} custom-call(s32[1]{0:T(128)} %bitcast.index_ref, f32[128,1024]{1,0:T(8,128)} %delta_ref.3, bf16[128,1024]{1,0:T(8,128)(2,1)} %u_ref.3, bf16[128,1024]{1,0:T(8,128)(2,1)} %z_ref.1, f32[32,128]{1,0:T(8,128)} %bc_ref.3, f32[128,128]{1,0:T(8,128)} %reshape.13.a_ref, f32[1,1024]{1,0:T(1,128)} %bitcast.6, ...), custom_call_target="tpu_custom_call" | custom-call | tf_op jit(solution)/shard_map/gated/pallas_call | solution.py:145
  62.6 0.0 all-gather.5.cloned.1.call-update
  62.6 41.1 %all-gather.5.cloned.1.call-done = bf16[2048,1024]{1,0:T(8,128)(2,1)} async-done(((bf16[128,1024]{1,0:T(8,128)(2,1)}), bf16[2048,1024]{1,0:T(8,128)(2,1)}) %all-gather.5.cloned.1.call-update) | async-done | bytes 4194320 | tf_op jit(solution)/shard_map/all_gather | solution.py:155
  103.7 0.0 copy-done
  103.7 4.5 %convolution_convert_fusion = bf16[2048,512]{1,0:T(8,128)(2,1)S(1)} fusion(bf16[2048,1024]{1,0:T(8,128)(2,1)} %all-gather.5.cloned.1.call-done, bf16[1024,512]{1,0:T(8,128)(2,1)S(1)} %copy-done), kind=kOutput, calls=%fused_computation | convolution fusion | flops 2148532224 | bytes 7340032 | tf_op jit(solution)/shard_map/dot_general | solution.py:154
  108.3 34.0 %all_to_all.5 = bf16[16,128,512]{2,1,0:T(8,128)(2,1)S(1)} all-to-all(bf16[16,128,512]{2,1,0:T(8,128)(2,1)S(1)} %bitcast.5), channel_id=1, replica_groups=mesh['ctx'=16,'exp'=16] {'exp'}, dimensions={0} | all-to-all | bytes 4194304 | tf_op jit(solution)/shard_map/all_to_all | solution.py:159
  142.3 1.0 reduce_sum.12
Async XLA Ops:
  6.5 97.2 %copy-start = (bf16[1024,512]{1,0:T(8,128)(2,1)S(1)}, bf16[1024,512]{1,0:T(8,128)(2,1)}, u32[]{:S(2)}) copy-start(bf16[1024,512]{1,0:T(8,128)(2,1)} %param.13) | copy-start | bytes 3145732
  6.5 49.1 %all-gather.3.cloned.1.call-start = ((), (), s32[]{:S(2)}) async-start(), calls=%async_computation.1 | async-start | bytes 1183744 | tf_op jit(solution)/shard_map/all_gather | solution.py:143
  12.5 91.3 %all-gather.5.cloned.1.call-start = ((), (), s32[]{:S(2)}) async-start(), calls=%async_computation.2 | async-start | bytes 4456448 | tf_op jit(solution)/shard_map/all_gather | solution.py:155
Sparse Core Ops, SparseCore 0:
  12.6 42.9 all-gather.2
  62.8 40.9 all-gather.4
where the time goes:
time: 150 us
  waiting for transfers between devices  84.2 us (56%)
  blocking collectives  34 us (23%)
  between operations  13.4 us (9%)
  Pallas kernels  11.4 us (8%)
  matrix products  4.52 us (3%)
  local copies, waits for them, and re-layouts  1.57 us (1%)
    all_gather x1, waiting for transfers between devices, body(): all_ends = lax.all_gather(ends, 'ctx', axis=0, tiled=True)  43.1 us
    all_gather x1, waiting for transfers between devices, body(): lax.all_gather(gated, 'ctx', axis=0, tiled=True)  41.1 us
    all_to_all x1, blocking collectives, body(): received = lax.all_to_all(terms, 'exp', split_axis=0, concat_axis=0)  34 us
    pallas_call x1, Pallas kernels, body(): pl.pallas_call(gated_kernel, out_shape=jax.ShapeDtypeStruct((rows, channe...  7.02 us
    dot_general x1, matrix products, body(): jnp.dot(lax.all_gather(gated, 'ctx', axis=0, tiled=True), w_out, preferre...  4.52 us
    pallas_call x1, Pallas kernels, body(): pl.pallas_call(end_state_kernel, out_shape=jax.ShapeDtypeStruct(((states...  4.34 us
  transfers between devices with their start and end apart: 2, of which 2 were waited for; matrix products, arithmetic and copies ran while one was open for 0% of the time, Pallas kernels for 0%

commit v1 on v0

--- a/solution.py
+++ b/solution.py
@@ -61,14 +61,30 @@
     out_ref[states * groups : (states + 1) * groups, :] = total
 
 
+def combine_kernel(own_ref, one_ref, two_ref, three_ref, a_ref, before_ref, through_ref):
+    groups = SUB
+    states = a_ref.shape[0] // groups
+    last = slice(states * groups, (states + 1) * groups)
+    for n in range(states):
+        at = slice(n * groups, (n + 1) * groups)
+        rate = a_ref[at, :] * NEG_LOG2E
+        state = three_ref[at, :]
+        for part in (two_ref, one_ref):
+            state = jnp.exp2(part[last, :] * rate) * state + part[at, :]
+        before_ref[at, :] = state
+        through_ref[at, :] = jnp.exp2(own_ref[last, :] * rate) * state + own_ref[at, :]
+    before = one_ref[last, :] + two_ref[last, :] + three_ref[last, :]
+    before_ref[last, :] = before
+    through_ref[last, :] = before + own_ref[last, :]
+
+
 def gated_kernel(
-    index_ref, delta_ref, u_ref, z_ref, bc_ref, a_ref, skip_ref, ends_ref, out_ref,
+    delta_ref, u_ref, z_ref, bc_ref, a_ref, skip_ref, p3_ref, p2_ref, p1_ref, p0_ref, out_ref,
     d_t, w_t, bc_t, y_t,
 ):
     rows, channels = delta_ref.shape
     groups = channels // LANES
     states = a_ref.shape[0] // groups
-    block = (states + 1) * groups
 
     def lanes(g):
         return slice(g * LANES, (g + 1) * LANES)
@@ -83,16 +99,14 @@
     fill_coefficients(bc_t, bc_ref[...], rows, 2 * states)
     rate = [a_ref[n * groups : (n + 1) * groups, :] * NEG_LOG2E for n in range(states)]
 
-    def carry_in(k, state):
-        base = pl.multiple_of(k * block, groups)
-        total = ends_ref[pl.ds(base + states * groups, groups), :]
-        return tuple(
-            jnp.exp2(total * rate[n]) * state[n] + ends_ref[pl.ds(base + n * groups, groups), :]
-            for n in range(states)
-        )
-
-    zero = jnp.zeros((groups, LANES), jnp.float32)
-    start = lax.fori_loop(0, index_ref[0], carry_in, (zero,) * states)
+    last = slice(states * groups, (states + 1) * groups)
+    start = []
+    for n in range(states):
+        at = slice(n * groups, (n + 1) * groups)
+        state = p3_ref[at, :]
+        for part in (p2_ref, p1_ref, p0_ref):
+            state = jnp.exp2(part[last, :] * rate[n]) * state + part[at, :]
+        start.append(state)
 
     def step(t, state):
         d = d_t[pl.ds(pl.multiple_of(t * groups, groups), groups), :]
@@ -111,7 +125,7 @@
         )
         return tuple(new)
 
-    lax.fori_loop(0, rows, step, start, unroll=4)
+    lax.fori_loop(0, rows, step, tuple(start), unroll=4)
 
     for g in range(groups):
         y = y_t[pl.ds(g, rows, stride=groups), :]
@@ -125,39 +139,146 @@
     return pl.BlockSpec(memory_space=pltpu.VMEM)
 
 
+def project_kernel(count, place_ref, *refs):
+    blocks, w_ref, outs, terms = refs[:count], refs[count], refs[count + 1 : -1], refs[-1]
+    rows = blocks[0].shape[0]
+    half = rows // 2
+    me, x, y = place_ref[0], place_ref[1], place_ref[2]
+    partner = me + 1 - 2 * lax.rem(me, 2)
+    chips = count // 2
+    for side, base in ((0, me), (1, partner)):
+        for o in range(chips):
+            k = lax.rem(base + 2 * o, count)
+            at = pl.multiple_of(k * rows, rows)
+            terms[pl.ds(at, rows), :] = jnp.dot(
+                blocks[side * chips + o][...], w_ref[...], preferred_element_type=jnp.float32
+            ).astype(jnp.bfloat16)
+    for d in range(4):
+        for m in range(4):
+            for part, k in ((0, m * 4 + lax.rem(x + d, 4)), (1, lax.rem(y + d, 4) * 4 + m)):
+                at = pl.multiple_of(k * rows + part * half, half)
+                outs[part * 4 + d][m * half : (m + 1) * half, :] = terms[pl.ds(at, half), :]
+
+
+def middle_kernel(place_ref, *refs):
+    ins, outs, total = refs[:8], refs[8:16], refs[16]
+    half = outs[0].shape[0]
+    for part in range(2):
+        mine = place_ref[2 - part]
+        total[...] = sum(ref[...].astype(jnp.float32) for ref in ins[part * 4 : part * 4 + 4])
+        for d in range(4):
+            at = pl.multiple_of(lax.rem(mine + d, 4) * half, half)
+            out = outs[part * 4 + d]
+            out[...] = total[pl.ds(at, half), :].astype(out.dtype)
+
+
+def final_kernel(*refs):
+    ins, out_ref = refs[:8], refs[8]
+    half = ins[0].shape[0]
+    for part in range(2):
+        out_ref[part * half : (part + 1) * half, :] = sum(
+            ref[...].astype(jnp.float32) for ref in ins[part * 4 : part * 4 + 4]
+        ).astype(out_ref.dtype)
+
+
 def body(u_in, z_in, delta, bc_proj, a_rate, d_skip, w_out):
     rows, channels = u_in.shape
     states = a_rate.shape[0]
     groups = channels // LANES
+    width = w_out.shape[1]
+    count = lax.axis_size("ctx")
     a_flat = a_rate.reshape(states * groups, LANES)
     flat = pltpu.VMEM((rows * groups, LANES), jnp.float32)
+    pair = jax.ShapeDtypeStruct(((states + 1) * groups, LANES), jnp.float32)
+    smem = pl.BlockSpec(memory_space=pltpu.SMEM)
+    me = lax.axis_index("ctx").astype(jnp.int32)
+    spot = lax.axis_index("exp").astype(jnp.int32)
+    place = jnp.stack([me, spot % 4, spot // 4])
 
     ends = pl.pallas_call(
         end_state_kernel,
-        out_shape=jax.ShapeDtypeStruct(((states + 1) * groups, LANES), jnp.float32),
+        out_shape=pair,
         in_specs=[whole()] * 4,
         out_specs=whole(),
         scratch_shapes=[flat, flat, pltpu.VMEM((rows * states, LANES), jnp.float32)],
         name="end_state",
     )(delta, u_in, bc_proj, a_flat)
-    all_ends = lax.all_gather(ends, "ctx", axis=0, tiled=True)
-    index = lax.axis_index("ctx").astype(jnp.int32).reshape(1)
+
+    def onward(value, shift):
+        return lax.ppermute(value, "ctx", [(i, i + shift) for i in range(count - shift)])
+
+    before, through = pl.pallas_call(
+        combine_kernel,
+        out_shape=(pair, pair),
+        in_specs=[whole()] * 5,
+        out_specs=(whole(), whole()),
+        name="combine",
+    )(ends, onward(ends, 1), onward(ends, 2), onward(ends, 3), a_flat)
     gated = pl.pallas_call(
         gated_kernel,
         out_shape=jax.ShapeDtypeStruct((rows, channels), jnp.bfloat16),
-        in_specs=[pl.BlockSpec(memory_space=pltpu.SMEM)] + [whole()] * 7,
+        in_specs=[whole()] * 10,
         out_specs=whole(),
         scratch_shapes=[flat, flat, pltpu.VMEM((rows * 2 * states, LANES), jnp.float32), flat],
         name="gated",
-    )(index, delta, u_in, z_in, bc_proj, a_flat, d_skip.reshape(1, channels), all_ends)
-
-    terms = jnp.dot(
-        lax.all_gather(gated, "ctx", axis=0, tiled=True), w_out, preferred_element_type=jnp.float32
-    ).astype(jnp.bfloat16)
-    count = lax.axis_size("exp")
-    terms = terms.reshape(count, terms.shape[0] // count, terms.shape[1])
-    received = lax.all_to_all(terms, "exp", split_axis=0, concat_axis=0)
-    return jnp.sum(received.astype(jnp.float32), axis=0).astype(jnp.bfloat16)
+    )(
+        delta, u_in, z_in, bc_proj, a_flat, d_skip.reshape(1, channels),
+        onward(through, 12), onward(through, 8), onward(through, 4), before,
+    )
+
+    def chip_step(value, way):
+        return lax.ppermute(value, "ctx", [(i, (i + 2 * way) % count) for i in range(count)])
+
+    def swap(value):
+        return lax.ppermute(value, "ctx", [(i, i ^ 1) for i in range(count)])
+
+    chips = count // 2
+    held = [None] * chips
+    held[0] = gated
+    for s in range(1, chips // 2 + 1):
+        held[(chips - s) % chips] = chip_step(held[(chips - s + 1) % chips], 1)
+        if s < chips - s:
+            held[s] = chip_step(held[s - 1], -1)
+    blocks = held + [swap(value) for value in held]
+
+    half = rows // 2
+    quarter = jax.ShapeDtypeStruct((4 * half, width), jnp.bfloat16)
+    sent = pl.pallas_call(
+        functools.partial(project_kernel, count),
+        out_shape=(quarter,) * 8,
+        in_specs=[smem] + [whole()] * (count + 1),
+        out_specs=(whole(),) * 8,
+        scratch_shapes=[pltpu.VMEM((rows * count, width), jnp.bfloat16)],
+        name="project",
+    )(place, *blocks, w_out)
+
+    def across(value, dx, dy):
+        pairs = [
+            (y * 4 + x, (y + dy) % 4 * 4 + (x + dx) % 4) for y in range(4) for x in range(4)
+        ]
+        return lax.ppermute(value, "exp", pairs)
+
+    got = [sent[0]] + [across(sent[d], d, 0) for d in range(1, 4)]
+    got += [sent[4]] + [across(sent[4 + d], 0, d) for d in range(1, 4)]
+    one = jax.ShapeDtypeStruct((half, width), jnp.bfloat16)
+    kept = jax.ShapeDtypeStruct((half, width), jnp.float32)
+    sent = pl.pallas_call(
+        middle_kernel,
+        out_shape=(kept, one, one, one) * 2,
+        in_specs=[smem] + [whole()] * 8,
+        out_specs=(whole(),) * 8,
+        scratch_shapes=[pltpu.VMEM((4 * half, width), jnp.float32)],
+        name="middle",
+    )(place, *got)
+    got = [sent[0]] + [across(sent[d], 0, d) for d in range(1, 4)]
+    got += [sent[4]] + [across(sent[4 + d], d, 0) for d in range(1, 4)]
+    return pl.pallas_call(
+        final_kernel,
+        out_shape=jax.ShapeDtypeStruct((rows, width), jnp.bfloat16),
+        in_specs=[whole()] * 8,
+        out_specs=whole(),
+        name="final",
+    )(*got)
 
 
 def solution(mesh):

time: 150 us -> 125 us (0.83); the launches traced: 150 us -> 123 us
  starting transfers between devices: 0.04 us -> 63.5 us
  waiting for transfers between devices: 84.2 us -> 30.6 us
  blocking collectives: 34 us -> 0 us
  between operations: 13.4 us -> 0.32 us
  Pallas kernels: 11.4 us -> 23.5 us
  matrix products: 4.52 us -> 0 us
  local copies, waits for them, and re-layouts: 1.57 us -> 4.34 us
    all_gather x2 -> x0, waiting for transfers between devices: 84.2 us -> none  [the longest x1 43.1 us: body(): all_ends = lax.all_gather(ends, 'ctx', axis=0, tiled=True)]
    ppermute x0 -> x33, starting transfers between devices: none -> 63.5 us  [the longest x6 22.6 us: onward(): lax.ppermute(value, 'ctx', [(i, i + shift) for i in range(count - shift)])]
    all_to_all x1 -> x0, blocking collectives: 34 us -> none  [body(): received = lax.all_to_all(terms, 'exp', split_axis=0, concat_axis=0)]
    ppermute x0 -> x33, waiting for transfers between devices: none -> 30.6 us  [the longest x7 12.7 us: chip_step(): lax.ppermute(value, 'ctx', [(i, (i + 2 * way) % count) for i in range(cou...]
    pallas_call x1 -> x5, Pallas kernels: 4.34 us -> 16.7 us  [the longest x1 6.2 us: body(): pl.pallas_call(functools.partial(project_kernel, count), out_shape=(quart...]
    dot_general x1 -> x0, matrix products: 4.52 us -> none  [body(): jnp.dot(lax.all_gather(gated, 'ctx', axis=0, tiled=True), w_out, preferre...]
    unnamed x2 -> x62, local copies, waits for them, and re-layouts: 0.01 us -> 2.87 us
  transfers between devices with their start and end apart: 2 -> 33, of which waited for: 2 -> 15; matrix products, arithmetic and copies ran while one was open for 0% -> 1% of each run, Pallas kernels for 0% -> 0%
where the time goes in v1:
time: 125 us; the launch traced here: 123 us
  starting transfers between devices  63.5 us (51%)
  waiting for transfers between devices  30.6 us (24%)
  Pallas kernels  23.5 us (19%)
  local copies, waits for them, and re-layouts  4.34 us (3%)
    ppermute x6, starting transfers between devices, onward(): lax.ppermute(value, 'ctx', [(i, i + shift) for i in range(count - shift)])  22.6 us
    ppermute x12, starting transfers between devices, across(): return lax.ppermute(value, 'exp', pairs)  19.9 us
    ppermute x8, starting transfers between devices, swap(): return lax.ppermute(value, 'ctx', [(i, i ^ 1) for i in range(count)])  12.7 us
    ppermute x7, waiting for transfers between devices, chip_step(): lax.ppermute(value, 'ctx', [(i, (i + 2 * way) % count) for i in range(cou...  12.7 us
    ppermute x12, waiting for transfers between devices, across(): return lax.ppermute(value, 'exp', pairs)  11.3 us
    ppermute x7, starting transfers between devices, chip_step(): lax.ppermute(value, 'ctx', [(i, (i + 2 * way) % count) for i in range(cou...  8.32 us
    pallas_call x1, Pallas kernels, body(): pl.pallas_call(gated_kernel, out_shape=jax.ShapeDtypeStruct((rows, channe...  6.71 us
    pallas_call x1, Pallas kernels, body(): pl.pallas_call(functools.partial(project_kernel, count), out_shape=(quart...  6.2 us
  transfers between devices with their start and end apart: 33, of which 15 were waited for; matrix products, arithmetic and copies ran while one was open for 1% of the time, Pallas kernels for 0%

profile of v1, /device:TPU:1, one launch (start us, length us, event | category | flops | bytes accessed | tf_op | source)
XLA Modules:
  0.0 122.9 jit_solution(11401296423685314112)
XLA Ops:
  1.5 4.3 %end_state.1.own_ref = f32[136,128]{1,0:T(8,128)} custom-call(f32[128,1024]{1,0:T(8,128)} %delta_ref.3, bf16[128,1024]{1,0:T(8,128)(2,1)} %u_ref.3, f32[32,128]{1,0:T(8,128)} %bc_ref.3, f32[128,128]{1,0:T(8,128)} %reshape.6.a_ref), custom_call_target="tpu_custom_call" | custom-call | tf_op jit(solution)/shard_map/end_state/pallas_call | solution.py:198
  5.8 6.3 %collective-permute-start.2 = (f32[136,128]{1,0:T(8,128)}, f32[136,128]{1,0:T(8,128)S(1)}, u32[]{:S(2)}, u32[]{:S(2)}) collective-permute-start(f32[136,128]{1,0:T(8,128)} %end_state.1.own_ref), channel_id=1, source_target_pairs={{0,48},{16,64},{32,80},{48,96},{64,112},{80,128},{96,144},{112,160... | collective-permute-start | bytes 208904 | tf_op jit(solution)/shard_map/ppermute | solution.py:208
  12.1 3.5 %collective-permute-start.1 = (f32[136,128]{1,0:T(8,128)}, f32[136,128]{1,0:T(8,128)S(1)}, u32[]{:S(2)}, u32[]{:S(2)}) collective-permute-start(f32[136,128]{1,0:T(8,128)} %end_state.1.own_ref), channel_id=1, source_target_pairs={{0,32},{16,48},{32,64},{48,80},{64,96},{80,112},{96,128},{112,144}... | collective-permute-start | bytes 208904 | tf_op jit(solution)/shard_map/ppermute | solution.py:208
  15.7 2.2 %collective-permute-start = (f32[136,128]{1,0:T(8,128)}, f32[136,128]{1,0:T(8,128)S(1)}, u32[]{:S(2)}, u32[]{:S(2)}) collective-permute-start(f32[136,128]{1,0:T(8,128)} %end_state.1.own_ref), channel_id=1, source_target_pairs={{0,16},{16,32},{32,48},{48,64},{64,80},{80,96},{96,112},{112,128},... | collective-permute-start | bytes 208904 | tf_op jit(solution)/shard_map/ppermute | solution.py:208
  21.8 5.2 %collective-permute-start.5 = (f32[136,128]{1,0:T(8,128)}, f32[136,128]{1,0:T(8,128)S(1)}, u32[]{:S(2)}, u32[]{:S(2)}) collective-permute-start(f32[136,128]{1,0:T(8,128)} %get-tuple-element.23), channel_id=1, source_target_pairs={{0,64},{16,80},{32,96},{48,112},{64,128},{80,144},{96,160},{112,17... | collective-permute-start | bytes 208904 | tf_op jit(solution)/shard_map/ppermute | solution.py:208
  27.0 4.1 %collective-permute-start.4 = (f32[136,128]{1,0:T(8,128)}, f32[136,128]{1,0:T(8,128)S(1)}, u32[]{:S(2)}, u32[]{:S(2)}) collective-permute-start(f32[136,128]{1,0:T(8,128)} %get-tuple-element.23), channel_id=1, source_target_pairs={{0,128},{16,144},{32,160},{48,176},{64,192},{80,208},{96,224},{112... | collective-permute-start | bytes 208904 | tf_op jit(solution)/shard_map/ppermute | solution.py:208
  32.8 4.0 %collective-permute-done.3.p3_ref = f32[136,128]{1,0:T(8,128)S(1)} collective-permute-done((f32[136,128]{1,0:T(8,128)}, f32[136,128]{1,0:T(8,128)S(1)}, u32[]{:S(2)}, u32[]{:S(2)}) %collective-permute-start.3) | collective-permute-done | bytes 69664 | tf_op jit(solution)/shard_map/ppermute | solution.py:208
  37.5 6.7 %gated.1.refs_0_ = bf16[128,1024]{1,0:T(8,128)(2,1)} custom-call(f32[128,1024]{1,0:T(8,128)} %delta_ref.3, bf16[128,1024]{1,0:T(8,128)(2,1)} %u_ref.3, bf16[128,1024]{1,0:T(8,128)(2,1)} %z_ref.1, f32[32,128]{1,0:T(8,128)} %bc_ref.3, f32[128,128]{1,0:T(8,128)} %reshape.6.a_ref, f32[1,1024]{1,0:T(1,128)} %bitcast.4, f32[136,128]{1,0:T(8,128)} %copy-done.21, ...), custom_call_target="tpu_custom_call" | custom-call | tf_op jit(solution)/shard_map/gated/pallas_call | solution.py:217
  44.2 2.7 %collective-permute-start.6 = (bf16[128,1024]{1,0:T(8,128)(2,1)}, bf16[128,1024]{1,0:T(8,128)(2,1)S(1)}, u32[]{:S(2)}, u32[]{:S(2)}) collective-permute-start(bf16[128,1024]{1,0:T(8,128)(2,1)} %gated.1.refs_0_), channel_id=1, source_target_pairs={{0,224},{16,240},{32,0},{48,16},{64,32},{80,48},{96,64},{112,80},{... | collective-permute-start | bytes 786440 | tf_op jit(solution)/shard_map/ppermute | solution.py:230
  46.8 6.0 %collective-permute-done.9.refs_7_ = bf16[128,1024]{1,0:T(8,128)(2,1)S(1)} collective-permute-done((bf16[128,1024]{1,0:T(8,128)(2,1)}, bf16[128,1024]{1,0:T(8,128)(2,1)S(1)}, u32[]{:S(2)}, u32[]{:S(2)}) %collective-permute-start.9) | collective-permute-done | bytes 262176 | tf_op jit(solution)/shard_map/ppermute | solution.py:230
  52.8 2.7 %collective-permute-start.7 = (bf16[128,1024]{1,0:T(8,128)(2,1)S(1)}, bf16[128,1024]{1,0:T(8,128)(2,1)S(1)}, u32[]{:S(2)}, u32[]{:S(2)}) collective-permute-start(bf16[128,1024]{1,0:T(8,128)(2,1)S(1)} %collective-permute-done.6.refs_1_), channel_id=1, source_target_pairs={{0,224},{16,240},{32,0},{48,16},{64,32},{80,48},{96,64},{112,80},{... | collective-permute-start | bytes 786440 | tf_op jit(solution)/shard_map/ppermute | solution.py:230
  55.5 4.8 %collective-permute-done.10.refs_6_ = bf16[128,1024]{1,0:T(8,128)(2,1)S(1)} collective-permute-done((bf16[128,1024]{1,0:T(8,128)(2,1)S(1)}, bf16[128,1024]{1,0:T(8,128)(2,1)S(1)}, u32[]{:S(2)}, u32[]{:S(2)}) %collective-permute-start.10) | collective-permute-done | bytes 262176 | tf_op jit(solution)/shard_map/ppermute | solution.py:230
  60.3 2.4 %collective-permute-start.13 = (bf16[128,1024]{1,0:T(8,128)(2,1)}, bf16[128,1024]{1,0:T(8,128)(2,1)S(1)}, u32[]{:S(2)}, u32[]{:S(2)}) collective-permute-start(bf16[128,1024]{1,0:T(8,128)(2,1)} %gated.1.refs_0_), channel_id=1, source_target_pairs={{0,16},{16,0},{32,48},{48,32},{64,80},{80,64},{96,112},{112,96},{1... | collective-permute-start | bytes 786440 | tf_op jit(solution)/shard_map/ppermute | solution.py:233
  63.3 3.0 %collective-permute-start.8 = (bf16[128,1024]{1,0:T(8,128)(2,1)S(1)}, bf16[128,1024]{1,0:T(8,128)(2,1)S(1)}, u32[]{:S(2)}, u32[]{:S(2)}) collective-permute-start(bf16[128,1024]{1,0:T(8,128)(2,1)S(1)} %collective-permute-done.7.refs_2_), channel_id=1, source_target_pairs={{0,224},{16,240},{32,0},{48,16},{64,32},{80,48},{96,64},{112,80},{... | collective-permute-start | bytes 786440 | tf_op jit(solution)/shard_map/ppermute | solution.py:230
  66.8 3.7 %collective-permute-start.19 = (bf16[128,1024]{1,0:T(8,128)(2,1)S(1)}, bf16[128,1024]{1,0:T(8,128)(2,1)S(1)}, u32[]{:S(2)}, u32[]{:S(2)}) collective-permute-start(bf16[128,1024]{1,0:T(8,128)(2,1)S(1)} %collective-permute-done.10.refs_6_), channel_id=1, source_target_pairs={{0,16},{16,0},{32,48},{48,32},{64,80},{80,64},{96,112},{112,96},{1... | collective-permute-start | bytes 786440 | tf_op jit(solution)/shard_map/ppermute | solution.py:233
  73.2 4.7 %collective-permute-start.17 = (bf16[128,1024]{1,0:T(8,128)(2,1)S(1)}, bf16[128,1024]{1,0:T(8,128)(2,1)}, u32[]{:S(2)}, u32[]{:S(2)}) collective-permute-start(bf16[128,1024]{1,0:T(8,128)(2,1)S(1)} %collective-permute-done.12.refs_4_), channel_id=1, source_target_pairs={{0,16},{16,0},{32,48},{48,32},{64,80},{80,64},{96,112},{112,96},{1... | collective-permute-start | bytes 786440 | tf_op jit(solution)/shard_map/ppermute | solution.py:233
  79.5 6.2 %project.1 = (bf16[256,512]{1,0:T(8,128)(2,1)}, bf16[256,512]{1,0:T(8,128)(2,1)}, bf16[256,512]{1,0:T(8,128)(2,1)}, bf16[256,512]{1,0:T(8,128)(2,1)}, bf16[256,5...) custom-call(s32[3]{0:T(128)} %pad_add_fusion.place_ref, ...), custom_call_target="tpu_custom_call" | custom-call | tf_op jit(solution)/shard_map/project/pallas_call | solution.py:246
  86.9 2.4 %collective-permute-start.22 = (bf16[256,512]{1,0:T(8,128)(2,1)}, bf16[256,512]{1,0:T(8,128)(2,1)S(1)}, u32[]{:S(2)}, u32[]{:S(2)}) collective-permute-start(bf16[256,512]{1,0:T(8,128)(2,1)} %get-tuple-element.27), channel_id=1, source_target_pairs={{0,2},{1,3},{2,0},{3,1},{4,6},{5,7},{6,4},{7,5},{8,10},{9,11},{10,... | collective-permute-start | bytes 786440 | tf_op jit(solution)/shard_map/ppermute | solution.py:259
  91.8 2.6 %collective-permute-start.25 = (bf16[256,512]{1,0:T(8,128)(2,1)}, bf16[256,512]{1,0:T(8,128)(2,1)S(1)}, u32[]{:S(2)}, u32[]{:S(2)}) collective-permute-start(bf16[256,512]{1,0:T(8,128)(2,1)} %get-tuple-element.31), channel_id=1, source_target_pairs={{0,8},{1,9},{2,10},{3,11},{4,12},{5,13},{6,14},{7,15},{8,0},{9,1},... | collective-permute-start | bytes 786440 | tf_op jit(solution)/shard_map/ppermute | solution.py:259
  94.8 2.7 %collective-permute-start.26 = (bf16[256,512]{1,0:T(8,128)(2,1)}, bf16[256,512]{1,0:T(8,128)(2,1)S(1)}, u32[]{:S(2)}, u32[]{:S(2)}) collective-permute-start(bf16[256,512]{1,0:T(8,128)(2,1)} %get-tuple-element.32), channel_id=1, source_target_pairs={{0,12},{1,13},{2,14},{3,15},{4,0},{5,1},{6,2},{7,3},{8,4},{9,5},{1... | collective-permute-start | bytes 786440 | tf_op jit(solution)/shard_map/ppermute | solution.py:259
  97.5 3.9 %collective-permute-done.22.refs_2_ = bf16[256,512]{1,0:T(8,128)(2,1)S(1)} collective-permute-done((bf16[256,512]{1,0:T(8,128)(2,1)}, bf16[256,512]{1,0:T(8,128)(2,1)S(1)}, u32[]{:S(2)}, u32[]{:S(2)}) %collective-permute-start.22) | collective-permute-done | bytes 262176 | tf_op jit(solution)/shard_map/ppermute | solution.py:259
  101.4 4.1 %collective-permute-done.25.refs_6_ = bf16[256,512]{1,0:T(8,128)(2,1)S(1)} collective-permute-done((bf16[256,512]{1,0:T(8,128)(2,1)}, bf16[256,512]{1,0:T(8,128)(2,1)S(1)}, u32[]{:S(2)}, u32[]{:S(2)}) %collective-permute-start.25) | collective-permute-done | bytes 262176 | tf_op jit(solution)/shard_map/ppermute | solution.py:259
  106.3 2.7 %middle.1 = (f32[64,512]{1,0:T(8,128)}, bf16[64,512]{1,0:T(8,128)(2,1)}, bf16[64,512]{1,0:T(8,128)(2,1)}, bf16[64,512]{1,0:T(8,128)(2,1)}, f32[64,512]{1,0:T(8,1...) custom-call(s32[3]{0:T(128)} %pad_add_fusion.place_ref, ...), custom_call_target="tpu_custom_call" | custom-call | tf_op jit(solution)/shard_map/middle/pallas_call | solution.py:265
  109.0 3.1 %collective-permute-start.27 = (bf16[64,512]{1,0:T(8,128)(2,1)}, bf16[64,512]{1,0:T(8,128)(2,1)S(1)}, u32[]{:S(2)}, u32[]{:S(2)}) collective-permute-start(bf16[64,512]{1,0:T(8,128)(2,1)} %get-tuple-element.34), channel_id=1, source_target_pairs={{0,4},{1,5},{2,6},{3,7},{4,8},{5,9},{6,10},{7,11},{8,12},{9,13},{1... | collective-permute-start | bytes 196616 | tf_op jit(solution)/shard_map/ppermute | solution.py:259
  (112 shorter events, 28.5 us)
Async XLA Ops:
  5.8 12.0 %collective-permute-start.2 = (f32[136,128]{1,0:T(8,128)}, f32[136,128]{1,0:T(8,128)S(1)}, u32[]{:S(2)}, u32[]{:S(2)}) collective-permute-start(f32[136,128]{1,0:T(8,128)} %end_state.1.own_ref), channel_id=1, source_target_pairs={{0,48},{16,64},{32,80},{48,96},{64,112},{80,128},{96,144},{112,160... | collective-permute-start | bytes 208904 | tf_op jit(solution)/shard_map/ppermute | solution.py:208
  21.8 10.6 %collective-permute-start.5 = (f32[136,128]{1,0:T(8,128)}, f32[136,128]{1,0:T(8,128)S(1)}, u32[]{:S(2)}, u32[]{:S(2)}) collective-permute-start(f32[136,128]{1,0:T(8,128)} %get-tuple-element.23), channel_id=1, source_target_pairs={{0,64},{16,80},{32,96},{48,112},{64,128},{80,144},{96,160},{112,17... | collective-permute-start | bytes 208904 | tf_op jit(solution)/shard_map/ppermute | solution.py:208
  44.2 8.6 %collective-permute-start.9 = (bf16[128,1024]{1,0:T(8,128)(2,1)}, bf16[128,1024]{1,0:T(8,128)(2,1)S(1)}, u32[]{:S(2)}, u32[]{:S(2)}) collective-permute-start(bf16[128,1024]{1,0:T(8,128)(2,1)} %gated.1.refs_0_), channel_id=1, source_target_pairs={{0,32},{16,48},{32,64},{48,80},{64,96},{80,112},{96,128},{112,144}... | collective-permute-start | bytes 786440 | tf_op jit(solution)/shard_map/ppermute | solution.py:230
  44.2 8.6 %collective-permute-start.6 = (bf16[128,1024]{1,0:T(8,128)(2,1)}, bf16[128,1024]{1,0:T(8,128)(2,1)S(1)}, u32[]{:S(2)}, u32[]{:S(2)}) collective-permute-start(bf16[128,1024]{1,0:T(8,128)(2,1)} %gated.1.refs_0_), channel_id=1, source_target_pairs={{0,224},{16,240},{32,0},{48,16},{64,32},{80,48},{96,64},{112,80},{... | collective-permute-start | bytes 786440 | tf_op jit(solution)/shard_map/ppermute | solution.py:230
  52.8 7.5 %collective-permute-start.10 = (bf16[128,1024]{1,0:T(8,128)(2,1)S(1)}, bf16[128,1024]{1,0:T(8,128)(2,1)S(1)}, u32[]{:S(2)}, u32[]{:S(2)}) collective-permute-start(bf16[128,1024]{1,0:T(8,128)(2,1)S(1)} %collective-permute-done.9.refs_7_), channel_id=1, source_target_pairs={{0,32},{16,48},{32,64},{48,80},{64,96},{80,112},{96,128},{112,144}... | collective-permute-start | bytes 786440 | tf_op jit(solution)/shard_map/ppermute | solution.py:230
  52.8 10.4 %collective-permute-start.7 = (bf16[128,1024]{1,0:T(8,128)(2,1)S(1)}, bf16[128,1024]{1,0:T(8,128)(2,1)S(1)}, u32[]{:S(2)}, u32[]{:S(2)}) collective-permute-start(bf16[128,1024]{1,0:T(8,128)(2,1)S(1)} %collective-permute-done.6.refs_1_), channel_id=1, source_target_pairs={{0,224},{16,240},{32,0},{48,16},{64,32},{80,48},{96,64},{112,80},{... | collective-permute-start | bytes 786440 | tf_op jit(solution)/shard_map/ppermute | solution.py:230
  60.3 6.4 %collective-permute-start.11 = (bf16[128,1024]{1,0:T(8,128)(2,1)S(1)}, bf16[128,1024]{1,0:T(8,128)(2,1)S(1)}, u32[]{:S(2)}, u32[]{:S(2)}) collective-permute-start(bf16[128,1024]{1,0:T(8,128)(2,1)S(1)} %collective-permute-done.10.refs_6_), channel_id=1, source_target_pairs={{0,32},{16,48},{32,64},{48,80},{64,96},{80,112},{96,128},{112,144}... | collective-permute-start | bytes 786440 | tf_op jit(solution)/shard_map/ppermute | solution.py:230
  60.3 6.4 %collective-permute-start.13 = (bf16[128,1024]{1,0:T(8,128)(2,1)}, bf16[128,1024]{1,0:T(8,128)(2,1)S(1)}, u32[]{:S(2)}, u32[]{:S(2)}) collective-permute-start(bf16[128,1024]{1,0:T(8,128)(2,1)} %gated.1.refs_0_), channel_id=1, source_target_pairs={{0,16},{16,0},{32,48},{48,32},{64,80},{80,64},{96,112},{112,96},{1... | collective-permute-start | bytes 786440 | tf_op jit(solution)/shard_map/ppermute | solution.py:233
  62.8 7.7 %collective-permute-start.20 = (bf16[128,1024]{1,0:T(8,128)(2,1)S(1)}, bf16[128,1024]{1,0:T(8,128)(2,1)S(1)}, u32[]{:S(2)}, u32[]{:S(2)}) collective-permute-start(bf16[128,1024]{1,0:T(8,128)(2,1)S(1)} %collective-permute-done.9.refs_7_), channel_id=1, source_target_pairs={{0,16},{16,0},{32,48},{48,32},{64,80},{80,64},{96,112},{112,96},{1... | collective-permute-start | bytes 786440 | tf_op jit(solution)/shard_map/ppermute | solution.py:233
  62.8 7.7 %collective-permute-start.14 = (bf16[128,1024]{1,0:T(8,128)(2,1)S(1)}, bf16[128,1024]{1,0:T(8,128)(2,1)S(1)}, u32[]{:S(2)}, u32[]{:S(2)}) collective-permute-start(bf16[128,1024]{1,0:T(8,128)(2,1)S(1)} %collective-permute-done.6.refs_1_), channel_id=1, source_target_pairs={{0,16},{16,0},{32,48},{48,32},{64,80},{80,64},{96,112},{112,96},{1... | collective-permute-start | bytes 786440 | tf_op jit(solution)/shard_map/ppermute | solution.py:233
  63.3 8.6 %collective-permute-start.8 = (bf16[128,1024]{1,0:T(8,128)(2,1)S(1)}, bf16[128,1024]{1,0:T(8,128)(2,1)S(1)}, u32[]{:S(2)}, u32[]{:S(2)}) collective-permute-start(bf16[128,1024]{1,0:T(8,128)(2,1)S(1)} %collective-permute-done.7.refs_2_), channel_id=1, source_target_pairs={{0,224},{16,240},{32,0},{48,16},{64,32},{80,48},{96,64},{112,80},{... | collective-permute-start | bytes 786440 | tf_op jit(solution)/shard_map/ppermute | solution.py:230
  66.8 6.4 %collective-permute-start.12 = (bf16[128,1024]{1,0:T(8,128)(2,1)S(1)}, bf16[128,1024]{1,0:T(8,128)(2,1)S(1)}, u32[]{:S(2)}, u32[]{:S(2)}) collective-permute-start(bf16[128,1024]{1,0:T(8,128)(2,1)S(1)} %collective-permute-done.11.refs_5_), channel_id=1, source_target_pairs={{0,32},{16,48},{32,64},{48,80},{64,96},{80,112},{96,128},{112,144}... | collective-permute-start | bytes 786440 | tf_op jit(solution)/shard_map/ppermute | solution.py:230
  66.8 11.8 %collective-permute-start.19 = (bf16[128,1024]{1,0:T(8,128)(2,1)S(1)}, bf16[128,1024]{1,0:T(8,128)(2,1)S(1)}, u32[]{:S(2)}, u32[]{:S(2)}) collective-permute-start(bf16[128,1024]{1,0:T(8,128)(2,1)S(1)} %collective-permute-done.10.refs_6_), channel_id=1, source_target_pairs={{0,16},{16,0},{32,48},{48,32},{64,80},{80,64},{96,112},{112,96},{1... | collective-permute-start | bytes 786440 | tf_op jit(solution)/shard_map/ppermute | solution.py:233
  70.4 8.1 %collective-permute-start.15 = (bf16[128,1024]{1,0:T(8,128)(2,1)S(1)}, bf16[128,1024]{1,0:T(8,128)(2,1)S(1)}, u32[]{:S(2)}, u32[]{:S(2)}) collective-permute-start(bf16[128,1024]{1,0:T(8,128)(2,1)S(1)} %collective-permute-done.7.refs_2_), channel_id=1, source_target_pairs={{0,16},{16,0},{32,48},{48,32},{64,80},{80,64},{96,112},{112,96},{1... | collective-permute-start | bytes 786440 | tf_op jit(solution)/shard_map/ppermute | solution.py:233
  70.6 8.0 %collective-permute-start.18 = (bf16[128,1024]{1,0:T(8,128)(2,1)S(1)}, bf16[128,1024]{1,0:T(8,128)(2,1)S(1)}, u32[]{:S(2)}, u32[]{:S(2)}) collective-permute-start(bf16[128,1024]{1,0:T(8,128)(2,1)S(1)} %collective-permute-done.11.refs_5_), channel_id=1, source_target_pairs={{0,16},{16,0},{32,48},{48,32},{64,80},{80,64},{96,112},{112,96},{1... | collective-permute-start | bytes 786440 | tf_op jit(solution)/shard_map/ppermute | solution.py:233
  71.9 6.7 %collective-permute-start.16 = (bf16[128,1024]{1,0:T(8,128)(2,1)S(1)}, bf16[128,1024]{1,0:T(8,128)(2,1)}, u32[]{:S(2)}, u32[]{:S(2)}) collective-permute-start(bf16[128,1024]{1,0:T(8,128)(2,1)S(1)} %collective-permute-done.8.refs_3_), channel_id=1, source_target_pairs={{0,16},{16,0},{32,48},{48,32},{64,80},{80,64},{96,112},{112,96},{1... | collective-permute-start | bytes 786440 | tf_op jit(solution)/shard_map/ppermute | solution.py:233
  73.2 6.0 %collective-permute-start.17 = (bf16[128,1024]{1,0:T(8,128)(2,1)S(1)}, bf16[128,1024]{1,0:T(8,128)(2,1)}, u32[]{:S(2)}, u32[]{:S(2)}) collective-permute-start(bf16[128,1024]{1,0:T(8,128)(2,1)S(1)} %collective-permute-done.12.refs_4_), channel_id=1, source_target_pairs={{0,16},{16,0},{32,48},{48,32},{64,80},{80,64},{96,112},{112,96},{1... | collective-permute-start | bytes 786440 | tf_op jit(solution)/shard_map/ppermute | solution.py:233
  85.7 9.1 %collective-permute-start.21 = (bf16[256,512]{1,0:T(8,128)(2,1)}, bf16[256,512]{1,0:T(8,128)(2,1)S(1)}, u32[]{:S(2)}, u32[]{:S(2)}) collective-permute-start(bf16[256,512]{1,0:T(8,128)(2,1)} %get-tuple-element.26), channel_id=1, source_target_pairs={{0,1},{1,2},{2,3},{3,0},{4,5},{5,6},{6,7},{7,4},{8,9},{9,10},{10,1... | collective-permute-start | bytes 786440 | tf_op jit(solution)/shard_map/ppermute | solution.py:259
  86.9 14.5 %collective-permute-start.22 = (bf16[256,512]{1,0:T(8,128)(2,1)}, bf16[256,512]{1,0:T(8,128)(2,1)S(1)}, u32[]{:S(2)}, u32[]{:S(2)}) collective-permute-start(bf16[256,512]{1,0:T(8,128)(2,1)} %get-tuple-element.27), channel_id=1, source_target_pairs={{0,2},{1,3},{2,0},{3,1},{4,6},{5,7},{6,4},{7,5},{8,10},{9,11},{10,... | collective-permute-start | bytes 786440 | tf_op jit(solution)/shard_map/ppermute | solution.py:259
  89.4 12.0 %collective-permute-start.23 = (bf16[256,512]{1,0:T(8,128)(2,1)}, bf16[256,512]{1,0:T(8,128)(2,1)S(1)}, u32[]{:S(2)}, u32[]{:S(2)}) collective-permute-start(bf16[256,512]{1,0:T(8,128)(2,1)} %get-tuple-element.28), channel_id=1, source_target_pairs={{0,3},{1,0},{2,1},{3,2},{4,7},{5,4},{6,5},{7,6},{8,11},{9,8},{10,9... | collective-permute-start | bytes 786440 | tf_op jit(solution)/shard_map/ppermute | solution.py:259
  90.5 10.9 %collective-permute-start.24 = (bf16[256,512]{1,0:T(8,128)(2,1)}, bf16[256,512]{1,0:T(8,128)(2,1)S(1)}, u32[]{:S(2)}, u32[]{:S(2)}) collective-permute-start(bf16[256,512]{1,0:T(8,128)(2,1)} %get-tuple-element.30), channel_id=1, source_target_pairs={{0,4},{1,5},{2,6},{3,7},{4,8},{5,9},{6,10},{7,11},{8,12},{9,13},{1... | collective-permute-start | bytes 786440 | tf_op jit(solution)/shard_map/ppermute | solution.py:259
  91.8 13.7 %collective-permute-start.25 = (bf16[256,512]{1,0:T(8,128)(2,1)}, bf16[256,512]{1,0:T(8,128)(2,1)S(1)}, u32[]{:S(2)}, u32[]{:S(2)}) collective-permute-start(bf16[256,512]{1,0:T(8,128)(2,1)} %get-tuple-element.31), channel_id=1, source_target_pairs={{0,8},{1,9},{2,10},{3,11},{4,12},{5,13},{6,14},{7,15},{8,0},{9,1},... | collective-permute-start | bytes 786440 | tf_op jit(solution)/shard_map/ppermute | solution.py:259
  94.8 10.7 %collective-permute-start.26 = (bf16[256,512]{1,0:T(8,128)(2,1)}, bf16[256,512]{1,0:T(8,128)(2,1)S(1)}, u32[]{:S(2)}, u32[]{:S(2)}) collective-permute-start(bf16[256,512]{1,0:T(8,128)(2,1)} %get-tuple-element.32), channel_id=1, source_target_pairs={{0,12},{1,13},{2,14},{3,15},{4,0},{5,1},{6,2},{7,3},{8,4},{9,5},{1... | collective-permute-start | bytes 786440 | tf_op jit(solution)/shard_map/ppermute | solution.py:259
  109.0 6.4 %collective-permute-start.27 = (bf16[64,512]{1,0:T(8,128)(2,1)}, bf16[64,512]{1,0:T(8,128)(2,1)S(1)}, u32[]{:S(2)}, u32[]{:S(2)}) collective-permute-start(bf16[64,512]{1,0:T(8,128)(2,1)} %get-tuple-element.34), channel_id=1, source_target_pairs={{0,4},{1,5},{2,6},{3,7},{4,8},{5,9},{6,10},{7,11},{8,12},{9,13},{1... | collective-permute-start | bytes 196616 | tf_op jit(solution)/shard_map/ppermute | solution.py:259
  (40 other events, 243.2 us)

commit v2 on v0

v2 whole, which is shorter than its diff:
```python
import functools
import math

import jax
import jax.numpy as jnp
from jax import lax
from jax.experimental import pallas as pl
from jax.experimental.pallas import tpu as pltpu
from jax.sharding import PartitionSpec as P

LANES = 128
SUB = 8
NEG_LOG2E = -math.log2(math.e)


def fill_transposed(dst, rows, groups, make):
    for g in range(groups):
        dst[pl.ds(g, rows, stride=groups), :] = make(g)


def fill_coefficients(dst, bc, rows, count):
    turned = bc.T
    for n in range(count):
        dst[pl.ds(n, rows, stride=count), :] = jnp.broadcast_to(
            turned[:, n : n + 1], (rows, LANES)
        )


def end_state_kernel(delta_ref, u_ref, bc_ref, a_ref, out_ref, d_t, w_t, b_t, a_t):
    rows, channels = delta_ref.shape
    groups = channels // LANES
    states = a_ref.shape[0]

    def lanes(g):
        return slice(g * LANES, (g + 1) * LANES)

    fill_transposed(d_t, rows, groups, lambda g: delta_ref[:, lanes(g)])
    fill_transposed(
        w_t,
        rows,
        groups,
        lambda g: delta_ref[:, lanes(g)] * u_ref[:, lanes(g)].astype(jnp.float32),
    )
    fill_coefficients(b_t, bc_ref[:states, :], rows, states)
    fill_transposed(a_t, states, groups, lambda g: a_ref[:, lanes(g)])
    rate = [a_t[n * groups : (n + 1) * groups, :] * NEG_LOG2E for n in range(states)]

    def step(t, carry):
        total, state = carry
        d = d_t[pl.ds(pl.multiple_of(t * groups, groups), groups), :]
        w = w_t[pl.ds(pl.multiple_of(t * groups, groups), groups), :]
        new = []
        for n in range(states):
            b = b_t[pl.ds(t * states + n, groups, stride=0), :]
            new.append(jnp.exp2(d * rate[n]) * state[n] + w * b)
        return total + d, tuple(new)

    zero = jnp.zeros((groups, LANES), jnp.float32)
    total, state = lax.fori_loop(0, rows, step, (zero, (zero,) * states), unroll=4)
    for n in range(states):
        base = 2 * n * groups
        out_ref[base : base + groups, :] = state[n]
        out_ref[base + groups : base + 2 * groups, :] = total


def carry_kernel(me_ref, ends_ref, a_ref, out_ref, rate_t):
    count = ends_ref.shape[0] // (2 * SUB)
    fill_transposed(
        rate_t, a_ref.shape[0], SUB, lambda g: a_ref[:, g * LANES : (g + 1) * LANES] * NEG_LOG2E
    )
    rate = rate_t[pl.ds(pl.multiple_of(me_ref[0] * SUB, SUB), SUB), :]
    state = jnp.zeros((SUB, LANES), jnp.float32)
    for k in range(count):
        out_ref[k * SUB : (k + 1) * SUB, :] = state
        base = 2 * k * SUB
        total = ends_ref[base + SUB : base + 2 * SUB, :]
        state = jnp.exp2(total * rate) * state + ends_ref[base : base + SUB, :]


def gated_kernel(
    delta_ref, u_ref, z_ref, bc_ref, a_ref, skip_ref, start_ref, out_ref, d_t, w_t, bc_t, y_t, a_t,
):
    rows, channels = delta_ref.shape
    groups = channels // LANES
    states = a_ref.shape[0]

    def lanes(g):
        return slice(g * LANES, (g + 1) * LANES)

    fill_transposed(d_t, rows, groups, lambda g: delta_ref[:, lanes(g)])
    fill_transposed(
        w_t,
        rows,
        groups,
        lambda g: delta_ref[:, lanes(g)] * u_ref[:, lanes(g)].astype(jnp.float32),
    )
    fill_coefficients(bc_t, bc_ref[...], rows, 2 * states)
    fill_transposed(a_t, states, groups, lambda g: a_ref[:, lanes(g)])
    rate = [a_t[n * groups : (n + 1) * groups, :] * NEG_LOG2E for n in range(states)]

    start = [start_ref[n * groups : (n + 1) * groups, :] for n in range(states)]

    def step(t, state):
        d = d_t[pl.ds(pl.multiple_of(t * groups, groups), groups), :]
        w = w_t[pl.ds(pl.multiple_of(t * groups, groups), groups), :]
        new = []
        parts = [None] * 4
        for n in range(states):
            b = bc_t[pl.ds(t * 2 * states + n, groups, stride=0), :]
            c = bc_t[pl.ds(t * 2 * states + states + n, groups, stride=0), :]
            s = jnp.exp2(d * rate[n]) * state[n] + w * b
            new.append(s)
            term = s * c
            parts[n % 4] = term if parts[n % 4] is None else parts[n % 4] + term
        y_t[pl.ds(pl.multiple_of(t * groups, groups), groups), :] = (parts[0] + parts[1]) + (
            parts[2] + parts[3]
        )
        return tuple(new)

    lax.fori_loop(0, rows, step, tuple(start), unroll=4)

    for g in range(groups):
        y = y_t[pl.ds(g, rows, stride=groups), :]
        u = u_ref[:, lanes(g)].astype(jnp.float32)
        z = z_ref[:, lanes(g)].astype(jnp.float32)
        mixed = y + skip_ref[:, lanes(g)] * u
        out_ref[:, lanes(g)] = (mixed * (z / (1.0 + jnp.exp(-z)))).astype(jnp.bfloat16)


def project_kernel(count, me_ref, *refs):
    blocks, w_ref, out_ref = refs[:count], refs[count], refs[count + 1]
    rows = blocks[0].shape[0]
    me = me_ref[0]
    core = lax.rem(me, 2)
    chip = me - core
    way = 2 - 4 * core
    units = (count - 2) // 2
    homes = [chip + core, chip + 1 - core]
    for side in (-1, 1):
        for unit in range(units):
            same = (unit % 2 == 0) == (side == -1)
            parity = core if same else 1 - core
            homes.append(chip + side * way * (unit // 2 + 1) + parity)
    for block, home in zip(blocks, homes):
        at = pl.multiple_of(lax.rem(home + 2 * count, count) * rows, rows)
        out_ref[pl.ds(at, rows), :] = jnp.dot(
            block[...], w_ref[...], preferred_element_type=jnp.float32
        ).astype(jnp.bfloat16)


def whole():
    return pl.BlockSpec(memory_space=pltpu.VMEM)


def body(u_in, z_in, delta, bc_proj, a_rate, d_skip, w_out):
    rows, channels = u_in.shape
    states = a_rate.shape[0]
    groups = channels // LANES
    width = w_out.shape[1]
    count = lax.axis_size("ctx")
    flat = pltpu.VMEM((rows * groups, LANES), jnp.float32)
    rates = pltpu.VMEM((states * groups, LANES), jnp.float32)
    smem = pl.BlockSpec(memory_space=pltpu.SMEM)
    me = lax.axis_index("ctx").astype(jnp.int32).reshape(1)

    ends = pl.pallas_call(
        end_state_kernel,
        out_shape=jax.ShapeDtypeStruct((2 * states * groups, LANES), jnp.float32),
        in_specs=[whole()] * 4,
        out_specs=whole(),
        scratch_shapes=[flat, flat, pltpu.VMEM((rows * states, LANES), jnp.float32), rates],
        name="end_state",
    )(delta, u_in, bc_proj, a_rate)
    ends = lax.all_to_all(ends, "ctx", split_axis=0, concat_axis=0, tiled=True)
    entering = pl.pallas_call(
        carry_kernel,
        out_shape=jax.ShapeDtypeStruct((count * groups, LANES), jnp.float32),
        in_specs=[smem, whole(), whole()],
        out_specs=whole(),
        scratch_shapes=[rates],
        name="carry",
    )(me, ends, a_rate)
    entering = lax.all_to_all(entering, "ctx", split_axis=0, concat_axis=0, tiled=True)
    gated = pl.pallas_call(
        gated_kernel,
        out_shape=jax.ShapeDtypeStruct((rows, channels), jnp.bfloat16),
        in_specs=[whole()] * 7,
        out_specs=whole(),
        scratch_shapes=[
            flat, flat, pltpu.VMEM((rows * 2 * states, LANES), jnp.float32), flat, rates
        ],
        name="gated",
    )(delta, u_in, z_in, bc_proj, a_rate, d_skip.reshape(1, channels), entering)

    ring = [(i, (i + 2 - 4 * (i % 2)) % count) for i in range(count)]
    trade = [(i, i ^ 1) for i in range(count)]
    local = [gated, lax.ppermute(gated, "ctx", trade)]
    arrived = []
    for unit in range(count // 2 - 1):
        source = (local + arrived)[unit]
        arrived.append(lax.ppermute(source, "ctx", ring))
    traded = [lax.ppermute(value, "ctx", trade) for value in arrived]
    terms = pl.pallas_call(
        functools.partial(project_kernel, count),
        out_shape=jax.ShapeDtypeStruct((rows * count, width), jnp.bfloat16),
        in_specs=[smem] + [whole()] * (count + 1),
        out_specs=whole(),
        name="project",
    )(me, *local, *arrived, *traded, w_out)

    received = lax.all_to_all(
        terms.reshape(count, rows, width), "exp", split_axis=0, concat_axis=0
    )
    return jnp.sum(received.astype(jnp.float32), axis=0).astype(jnp.bfloat16)


def solution(mesh):
    return jax.shard_map(
        body,
        mesh=mesh,
        in_specs=(
            P("ctx", "exp"),
            P("ctx", "exp"),
            P("ctx", "exp"),
            P(None, "ctx"),
            P(None, "exp"),
            P("exp"),
            P("exp", "ctx"),
        ),
        out_specs=P("exp", "ctx"),
        check_vma=False,
    )
```

time: 150 us -> 120 us (0.80)
  waiting for transfers between devices: 84.2 us -> 19.4 us
  starting transfers between devices: 0.04 us -> 33.8 us
  between operations: 13.4 us -> 0.15 us
  blocking collectives: 34 us -> 45.7 us
  Pallas kernels: 11.4 us -> 18.2 us
  matrix products: 4.52 us -> 0 us
    all_gather x2 -> x0, waiting for transfers between devices: 84.2 us -> none  [the longest x1 43.1 us: body(): all_ends = lax.all_gather(ends, 'ctx', axis=0, tiled=True)]
    ppermute x0 -> x15, starting transfers between devices: none -> 23.8 us  [the longest x7 13.6 us: body(): traded = [lax.ppermute(value, 'ctx', trade) for value in arrived]]
    all_to_all x1 -> x2, blocking collectives: 34 us -> 45.7 us  [the longest x1 34.3 us: body(): lax.all_to_all(terms.reshape(count, rows, width), 'exp', split_axis=0, co...]
    ppermute x0 -> x15, waiting for transfers between devices: none -> 10.3 us  [the longest x7 9.78 us: body(): arrived.append(lax.ppermute(source, 'ctx', ring))]
    all_to_all x0 -> x1, starting transfers between devices: none -> 9.98 us  [body(): ends = lax.all_to_all(ends, 'ctx', split_axis=0, concat_axis=0, tiled=True)]
    all_to_all x0 -> x1, waiting for transfers between devices: none -> 9.17 us  [body(): ends = lax.all_to_all(ends, 'ctx', split_axis=0, concat_axis=0, tiled=True)]
    pallas_call x1 -> x3, Pallas kernels: 4.34 us -> 11.9 us  [the longest x1 6.21 us: body(): pl.pallas_call(functools.partial(project_kernel, count), out_shape=jax.Sh...]
    dot_general x1 -> x0, matrix products: 4.52 us -> none  [body(): jnp.dot(lax.all_gather(gated, 'ctx', axis=0, tiled=True), w_out, preferre...]
  transfers between devices with their start and end apart: 2 -> 16, of which waited for: 2 -> 5; matrix products, arithmetic and copies ran while one was open for 0% -> 0% of each run, Pallas kernels for 0% -> 0%
where the time goes in v2:
time: 120 us
  blocking collectives  45.7 us (38%)
  starting transfers between devices  33.8 us (28%)
  waiting for transfers between devices  19.4 us (16%)
  Pallas kernels  18.2 us (15%)
  local copies, waits for them, and re-layouts  1.48 us (1%)
    all_to_all x1, blocking collectives, body(): lax.all_to_all(terms.reshape(count, rows, width), 'exp', split_axis=0, co...  34.3 us
    ppermute x7, starting transfers between devices, body(): traded = [lax.ppermute(value, 'ctx', trade) for value in arrived]  13.6 us
    all_to_all x1, blocking collectives, body(): lax.all_to_all(entering, 'ctx', split_axis=0, concat_axis=0, tiled=True)  11.4 us
    all_to_all x1, starting transfers between devices, body(): ends = lax.all_to_all(ends, 'ctx', split_axis=0, concat_axis=0, tiled=True)  9.98 us
    ppermute x7, waiting for transfers between devices, body(): arrived.append(lax.ppermute(source, 'ctx', ring))  9.78 us
    ppermute x7, starting transfers between devices, body(): arrived.append(lax.ppermute(source, 'ctx', ring))  9.49 us
    all_to_all x1, waiting for transfers between devices, body(): ends = lax.all_to_all(ends, 'ctx', split_axis=0, concat_axis=0, tiled=True)  9.17 us
    pallas_call x1, Pallas kernels, body(): pl.pallas_call(gated_kernel, out_shape=jax.ShapeDtypeStruct((rows, channe...  6.32 us
  transfers between devices with their start and end apart: 16, of which 5 were waited for; matrix products, arithmetic and copies ran while one was open for 0% of the time, Pallas kernels for 0%

profile of v2, /device:TPU:1, one launch (start us, length us, event | category | flops | bytes accessed | tf_op | source)
XLA Modules:
  0.0 119.7 jit_solution(9031569002730901059)
XLA Ops:
  0.0 4.1 %end_state.1 = f32[256,128]{1,0:T(8,128)} custom-call(f32[128,1024]{1,0:T(8,128)} %delta_ref.3, bf16[128,1024]{1,0:T(8,128)(2,1)} %u_ref.3, f32[32,128]{1,0:T(8,128)} %bc_ref.3, f32[16,1024]{1,0:T(8,128)} %a_ref.5), custom_call_target="tpu_custom_call" | custom-call | tf_op jit(solution)/shard_map/end_state/pallas_call | solution.py:166
  4.1 10.0 %all-to-all-start = ((f32[16,16,128]{2,1,0:T(8,128)}), f32[16,16,128]{2,1,0:T(8,128)S(1)}, u32[]{:S(2)}, u32[]{:S(2)}) async-start(f32[16,16,128]{2,1,0:T(8,128)} %bitcast.8), calls=%async_computation | async-start | bytes 262144 | tf_op jit(solution)/shard_map/all_to_all | solution.py:174
  14.1 9.2 %all-to-all-done = f32[16,16,128]{2,1,0:T(8,128)S(1)} async-done(((f32[16,16,128]{2,1,0:T(8,128)}), f32[16,16,128]{2,1,0:T(8,128)S(1)}, u32[]{:S(2)}, u32[]{:S(2)}) %all-to-all-start) | async-done | bytes 131104 | tf_op jit(solution)/shard_map/all_to_all | solution.py:174
  23.3 0.7 copy-done
  23.9 1.6 %carry.1 = f32[128,128]{1,0:T(8,128)} custom-call(s32[1]{0:T(128)} %bitcast.me_ref, f32[256,128]{1,0:T(8,128)} %bitcast.9, f32[16,1024]{1,0:T(8,128)} %a_ref.5), custom_call_target="tpu_custom_call" | custom-call | tf_op jit(solution)/shard_map/carry/pallas_call | solution.py:175
  25.5 11.4 %all_to_all.27 = f32[16,8,128]{2,1,0:T(8,128)} all-to-all(f32[16,8,128]{2,1,0:T(8,128)} %bitcast.11), channel_id=1, replica_groups=mesh['ctx'=16,'exp'=16] {'ctx'}, dimensions={0} | all-to-all | bytes 131072 | tf_op jit(solution)/shard_map/all_to_all | solution.py:183
  36.9 6.3 %gated.1.refs_0_ = bf16[128,1024]{1,0:T(8,128)(2,1)} custom-call(f32[128,1024]{1,0:T(8,128)} %delta_ref.3, bf16[128,1024]{1,0:T(8,128)(2,1)} %u_ref.3, bf16[128,1024]{1,0:T(8,128)(2,1)} %z_ref.1, f32[32,128]{1,0:T(8,128)} %bc_ref.3, f32[16,1024]{1,0:T(8,128)} %a_ref.5, f32[1,1024]{1,0:T(1,128)} %bitcast.12, f32[128,128]{1,0:T(8,128)} %bitcast.10), custom_call_target="tpu_custom_call" | custom-call | tf_op jit(solution)/shard_map/gated/pallas_call | solution.py:184
  43.4 0.7 collective-permute-start
  44.0 4.9 %collective-permute-done.1.refs_2_ = bf16[128,1024]{1,0:T(8,128)(2,1)S(1)} collective-permute-done((bf16[128,1024]{1,0:T(8,128)(2,1)}, bf16[128,1024]{1,0:T(8,128)(2,1)S(1)}, u32[]{:S(2)}, u32[]{:S(2)}) %collective-permute-start.1) | collective-permute-done | bytes 262176 | tf_op jit(solution)/shard_map/ppermute | solution.py:201
  48.9 1.1 collective-permute-start.3
  50.1 4.1 %collective-permute-done.3.refs_4_ = bf16[128,1024]{1,0:T(8,128)(2,1)S(1)} collective-permute-done((bf16[128,1024]{1,0:T(8,128)(2,1)S(1)}, bf16[128,1024]{1,0:T(8,128)(2,1)S(1)}, u32[]{:S(2)}, u32[]{:S(2)}) %collective-permute-start.3) | collective-permute-done | bytes 262176 | tf_op jit(solution)/shard_map/ppermute | solution.py:201
  54.2 2.3 %collective-permute-start.5 = (bf16[128,1024]{1,0:T(8,128)(2,1)S(1)}, bf16[128,1024]{1,0:T(8,128)(2,1)S(1)}, u32[]{:S(2)}, u32[]{:S(2)}) collective-permute-start(bf16[128,1024]{1,0:T(8,128)(2,1)S(1)} %collective-permute-done.3.refs_4_), channel_id=1, source_target_pairs={{0,32},{16,240},{32,64},{48,16},{64,96},{80,48},{96,128},{112,80},... | collective-permute-start | bytes 786440 | tf_op jit(solution)/shard_map/ppermute | solution.py:201
  56.4 0.8 collective-permute-done.2.refs_3_
  57.3 2.0 %collective-permute-start.4 = (bf16[128,1024]{1,0:T(8,128)(2,1)S(1)}, bf16[128,1024]{1,0:T(8,128)(2,1)S(1)}, u32[]{:S(2)}, u32[]{:S(2)}) collective-permute-start(bf16[128,1024]{1,0:T(8,128)(2,1)S(1)} %collective-permute-done.2.refs_3_), channel_id=1, source_target_pairs={{0,32},{16,240},{32,64},{48,16},{64,96},{80,48},{96,128},{112,80},... | collective-permute-start | bytes 786440 | tf_op jit(solution)/shard_map/ppermute | solution.py:201
  59.2 2.4 %collective-permute-start.8 = (bf16[128,1024]{1,0:T(8,128)(2,1)S(1)}, bf16[128,1024]{1,0:T(8,128)(2,1)S(1)}, u32[]{:S(2)}, u32[]{:S(2)}) collective-permute-start(bf16[128,1024]{1,0:T(8,128)(2,1)S(1)} %collective-permute-done.1.refs_2_), channel_id=1, source_target_pairs={{0,16},{16,0},{32,48},{48,32},{64,80},{80,64},{96,112},{112,96},{1... | collective-permute-start | bytes 786440 | tf_op jit(solution)/shard_map/ppermute | solution.py:202
  61.8 2.9 %collective-permute-start.7 = (bf16[128,1024]{1,0:T(8,128)(2,1)S(1)}, bf16[128,1024]{1,0:T(8,128)(2,1)S(1)}, u32[]{:S(2)}, u32[]{:S(2)}) collective-permute-start(bf16[128,1024]{1,0:T(8,128)(2,1)S(1)} %collective-permute-done.5.refs_6_), channel_id=1, source_target_pairs={{0,32},{16,240},{32,64},{48,16},{64,96},{80,48},{96,128},{112,80},... | collective-permute-start | bytes 786440 | tf_op jit(solution)/shard_map/ppermute | solution.py:201
  64.7 1.0 collective-permute-start.6
  65.7 3.6 %collective-permute-start.9 = (bf16[128,1024]{1,0:T(8,128)(2,1)S(1)}, bf16[128,1024]{1,0:T(8,128)(2,1)S(1)}, u32[]{:S(2)}, u32[]{:S(2)}) collective-permute-start(bf16[128,1024]{1,0:T(8,128)(2,1)S(1)} %collective-permute-done.2.refs_3_), channel_id=1, source_target_pairs={{0,16},{16,0},{32,48},{48,32},{64,80},{80,64},{96,112},{112,96},{1... | collective-permute-start | bytes 786440 | tf_op jit(solution)/shard_map/ppermute | solution.py:202
  69.8 4.2 %collective-permute-start.14 = (bf16[128,1024]{1,0:T(8,128)(2,1)S(1)}, bf16[128,1024]{1,0:T(8,128)(2,1)S(1)}, u32[]{:S(2)}, u32[]{:S(2)}) collective-permute-start(bf16[128,1024]{1,0:T(8,128)(2,1)S(1)} %collective-permute-done.7.refs_8_), channel_id=1, source_target_pairs={{0,16},{16,0},{32,48},{48,32},{64,80},{80,64},{96,112},{112,96},{1... | collective-permute-start | bytes 786440 | tf_op jit(solution)/shard_map/ppermute | solution.py:202
  74.0 2.8 %collective-permute-start.13 = (bf16[128,1024]{1,0:T(8,128)(2,1)S(1)}, bf16[128,1024]{1,0:T(8,128)(2,1)}, u32[]{:S(2)}, u32[]{:S(2)}) collective-permute-start(bf16[128,1024]{1,0:T(8,128)(2,1)S(1)} %collective-permute-done.6.refs_7_), channel_id=1, source_target_pairs={{0,16},{16,0},{32,48},{48,32},{64,80},{80,64},{96,112},{112,96},{1... | collective-permute-start | bytes 786440 | tf_op jit(solution)/shard_map/ppermute | solution.py:202
  76.9 0.8 copy-done.14
  78.2 6.2 %project.1 = bf16[2048,512]{1,0:T(8,128)(2,1)} custom-call(s32[1]{0:T(128)} %bitcast.me_ref, bf16[128,1024]{1,0:T(8,128)(2,1)} %gated.1.refs_0_, bf16[128,1024]{1,0:T(8,128)(2,1)} %copy-done.2, bf16[128,1024]{1,0:T(8,128)(2,1)} %copy-done.1, bf16[128,1024]{1,0:T(8,128)(2,1)} %copy-done.4, bf16[128,1024]{1,0:T(8,128)(2,1)} %copy-done.3, ...), custom_call_target="tpu_custom_call" | custom-call | tf_op jit(solution)/shard_map/project/pallas_call | solution.py:203
  84.4 34.3 %all_to_all.28 = bf16[16,128,512]{2,1,0:T(8,128)(2,1)S(1)} all-to-all(bf16[16,128,512]{2,1,0:T(8,128)(2,1)} %bitcast.7), channel_id=1, replica_groups=mesh['ctx'=16,'exp'=16] {'exp'}, dimensions={0} | all-to-all | bytes 4194304 | tf_op jit(solution)/shard_map/all_to_all | solution.py:211
  118.7 1.0 reduce_sum.12
  (45 shorter events, 1.4 us)
Async XLA Ops:
  4.1 19.1 %all-to-all-start = ((f32[16,16,128]{2,1,0:T(8,128)}), f32[16,16,128]{2,1,0:T(8,128)S(1)}, u32[]{:S(2)}, u32[]{:S(2)}) async-start(f32[16,16,128]{2,1,0:T(8,128)} %bitcast.8), calls=%async_computation | async-start | bytes 262144 | tf_op jit(solution)/shard_map/all_to_all | solution.py:174
  43.2 5.7 %collective-permute-start.1 = (bf16[128,1024]{1,0:T(8,128)(2,1)}, bf16[128,1024]{1,0:T(8,128)(2,1)S(1)}, u32[]{:S(2)}, u32[]{:S(2)}) collective-permute-start(bf16[128,1024]{1,0:T(8,128)(2,1)} %gated.1.refs_0_), channel_id=1, source_target_pairs={{0,32},{16,240},{32,64},{48,16},{64,96},{80,48},{96,128},{112,80},... | collective-permute-start | bytes 786440 | tf_op jit(solution)/shard_map/ppermute | solution.py:201
  43.4 6.6 %collective-permute-start = (bf16[128,1024]{1,0:T(8,128)(2,1)}, bf16[128,1024]{1,0:T(8,128)(2,1)S(1)}, u32[]{:S(2)}, u32[]{:S(2)}) collective-permute-start(bf16[128,1024]{1,0:T(8,128)(2,1)} %gated.1.refs_0_), channel_id=1, source_target_pairs={{0,16},{16,0},{32,48},{48,32},{64,80},{80,64},{96,112},{112,96},{1... | collective-permute-start | bytes 786440 | tf_op jit(solution)/shard_map/ppermute | solution.py:197
  48.9 29.2 %copy-start.1 = (bf16[128,1024]{1,0:T(8,128)(2,1)}, bf16[128,1024]{1,0:T(8,128)(2,1)S(1)}, u32[]{:S(2)}) copy-start(bf16[128,1024]{1,0:T(8,128)(2,1)S(1)} %collective-permute-done.1.refs_2_) | copy-start | bytes 786436
  48.9 5.2 %collective-permute-start.3 = (bf16[128,1024]{1,0:T(8,128)(2,1)S(1)}, bf16[128,1024]{1,0:T(8,128)(2,1)S(1)}, u32[]{:S(2)}, u32[]{:S(2)}) collective-permute-start(bf16[128,1024]{1,0:T(8,128)(2,1)S(1)} %collective-permute-done.1.refs_2_), channel_id=1, source_target_pairs={{0,32},{16,240},{32,64},{48,16},{64,96},{80,48},{96,128},{112,80},... | collective-permute-start | bytes 786440 | tf_op jit(solution)/shard_map/ppermute | solution.py:201
  50.0 28.1 %copy-start.2 = (bf16[128,1024]{1,0:T(8,128)(2,1)}, bf16[128,1024]{1,0:T(8,128)(2,1)S(1)}, u32[]{:S(2)}) copy-start(bf16[128,1024]{1,0:T(8,128)(2,1)S(1)} %collective-permute-done.refs_1_) | copy-start | bytes 786436
  50.0 7.3 %collective-permute-start.2 = (bf16[128,1024]{1,0:T(8,128)(2,1)S(1)}, bf16[128,1024]{1,0:T(8,128)(2,1)S(1)}, u32[]{:S(2)}, u32[]{:S(2)}) collective-permute-start(bf16[128,1024]{1,0:T(8,128)(2,1)S(1)} %collective-permute-done.refs_1_), channel_id=1, source_target_pairs={{0,32},{16,240},{32,64},{48,16},{64,96},{80,48},{96,128},{112,80},... | collective-permute-start | bytes 786440 | tf_op jit(solution)/shard_map/ppermute | solution.py:201
  54.2 24.0 %copy-start.3 = (bf16[128,1024]{1,0:T(8,128)(2,1)}, bf16[128,1024]{1,0:T(8,128)(2,1)S(1)}, u32[]{:S(2)}) copy-start(bf16[128,1024]{1,0:T(8,128)(2,1)S(1)} %collective-permute-done.3.refs_4_) | copy-start | bytes 786436
  54.2 7.6 %collective-permute-start.5 = (bf16[128,1024]{1,0:T(8,128)(2,1)S(1)}, bf16[128,1024]{1,0:T(8,128)(2,1)S(1)}, u32[]{:S(2)}, u32[]{:S(2)}) collective-permute-start(bf16[128,1024]{1,0:T(8,128)(2,1)S(1)} %collective-permute-done.3.refs_4_), channel_id=1, source_target_pairs={{0,32},{16,240},{32,64},{48,16},{64,96},{80,48},{96,128},{112,80},... | collective-permute-start | bytes 786440 | tf_op jit(solution)/shard_map/ppermute | solution.py:201
  57.3 20.9 %copy-start.4 = (bf16[128,1024]{1,0:T(8,128)(2,1)}, bf16[128,1024]{1,0:T(8,128)(2,1)S(1)}, u32[]{:S(2)}) copy-start(bf16[128,1024]{1,0:T(8,128)(2,1)S(1)} %collective-permute-done.2.refs_3_) | copy-start | bytes 786436
  57.3 7.4 %collective-permute-start.4 = (bf16[128,1024]{1,0:T(8,128)(2,1)S(1)}, bf16[128,1024]{1,0:T(8,128)(2,1)S(1)}, u32[]{:S(2)}, u32[]{:S(2)}) collective-permute-start(bf16[128,1024]{1,0:T(8,128)(2,1)S(1)} %collective-permute-done.2.refs_3_), channel_id=1, source_target_pairs={{0,32},{16,240},{32,64},{48,16},{64,96},{80,48},{96,128},{112,80},... | collective-permute-start | bytes 786440 | tf_op jit(solution)/shard_map/ppermute | solution.py:201
  59.2 10.0 %collective-permute-start.8 = (bf16[128,1024]{1,0:T(8,128)(2,1)S(1)}, bf16[128,1024]{1,0:T(8,128)(2,1)S(1)}, u32[]{:S(2)}, u32[]{:S(2)}) collective-permute-start(bf16[128,1024]{1,0:T(8,128)(2,1)S(1)} %collective-permute-done.1.refs_2_), channel_id=1, source_target_pairs={{0,16},{16,0},{32,48},{48,32},{64,80},{80,64},{96,112},{112,96},{1... | collective-permute-start | bytes 786440 | tf_op jit(solution)/shard_map/ppermute | solution.py:202
  61.7 7.7 %collective-permute-start.10 = (bf16[128,1024]{1,0:T(8,128)(2,1)S(1)}, bf16[128,1024]{1,0:T(8,128)(2,1)S(1)}, u32[]{:S(2)}, u32[]{:S(2)}) collective-permute-start(bf16[128,1024]{1,0:T(8,128)(2,1)S(1)} %collective-permute-done.3.refs_4_), channel_id=1, source_target_pairs={{0,16},{16,0},{32,48},{48,32},{64,80},{80,64},{96,112},{112,96},{1... | collective-permute-start | bytes 786440 | tf_op jit(solution)/shard_map/ppermute | solution.py:202
  61.7 16.4 %copy-start.5 = (bf16[128,1024]{1,0:T(8,128)(2,1)}, bf16[128,1024]{1,0:T(8,128)(2,1)S(1)}, u32[]{:S(2)}) copy-start(bf16[128,1024]{1,0:T(8,128)(2,1)S(1)} %collective-permute-done.5.refs_6_) | copy-start | bytes 786436
  61.8 8.0 %collective-permute-start.7 = (bf16[128,1024]{1,0:T(8,128)(2,1)S(1)}, bf16[128,1024]{1,0:T(8,128)(2,1)S(1)}, u32[]{:S(2)}, u32[]{:S(2)}) collective-permute-start(bf16[128,1024]{1,0:T(8,128)(2,1)S(1)} %collective-permute-done.5.refs_6_), channel_id=1, source_target_pairs={{0,32},{16,240},{32,64},{48,16},{64,96},{80,48},{96,128},{112,80},... | collective-permute-start | bytes 786440 | tf_op jit(solution)/shard_map/ppermute | solution.py:201
  64.7 13.4 %copy-start.6 = (bf16[128,1024]{1,0:T(8,128)(2,1)}, bf16[128,1024]{1,0:T(8,128)(2,1)S(1)}, u32[]{:S(2)}) copy-start(bf16[128,1024]{1,0:T(8,128)(2,1)S(1)} %collective-permute-done.4.refs_5_) | copy-start | bytes 786436
  64.7 9.3 %collective-permute-start.6 = (bf16[128,1024]{1,0:T(8,128)(2,1)S(1)}, bf16[128,1024]{1,0:T(8,128)(2,1)S(1)}, u32[]{:S(2)}, u32[]{:S(2)}) collective-permute-start(bf16[128,1024]{1,0:T(8,128)(2,1)S(1)} %collective-permute-done.4.refs_5_), channel_id=1, source_target_pairs={{0,32},{16,240},{32,64},{48,16},{64,96},{80,48},{96,128},{112,80},... | collective-permute-start | bytes 786440 | tf_op jit(solution)/shard_map/ppermute | solution.py:201
  65.7 11.1 %collective-permute-start.9 = (bf16[128,1024]{1,0:T(8,128)(2,1)S(1)}, bf16[128,1024]{1,0:T(8,128)(2,1)S(1)}, u32[]{:S(2)}, u32[]{:S(2)}) collective-permute-start(bf16[128,1024]{1,0:T(8,128)(2,1)S(1)} %collective-permute-done.2.refs_3_), channel_id=1, source_target_pairs={{0,16},{16,0},{32,48},{48,32},{64,80},{80,64},{96,112},{112,96},{1... | collective-permute-start | bytes 786440 | tf_op jit(solution)/shard_map/ppermute | solution.py:202
  69.2 8.9 %copy-start.7 = (bf16[128,1024]{1,0:T(8,128)(2,1)}, bf16[128,1024]{1,0:T(8,128)(2,1)S(1)}, u32[]{:S(2)}) copy-start(bf16[128,1024]{1,0:T(8,128)(2,1)S(1)} %collective-permute-done.8.refs_9_) | copy-start | bytes 786436
  69.2 7.6 %collective-permute-start.12 = (bf16[128,1024]{1,0:T(8,128)(2,1)S(1)}, bf16[128,1024]{1,0:T(8,128)(2,1)S(1)}, u32[]{:S(2)}, u32[]{:S(2)}) collective-permute-start(bf16[128,1024]{1,0:T(8,128)(2,1)S(1)} %collective-permute-done.5.refs_6_), channel_id=1, source_target_pairs={{0,16},{16,0},{32,48},{48,32},{64,80},{80,64},{96,112},{112,96},{1... | collective-permute-start | bytes 786440 | tf_op jit(solution)/shard_map/ppermute | solution.py:202
  69.4 8.8 %copy-start.8 = (bf16[128,1024]{1,0:T(8,128)(2,1)}, bf16[128,1024]{1,0:T(8,128)(2,1)S(1)}, u32[]{:S(2)}) copy-start(bf16[128,1024]{1,0:T(8,128)(2,1)S(1)} %collective-permute-done.10.refs_11_) | copy-start | bytes 786436
  69.4 7.5 %collective-permute-start.11 = (bf16[128,1024]{1,0:T(8,128)(2,1)S(1)}, bf16[128,1024]{1,0:T(8,128)(2,1)S(1)}, u32[]{:S(2)}, u32[]{:S(2)}) collective-permute-start(bf16[128,1024]{1,0:T(8,128)(2,1)S(1)} %collective-permute-done.4.refs_5_), channel_id=1, source_target_pairs={{0,16},{16,0},{32,48},{48,32},{64,80},{80,64},{96,112},{112,96},{1... | collective-permute-start | bytes 786440 | tf_op jit(solution)/shard_map/ppermute | solution.py:202
  69.8 7.1 %collective-permute-start.14 = (bf16[128,1024]{1,0:T(8,128)(2,1)S(1)}, bf16[128,1024]{1,0:T(8,128)(2,1)S(1)}, u32[]{:S(2)}, u32[]{:S(2)}) collective-permute-start(bf16[128,1024]{1,0:T(8,128)(2,1)S(1)} %collective-permute-done.7.refs_8_), channel_id=1, source_target_pairs={{0,16},{16,0},{32,48},{48,32},{64,80},{80,64},{96,112},{112,96},{1... | collective-permute-start | bytes 786440 | tf_op jit(solution)/shard_map/ppermute | solution.py:202
  74.0 4.1 %collective-permute-start.13 = (bf16[128,1024]{1,0:T(8,128)(2,1)S(1)}, bf16[128,1024]{1,0:T(8,128)(2,1)}, u32[]{:S(2)}, u32[]{:S(2)}) collective-permute-start(bf16[128,1024]{1,0:T(8,128)(2,1)S(1)} %collective-permute-done.6.refs_7_), channel_id=1, source_target_pairs={{0,16},{16,0},{32,48},{48,32},{64,80},{80,64},{96,112},{112,96},{1... | collective-permute-start | bytes 786440 | tf_op jit(solution)/shard_map/ppermute | solution.py:202
  (7 other events, 18.1 us)

commit v3 on v2

--- a/solution.py
+++ b/solution.py
@@ -78,7 +78,8 @@
 
 
 def gated_kernel(
-    delta_ref, u_ref, z_ref, bc_ref, a_ref, skip_ref, start_ref, out_ref, d_t, w_t, bc_t, y_t, a_t,
+    delta_ref, u_ref, z_ref, bc_ref, a_ref, skip_ref, start_ref, top_ref, low_ref,
+    d_t, w_t, bc_t, y_t, a_t,
 ):
     rows, channels = delta_ref.shape
     groups = channels // LANES
@@ -124,28 +125,35 @@
         u = u_ref[:, lanes(g)].astype(jnp.float32)
         z = z_ref[:, lanes(g)].astype(jnp.float32)
         mixed = y + skip_ref[:, lanes(g)] * u
-        out_ref[:, lanes(g)] = (mixed * (z / (1.0 + jnp.exp(-z)))).astype(jnp.bfloat16)
-
-
-def project_kernel(count, me_ref, *refs):
-    blocks, w_ref, out_ref = refs[:count], refs[count], refs[count + 1]
+        gated = (mixed * (z / (1.0 + jnp.exp(-z)))).astype(jnp.bfloat16)
+        top_ref[:, lanes(g)] = gated[: rows // 2]
+        low_ref[:, lanes(g)] = gated[rows // 2 :]
+
+
+def project_kernel(places, me_ref, w_ref, *refs):
+    units = len(places)
+    blocks, out_ref, joined, result, sems = refs[:units], *refs[-4:]
     rows = blocks[0].shape[0]
+    count = out_ref.shape[0] // (2 * rows)
     me = me_ref[0]
-    core = lax.rem(me, 2)
-    chip = me - core
-    way = 2 - 4 * core
-    units = (count - 2) // 2
-    homes = [chip + core, chip + 1 - core]
-    for side in (-1, 1):
-        for unit in range(units):
-            same = (unit % 2 == 0) == (side == -1)
-            parity = core if same else 1 - core
-            homes.append(chip + side * way * (unit // 2 + 1) + parity)
-    for block, home in zip(blocks, homes):
-        at = pl.multiple_of(lax.rem(home + 2 * count, count) * rows, rows)
-        out_ref[pl.ds(at, rows), :] = jnp.dot(
-            block[...], w_ref[...], preferred_element_type=jnp.float32
-        ).astype(jnp.bfloat16)
+    partner = me + 1 - 2 * lax.rem(me, 2)
+    for i, block in enumerate(blocks):
+        joined[i * rows : (i + 1) * rows, :] = block[...]
+    result[...] = jnp.dot(
+        joined[...], w_ref[...], preferred_element_type=jnp.float32
+    ).astype(jnp.bfloat16)
+    copies = []
+    for i, (side, offset, half) in enumerate(places):
+        home = lax.rem((partner if side else me) + 2 * offset, count)
+        at = pl.multiple_of((2 * home + half) * rows, rows)
+        copies.append(
+            pltpu.make_async_copy(
+                result.at[pl.ds(i * rows, rows), :], out_ref.at[pl.ds(at, rows), :], sems.at[i]
+            )
+        )
+        copies[-1].start()
+    for copy in copies:
+        copy.wait()
 
 
 def whole():
@@ -181,32 +189,58 @@
         name="carry",
     )(me, ends, a_rate)
     entering = lax.all_to_all(entering, "ctx", split_axis=0, concat_axis=0, tiled=True)
-    gated = pl.pallas_call(
+    half_block = jax.ShapeDtypeStruct((rows // 2, channels), jnp.bfloat16)
+    halves = pl.pallas_call(
         gated_kernel,
-        out_shape=jax.ShapeDtypeStruct((rows, channels), jnp.bfloat16),
+        out_shape=(half_block, half_block),
         in_specs=[whole()] * 7,
-        out_specs=whole(),
+        out_specs=(whole(), whole()),
         scratch_shapes=[
             flat, flat, pltpu.VMEM((rows * 2 * states, LANES), jnp.float32), flat, rates
         ],
         name="gated",
     )(delta, u_in, z_in, bc_proj, a_rate, d_skip.reshape(1, channels), entering)
 
-    ring = [(i, (i + 2 - 4 * (i % 2)) % count) for i in range(count)]
+    up = [(i, (i + 2) % count) for i in range(count)]
+    down = [(i, (i - 2) % count) for i in range(count)]
     trade = [(i, i ^ 1) for i in range(count)]
-    local = [gated, lax.ppermute(gated, "ctx", trade)]
-    arrived = []
-    for unit in range(count // 2 - 1):
-        source = (local + arrived)[unit]
-        arrived.append(lax.ppermute(source, "ctx", ring))
-    traded = [lax.ppermute(value, "ctx", trade) for value in arrived]
-    terms = pl.pallas_call(
-        functools.partial(project_kernel, count),
-        out_shape=jax.ShapeDtypeStruct((rows * count, width), jnp.bfloat16),
-        in_specs=[smem] + [whole()] * (count + 1),
-        out_specs=whole(),
-        name="project",
-    )(me, *local, *arrived, *traded, w_out)
+    chips = count // 2
+    held = {(0, h): value for h, value in enumerate(halves)}
+    for s in range(1, chips // 2 + 1):
+        for h in range(2):
+            if s < chips - s or h == 0:
+                held[chips - s, h] = lax.ppermute(held[(chips - s + 1) % chips, h], "ctx", up)
+            if s < chips - s or h == 1:
+                held[s, h] = lax.ppermute(held[s - 1, h], "ctx", down)
+    late = range(chips // 2 - 1, chips // 2 + 2)
+    terms = None
+    for now in (False, True):
+        keys = [key for key in held if (key[0] in late) == now]
+        places = [(0, *key) for key in keys] + [(1, *key) for key in keys]
+        blocks = [held[key] for key in keys]
+        blocks += [lax.ppermute(value, "ctx", trade) for value in blocks]
+        done = [] if terms is None else [terms]
+        tall = len(places) * (rows // 2)
+        terms = pl.pallas_call(
+            functools.partial(project_kernel, tuple(places)),
+            out_shape=jax.ShapeDtypeStruct((rows * count, width), jnp.bfloat16),
+            in_specs=[smem]
+            + [whole()] * (len(places) + 1)
+            + [pl.BlockSpec(memory_space=pl.ANY)] * len(done),
+            out_specs=pl.BlockSpec(memory_space=pl.ANY),
+            scratch_shapes=[
+                pltpu.VMEM((tall, channels), jnp.bfloat16),
+                pltpu.VMEM((tall, width), jnp.bfloat16),
+                pltpu.SemaphoreType.DMA((len(places),)),
+            ],
+            input_output_aliases={len(places) + 2: 0} if done else {},
+            cost_estimate=pl.CostEstimate(
+                flops=2 * tall * channels * width,
+                bytes_accessed=2 * tall * (channels + width),
+                transcendentals=0,
+            ),
+            name="project",
+        )(me, w_out, *blocks, *done)
 
     received = lax.all_to_all(
         terms.reshape(count, rows, width), "exp", split_axis=0, concat_axis=0

time: 120 us -> 122 us (1.017)
  waiting for transfers between devices: 19.4 us -> 12.4 us
  starting transfers between devices: 33.8 us -> 39.9 us
  Pallas kernels: 18.2 us -> 20.6 us
    ppermute x15 -> x30, waiting for transfers between devices: 10.3 us -> 3.2 us  [the longest x7 2.87 us: body(): lax.ppermute(held[(chips - s + 1) % chips, h], 'ctx', up)]
    ppermute x15 -> x30, starting transfers between devices: 23.8 us -> 29.9 us  [the longest x7 15.4 us: body(): held[s, h] = lax.ppermute(held[s - 1, h], 'ctx', down)]
    pallas_call x2 -> x3, Pallas kernels: 12.5 us -> 14.9 us  [the longest x2 8.6 us: body(): pl.pallas_call(functools.partial(project_kernel, tuple(places)), out_shap...]
  transfers between devices with their start and end apart: 16 -> 31, of which waited for: 5 -> 5; matrix products, arithmetic and copies ran while one was open for 0% -> 0% of each run, Pallas kernels for 0% -> 4%
where the time goes in v3:
time: 122 us
  blocking collectives  46 us (38%)
  starting transfers between devices  39.9 us (33%)
  Pallas kernels  20.6 us (17%)
  waiting for transfers between devices  12.4 us (10%)
  local copies, waits for them, and re-layouts  1.39 us (1%)
    all_to_all x1, blocking collectives, body(): lax.all_to_all(terms.reshape(count, rows, width), 'exp', split_axis=0, co...  34.7 us
    ppermute x7, starting transfers between devices, body(): held[s, h] = lax.ppermute(held[s - 1, h], 'ctx', down)  15.4 us
    ppermute x16, starting transfers between devices, body(): blocks += [lax.ppermute(value, 'ctx', trade) for value in blocks]  13.8 us
    all_to_all x1, blocking collectives, body(): lax.all_to_all(entering, 'ctx', split_axis=0, concat_axis=0, tiled=True)  11.4 us
    all_to_all x1, starting transfers between devices, body(): ends = lax.all_to_all(ends, 'ctx', split_axis=0, concat_axis=0, tiled=True)  9.98 us
    all_to_all x1, waiting for transfers between devices, body(): ends = lax.all_to_all(ends, 'ctx', split_axis=0, concat_axis=0, tiled=True)  9.17 us
    pallas_call x2, Pallas kernels, body(): pl.pallas_call(functools.partial(project_kernel, tuple(places)), out_shap...  8.6 us
    pallas_call x1, Pallas kernels, body(): pl.pallas_call(gated_kernel, out_shape=(half_block, half_block), in_specs...  6.29 us
  transfers between devices with their start and end apart: 31, of which 5 were waited for; matrix products, arithmetic and copies ran while one was open for 0% of the time, Pallas kernels for 4%

profile of v3, /device:TPU:1, one launch (start us, length us, event | category | flops | bytes accessed | tf_op | source)
XLA Modules:
  0.0 121.5 jit_solution(1606773194282189969)
XLA Ops:
  0.0 4.1 %end_state.1 = f32[256,128]{1,0:T(8,128)} custom-call(f32[128,1024]{1,0:T(8,128)} %delta_ref.3, bf16[128,1024]{1,0:T(8,128)(2,1)} %u_ref.3, f32[32,128]{1,0:T(8,128)} %bc_ref.3, f32[16,1024]{1,0:T(8,128)} %a_ref.5), custom_call_target="tpu_custom_call" | custom-call | tf_op jit(solution)/shard_map/end_state/pallas_call | solution.py:174
  4.1 10.0 %all-to-all-start = ((f32[16,16,128]{2,1,0:T(8,128)}), f32[16,16,128]{2,1,0:T(8,128)S(1)}, u32[]{:S(2)}, u32[]{:S(2)}) async-start(f32[16,16,128]{2,1,0:T(8,128)} %bitcast.8), calls=%async_computation | async-start | bytes 262144 | tf_op jit(solution)/shard_map/all_to_all | solution.py:182
  14.1 9.2 %all-to-all-done = f32[16,16,128]{2,1,0:T(8,128)S(1)} async-done(((f32[16,16,128]{2,1,0:T(8,128)}), f32[16,16,128]{2,1,0:T(8,128)S(1)}, u32[]{:S(2)}, u32[]{:S(2)}) %all-to-all-start) | async-done | bytes 131104 | tf_op jit(solution)/shard_map/all_to_all | solution.py:182
  23.9 1.6 %carry.1 = f32[128,128]{1,0:T(8,128)} custom-call(s32[1]{0:T(128)} %bitcast.me_ref, f32[256,128]{1,0:T(8,128)} %bitcast.9, f32[16,1024]{1,0:T(8,128)} %a_ref.5), custom_call_target="tpu_custom_call" | custom-call | tf_op jit(solution)/shard_map/carry/pallas_call | solution.py:183
  25.5 11.4 %all_to_all.27 = f32[16,8,128]{2,1,0:T(8,128)} all-to-all(f32[16,8,128]{2,1,0:T(8,128)} %bitcast.11), channel_id=1, replica_groups=mesh['ctx'=16,'exp'=16] {'ctx'}, dimensions={0} | all-to-all | bytes 131072 | tf_op jit(solution)/shard_map/all_to_all | solution.py:191
  36.9 6.3 %gated.1 = (bf16[64,1024]{1,0:T(8,128)(2,1)}, bf16[64,1024]{1,0:T(8,128)(2,1)}) custom-call(f32[128,1024]{1,0:T(8,128)} %delta_ref.3, bf16[128,1024]{1,0:T(8,128)(2,1)} %u_ref.3, bf16[128,1024]{1,0:T(8,128)(2,1)} %z_ref.1, f32[32,128]{1,0:T(8,128)} %bc_ref.3, f32[16,1024]{1,0:T(8,128)} %a_ref.5, f32[1,1024]{1,0:T(1,128)} %bitcast.12, f32[128,128]{1,0:T(8,128)} %bitcast.10), custom_call_target="tpu_custom_call" | custom-call | tf_op jit(solution)/shard_map/gated/pallas_call | solution.py:193
  43.4 2.4 %collective-permute-start.3 = (bf16[64,1024]{1,0:T(8,128)(2,1)}, bf16[64,1024]{1,0:T(8,128)(2,1)S(1)}, u32[]{:S(2)}, u32[]{:S(2)}) collective-permute-start(bf16[64,1024]{1,0:T(8,128)(2,1)} %get-tuple-element.7.refs_0_), channel_id=1, source_target_pairs={{0,224},{16,240},{32,0},{48,16},{64,32},{80,48},{96,64},{112,80},{... | collective-permute-start | bytes 393224 | tf_op jit(solution)/shard_map/ppermute | solution.py:214
  45.8 2.7 %collective-permute-start.9 = (bf16[64,1024]{1,0:T(8,128)(2,1)}, bf16[64,1024]{1,0:T(8,128)(2,1)S(1)}, u32[]{:S(2)}, u32[]{:S(2)}) collective-permute-start(bf16[64,1024]{1,0:T(8,128)(2,1)} %get-tuple-element.8.refs_1_), channel_id=1, source_target_pairs={{0,224},{16,240},{32,0},{48,16},{64,32},{80,48},{96,64},{112,80},{... | collective-permute-start | bytes 393224 | tf_op jit(solution)/shard_map/ppermute | solution.py:214
  48.5 1.4 %collective-permute-start.20 = (bf16[64,1024]{1,0:T(8,128)(2,1)}, bf16[64,1024]{1,0:T(8,128)(2,1)S(1)}, u32[]{:S(2)}, u32[]{:S(2)}) collective-permute-start(bf16[64,1024]{1,0:T(8,128)(2,1)} %get-tuple-element.7.refs_0_), channel_id=1, source_target_pairs={{0,16},{16,0},{32,48},{48,32},{64,80},{80,64},{96,112},{112,96},{1... | collective-permute-start | bytes 393224 | tf_op jit(solution)/shard_map/ppermute | solution.py:221
  50.6 1.2 collective-permute-done.6.refs_4_
  51.7 1.5 %collective-permute-start.4 = (bf16[64,1024]{1,0:T(8,128)(2,1)S(1)}, bf16[64,1024]{1,0:T(8,128)(2,1)S(1)}, u32[]{:S(2)}, u32[]{:S(2)}) collective-permute-start(bf16[64,1024]{1,0:T(8,128)(2,1)S(1)} %collective-permute-done.3.refs_3_), channel_id=1, source_target_pairs={{0,224},{16,240},{32,0},{48,16},{64,32},{80,48},{96,64},{112,80},{... | collective-permute-start | bytes 393224 | tf_op jit(solution)/shard_map/ppermute | solution.py:214
  53.3 2.7 %collective-permute-start.10 = (bf16[64,1024]{1,0:T(8,128)(2,1)S(1)}, bf16[64,1024]{1,0:T(8,128)(2,1)S(1)}, u32[]{:S(2)}, u32[]{:S(2)}) collective-permute-start(bf16[64,1024]{1,0:T(8,128)(2,1)S(1)} %collective-permute-done.9.refs_5_), channel_id=1, source_target_pairs={{0,224},{16,240},{32,0},{48,16},{64,32},{80,48},{96,64},{112,80},{... | collective-permute-start | bytes 393224 | tf_op jit(solution)/shard_map/ppermute | solution.py:214
  56.0 1.2 collective-permute-start.22
  57.8 1.5 %collective-permute-start.24 = (bf16[64,1024]{1,0:T(8,128)(2,1)S(1)}, bf16[64,1024]{1,0:T(8,128)(2,1)S(1)}, u32[]{:S(2)}, u32[]{:S(2)}) collective-permute-start(bf16[64,1024]{1,0:T(8,128)(2,1)S(1)} %collective-permute-done.6.refs_4_), channel_id=1, source_target_pairs={{0,16},{16,0},{32,48},{48,32},{64,80},{80,64},{96,112},{112,96},{1... | collective-permute-start | bytes 393224 | tf_op jit(solution)/shard_map/ppermute | solution.py:221
  59.3 1.2 %collective-permute-start.25 = (bf16[64,1024]{1,0:T(8,128)(2,1)S(1)}, bf16[64,1024]{1,0:T(8,128)(2,1)S(1)}, u32[]{:S(2)}, u32[]{:S(2)}) collective-permute-start(bf16[64,1024]{1,0:T(8,128)(2,1)S(1)} %collective-permute-done.9.refs_5_), channel_id=1, source_target_pairs={{0,16},{16,0},{32,48},{48,32},{64,80},{80,64},{96,112},{112,96},{1... | collective-permute-start | bytes 393224 | tf_op jit(solution)/shard_map/ppermute | solution.py:221
  61.5 2.4 %collective-permute-start.11 = (bf16[64,1024]{1,0:T(8,128)(2,1)S(1)}, bf16[64,1024]{1,0:T(8,128)(2,1)S(1)}, u32[]{:S(2)}, u32[]{:S(2)}) collective-permute-start(bf16[64,1024]{1,0:T(8,128)(2,1)S(1)} %collective-permute-done.10.refs_9_), channel_id=1, source_target_pairs={{0,224},{16,240},{32,0},{48,16},{64,32},{80,48},{96,64},{112,80},{... | collective-permute-start | bytes 393224 | tf_op jit(solution)/shard_map/ppermute | solution.py:214
  64.8 1.1 collective-permute-start.5
  67.2 2.7 %collective-permute-start.13 = (bf16[64,1024]{1,0:T(8,128)(2,1)S(1)}, bf16[64,1024]{1,0:T(8,128)(2,1)S(1)}, u32[]{:S(2)}, u32[]{:S(2)}) collective-permute-start(bf16[64,1024]{1,0:T(8,128)(2,1)S(1)} %collective-permute-done.11.refs_3_), channel_id=1, source_target_pairs={{0,224},{16,240},{32,0},{48,16},{64,32},{80,48},{96,64},{112,80},{... | collective-permute-start | bytes 393224 | tf_op jit(solution)/shard_map/ppermute | solution.py:214
  69.9 2.3 %collective-permute-start.14 = (bf16[64,1024]{1,0:T(8,128)(2,1)S(1)}, bf16[64,1024]{1,0:T(8,128)(2,1)S(1)}, u32[]{:S(2)}, u32[]{:S(2)}) collective-permute-start(bf16[64,1024]{1,0:T(8,128)(2,1)S(1)} %collective-permute-done.2.refs_0_), channel_id=1, source_target_pairs={{0,16},{16,0},{32,48},{48,32},{64,80},{80,64},{96,112},{112,96},{1... | collective-permute-start | bytes 393224 | tf_op jit(solution)/shard_map/ppermute | solution.py:221
  72.3 1.5 %collective-permute-start.15 = (bf16[64,1024]{1,0:T(8,128)(2,1)S(1)}, bf16[64,1024]{1,0:T(8,128)(2,1)S(1)}, u32[]{:S(2)}, u32[]{:S(2)}) collective-permute-start(bf16[64,1024]{1,0:T(8,128)(2,1)S(1)} %collective-permute-done.5.refs_1_), channel_id=1, source_target_pairs={{0,16},{16,0},{32,48},{48,32},{64,80},{80,64},{96,112},{112,96},{1... | collective-permute-start | bytes 393224 | tf_op jit(solution)/shard_map/ppermute | solution.py:221
  74.6 1.2 collective-permute-start.16
  76.5 4.8 %project.2.refs_12_ = bf16[2048,512]{1,0:T(8,128)(2,1)} custom-call(s32[1]{0:T(128)} %bitcast.me_ref, bf16[1024,512]{1,0:T(8,128)(2,1)} %w_ref.3, bf16[64,1024]{1,0:T(8,128)(2,1)} %get-tuple-element.7.refs_0_, bf16[64,1024]{1,0:T(8,128)(2,1)} %get-tuple-element.8.refs_1_, bf16[64,1024]{1,0:T(8,128)(2,1)} %copy-done.1, bf16[64,1024]{1,0:T(8,128)(2,1)} %copy-done.2, ...), custom_call_target="tpu_custom_call" | custom-call | flops 1342177280 | bytes 3932160 | tf_op jit(solution)/shard_map/project/pallas_call | solution.py:224
  82.1 3.8 %project.3 = bf16[2048,512]{1,0:T(8,128)(2,1)} custom-call(s32[1]{0:T(128)} %bitcast.me_ref, bf16[1024,512]{1,0:T(8,128)(2,1)} %w_ref.3, bf16[64,1024]{1,0:T(8,128)(2,1)} %copy-done.16, bf16[64,1024]{1,0:T(8,128)(2,1)} %copy-done.20, bf16[64,1024]{1,0:T(8,128)(2,1)} %copy-done.21, bf16[64,1024]{1,0:T(8,128)(2,1)} %copy-done.18, ...), custom_call_target="tpu_custom_call", output_to_operand_aliasing={{}: (14, {})} | custom-call | flops 805306368 | bytes 2359296 | tf_op jit(solution)/shard_map/project/pallas_call | solution.py:224
  85.9 34.7 %all_to_all.28 = bf16[16,128,512]{2,1,0:T(8,128)(2,1)S(1)} all-to-all(bf16[16,128,512]{2,1,0:T(8,128)(2,1)} %bitcast.7), channel_id=1, replica_groups=mesh['ctx'=16,'exp'=16] {'exp'}, dimensions={0} | all-to-all | bytes 4194304 | tf_op jit(solution)/shard_map/all_to_all | solution.py:245
  (102 shorter events, 8.5 us)
Async XLA Ops:
  4.1 19.1 %all-to-all-start = ((f32[16,16,128]{2,1,0:T(8,128)}), f32[16,16,128]{2,1,0:T(8,128)S(1)}, u32[]{:S(2)}, u32[]{:S(2)}) async-start(f32[16,16,128]{2,1,0:T(8,128)} %bitcast.8), calls=%async_computation | async-start | bytes 262144 | tf_op jit(solution)/shard_map/all_to_all | solution.py:182
  43.2 6.7 %collective-permute-start = (bf16[64,1024]{1,0:T(8,128)(2,1)}, bf16[64,1024]{1,0:T(8,128)(2,1)S(1)}, u32[]{:S(2)}, u32[]{:S(2)}) collective-permute-start(bf16[64,1024]{1,0:T(8,128)(2,1)} %get-tuple-element.7.refs_0_), channel_id=1, source_target_pairs={{0,32},{16,48},{32,64},{48,80},{64,96},{80,112},{96,128},{112,144}... | collective-permute-start | bytes 393224 | tf_op jit(solution)/shard_map/ppermute | solution.py:212
  43.4 7.1 %collective-permute-start.3 = (bf16[64,1024]{1,0:T(8,128)(2,1)}, bf16[64,1024]{1,0:T(8,128)(2,1)S(1)}, u32[]{:S(2)}, u32[]{:S(2)}) collective-permute-start(bf16[64,1024]{1,0:T(8,128)(2,1)} %get-tuple-element.7.refs_0_), channel_id=1, source_target_pairs={{0,224},{16,240},{32,0},{48,16},{64,32},{80,48},{96,64},{112,80},{... | collective-permute-start | bytes 393224 | tf_op jit(solution)/shard_map/ppermute | solution.py:214
  45.8 5.9 %collective-permute-start.6 = (bf16[64,1024]{1,0:T(8,128)(2,1)}, bf16[64,1024]{1,0:T(8,128)(2,1)S(1)}, u32[]{:S(2)}, u32[]{:S(2)}) collective-permute-start(bf16[64,1024]{1,0:T(8,128)(2,1)} %get-tuple-element.8.refs_1_), channel_id=1, source_target_pairs={{0,32},{16,48},{32,64},{48,80},{64,96},{80,112},{96,128},{112,144}... | collective-permute-start | bytes 393224 | tf_op jit(solution)/shard_map/ppermute | solution.py:212
  45.8 7.4 %collective-permute-start.9 = (bf16[64,1024]{1,0:T(8,128)(2,1)}, bf16[64,1024]{1,0:T(8,128)(2,1)S(1)}, u32[]{:S(2)}, u32[]{:S(2)}) collective-permute-start(bf16[64,1024]{1,0:T(8,128)(2,1)} %get-tuple-element.8.refs_1_), channel_id=1, source_target_pairs={{0,224},{16,240},{32,0},{48,16},{64,32},{80,48},{96,64},{112,80},{... | collective-permute-start | bytes 393224 | tf_op jit(solution)/shard_map/ppermute | solution.py:214
  49.9 6.1 %collective-permute-start.21 = (bf16[64,1024]{1,0:T(8,128)(2,1)}, bf16[64,1024]{1,0:T(8,128)(2,1)S(1)}, u32[]{:S(2)}, u32[]{:S(2)}) collective-permute-start(bf16[64,1024]{1,0:T(8,128)(2,1)} %get-tuple-element.8.refs_1_), channel_id=1, source_target_pairs={{0,16},{16,0},{32,48},{48,32},{64,80},{80,64},{96,112},{112,96},{1... | collective-permute-start | bytes 393224 | tf_op jit(solution)/shard_map/ppermute | solution.py:221
  50.6 6.6 %collective-permute-start.1 = (bf16[64,1024]{1,0:T(8,128)(2,1)S(1)}, bf16[64,1024]{1,0:T(8,128)(2,1)S(1)}, u32[]{:S(2)}, u32[]{:S(2)}) collective-permute-start(bf16[64,1024]{1,0:T(8,128)(2,1)S(1)} %collective-permute-done.refs_2_), channel_id=1, source_target_pairs={{0,32},{16,48},{32,64},{48,80},{64,96},{80,112},{96,128},{112,144}... | collective-permute-start | bytes 393224 | tf_op jit(solution)/shard_map/ppermute | solution.py:212
  51.7 6.0 %collective-permute-start.4 = (bf16[64,1024]{1,0:T(8,128)(2,1)S(1)}, bf16[64,1024]{1,0:T(8,128)(2,1)S(1)}, u32[]{:S(2)}, u32[]{:S(2)}) collective-permute-start(bf16[64,1024]{1,0:T(8,128)(2,1)S(1)} %collective-permute-done.3.refs_3_), channel_id=1, source_target_pairs={{0,224},{16,240},{32,0},{48,16},{64,32},{80,48},{96,64},{112,80},{... | collective-permute-start | bytes 393224 | tf_op jit(solution)/shard_map/ppermute | solution.py:214
  53.3 6.0 %collective-permute-start.7 = (bf16[64,1024]{1,0:T(8,128)(2,1)S(1)}, bf16[64,1024]{1,0:T(8,128)(2,1)S(1)}, u32[]{:S(2)}, u32[]{:S(2)}) collective-permute-start(bf16[64,1024]{1,0:T(8,128)(2,1)S(1)} %collective-permute-done.6.refs_4_), channel_id=1, source_target_pairs={{0,32},{16,48},{32,64},{48,80},{64,96},{80,112},{96,128},{112,144}... | collective-permute-start | bytes 393224 | tf_op jit(solution)/shard_map/ppermute | solution.py:212
  53.3 7.2 %collective-permute-start.10 = (bf16[64,1024]{1,0:T(8,128)(2,1)S(1)}, bf16[64,1024]{1,0:T(8,128)(2,1)S(1)}, u32[]{:S(2)}, u32[]{:S(2)}) collective-permute-start(bf16[64,1024]{1,0:T(8,128)(2,1)S(1)} %collective-permute-done.9.refs_5_), channel_id=1, source_target_pairs={{0,224},{16,240},{32,0},{48,16},{64,32},{80,48},{96,64},{112,80},{... | collective-permute-start | bytes 393224 | tf_op jit(solution)/shard_map/ppermute | solution.py:214
  61.0 4.9 %collective-permute-start.28 = (bf16[64,1024]{1,0:T(8,128)(2,1)S(1)}, bf16[64,1024]{1,0:T(8,128)(2,1)S(1)}, u32[]{:S(2)}, u32[]{:S(2)}) collective-permute-start(bf16[64,1024]{1,0:T(8,128)(2,1)S(1)} %collective-permute-done.7.refs_8_), channel_id=1, source_target_pairs={{0,16},{16,0},{32,48},{48,32},{64,80},{80,64},{96,112},{112,96},{1... | collective-permute-start | bytes 393224 | tf_op jit(solution)/shard_map/ppermute | solution.py:221
  61.2 6.0 %collective-permute-start.2 = (bf16[64,1024]{1,0:T(8,128)(2,1)S(1)}, bf16[64,1024]{1,0:T(8,128)(2,1)S(1)}, u32[]{:S(2)}, u32[]{:S(2)}) collective-permute-start(bf16[64,1024]{1,0:T(8,128)(2,1)S(1)} %collective-permute-done.1.refs_6_), channel_id=1, source_target_pairs={{0,32},{16,48},{32,64},{48,80},{64,96},{80,112},{96,128},{112,144}... | collective-permute-start | bytes 393224 | tf_op jit(solution)/shard_map/ppermute | solution.py:212
  61.5 5.7 %collective-permute-start.11 = (bf16[64,1024]{1,0:T(8,128)(2,1)S(1)}, bf16[64,1024]{1,0:T(8,128)(2,1)S(1)}, u32[]{:S(2)}, u32[]{:S(2)}) collective-permute-start(bf16[64,1024]{1,0:T(8,128)(2,1)S(1)} %collective-permute-done.10.refs_9_), channel_id=1, source_target_pairs={{0,224},{16,240},{32,0},{48,16},{64,32},{80,48},{96,64},{112,80},{... | collective-permute-start | bytes 393224 | tf_op jit(solution)/shard_map/ppermute | solution.py:214
  63.9 6.0 %collective-permute-start.29 = (bf16[64,1024]{1,0:T(8,128)(2,1)S(1)}, bf16[64,1024]{1,0:T(8,128)(2,1)S(1)}, u32[]{:S(2)}, u32[]{:S(2)}) collective-permute-start(bf16[64,1024]{1,0:T(8,128)(2,1)S(1)} %collective-permute-done.10.refs_9_), channel_id=1, source_target_pairs={{0,16},{16,0},{32,48},{48,32},{64,80},{80,64},{96,112},{112,96},{1... | collective-permute-start | bytes 393224 | tf_op jit(solution)/shard_map/ppermute | solution.py:221
  64.8 7.3 %collective-permute-start.5 = (bf16[64,1024]{1,0:T(8,128)(2,1)S(1)}, bf16[64,1024]{1,0:T(8,128)(2,1)S(1)}, u32[]{:S(2)}, u32[]{:S(2)}) collective-permute-start(bf16[64,1024]{1,0:T(8,128)(2,1)S(1)} %collective-permute-done.4.refs_7_), channel_id=1, source_target_pairs={{0,224},{16,240},{32,0},{48,16},{64,32},{80,48},{96,64},{112,80},{... | collective-permute-start | bytes 393224 | tf_op jit(solution)/shard_map/ppermute | solution.py:214
  65.9 6.4 %collective-permute-start.8 = (bf16[64,1024]{1,0:T(8,128)(2,1)S(1)}, bf16[64,1024]{1,0:T(8,128)(2,1)S(1)}, u32[]{:S(2)}, u32[]{:S(2)}) collective-permute-start(bf16[64,1024]{1,0:T(8,128)(2,1)S(1)} %collective-permute-done.7.refs_8_), channel_id=1, source_target_pairs={{0,32},{16,48},{32,64},{48,80},{64,96},{80,112},{96,128},{112,144}... | collective-permute-start | bytes 393224 | tf_op jit(solution)/shard_map/ppermute | solution.py:212
  67.2 7.5 %collective-permute-start.12 = (bf16[64,1024]{1,0:T(8,128)(2,1)S(1)}, bf16[64,1024]{1,0:T(8,128)(2,1)S(1)}, u32[]{:S(2)}, u32[]{:S(2)}) collective-permute-start(bf16[64,1024]{1,0:T(8,128)(2,1)S(1)} %collective-permute-done.2.refs_0_), channel_id=1, source_target_pairs={{0,32},{16,48},{32,64},{48,80},{64,96},{80,112},{96,128},{112,144}... | collective-permute-start | bytes 393224 | tf_op jit(solution)/shard_map/ppermute | solution.py:212
  67.2 8.6 %collective-permute-start.13 = (bf16[64,1024]{1,0:T(8,128)(2,1)S(1)}, bf16[64,1024]{1,0:T(8,128)(2,1)S(1)}, u32[]{:S(2)}, u32[]{:S(2)}) collective-permute-start(bf16[64,1024]{1,0:T(8,128)(2,1)S(1)} %collective-permute-done.11.refs_3_), channel_id=1, source_target_pairs={{0,224},{16,240},{32,0},{48,16},{64,32},{80,48},{96,64},{112,80},{... | collective-permute-start | bytes 393224 | tf_op jit(solution)/shard_map/ppermute | solution.py:214
  69.9 6.1 %collective-permute-start.14 = (bf16[64,1024]{1,0:T(8,128)(2,1)S(1)}, bf16[64,1024]{1,0:T(8,128)(2,1)S(1)}, u32[]{:S(2)}, u32[]{:S(2)}) collective-permute-start(bf16[64,1024]{1,0:T(8,128)(2,1)S(1)} %collective-permute-done.2.refs_0_), channel_id=1, source_target_pairs={{0,16},{16,0},{32,48},{48,32},{64,80},{80,64},{96,112},{112,96},{1... | collective-permute-start | bytes 393224 | tf_op jit(solution)/shard_map/ppermute | solution.py:221
  72.2 9.3 %collective-permute-start.17 = (bf16[64,1024]{1,0:T(8,128)(2,1)S(1)}, bf16[64,1024]{1,0:T(8,128)(2,1)S(1)}, u32[]{:S(2)}, u32[]{:S(2)}) collective-permute-start(bf16[64,1024]{1,0:T(8,128)(2,1)S(1)} %collective-permute-done.11.refs_3_), channel_id=1, source_target_pairs={{0,16},{16,0},{32,48},{48,32},{64,80},{80,64},{96,112},{112,96},{1... | collective-permute-start | bytes 393224 | tf_op jit(solution)/shard_map/ppermute | solution.py:221
  72.3 9.2 %collective-permute-start.15 = (bf16[64,1024]{1,0:T(8,128)(2,1)S(1)}, bf16[64,1024]{1,0:T(8,128)(2,1)S(1)}, u32[]{:S(2)}, u32[]{:S(2)}) collective-permute-start(bf16[64,1024]{1,0:T(8,128)(2,1)S(1)} %collective-permute-done.5.refs_1_), channel_id=1, source_target_pairs={{0,16},{16,0},{32,48},{48,32},{64,80},{80,64},{96,112},{112,96},{1... | collective-permute-start | bytes 393224 | tf_op jit(solution)/shard_map/ppermute | solution.py:221
  74.6 6.8 %collective-permute-start.16 = (bf16[64,1024]{1,0:T(8,128)(2,1)S(1)}, bf16[64,1024]{1,0:T(8,128)(2,1)}, u32[]{:S(2)}, u32[]{:S(2)}) collective-permute-start(bf16[64,1024]{1,0:T(8,128)(2,1)S(1)} %collective-permute-done.8.refs_2_), channel_id=1, source_target_pairs={{0,16},{16,0},{32,48},{48,32},{64,80},{80,64},{96,112},{112,96},{1... | collective-permute-start | bytes 393224 | tf_op jit(solution)/shard_map/ppermute | solution.py:221
  75.8 5.7 %collective-permute-start.18 = (bf16[64,1024]{1,0:T(8,128)(2,1)S(1)}, bf16[64,1024]{1,0:T(8,128)(2,1)}, u32[]{:S(2)}, u32[]{:S(2)}) collective-permute-start(bf16[64,1024]{1,0:T(8,128)(2,1)S(1)} %collective-permute-done.12.refs_4_), channel_id=1, source_target_pairs={{0,16},{16,0},{32,48},{48,32},{64,80},{80,64},{96,112},{112,96},{1... | collective-permute-start | bytes 393224 | tf_op jit(solution)/shard_map/ppermute | solution.py:221
  75.9 5.6 %collective-permute-start.19 = (bf16[64,1024]{1,0:T(8,128)(2,1)S(1)}, bf16[64,1024]{1,0:T(8,128)(2,1)}, u32[]{:S(2)}, u32[]{:S(2)}) collective-permute-start(bf16[64,1024]{1,0:T(8,128)(2,1)S(1)} %collective-permute-done.13.refs_5_), channel_id=1, source_target_pairs={{0,16},{16,0},{32,48},{48,32},{64,80},{80,64},{96,112},{112,96},{1... | collective-permute-start | bytes 393224 | tf_op jit(solution)/shard_map/ppermute | solution.py:221
  (35 other events, 410.2 us)

commit v4 on v2

--- a/solution.py
+++ b/solution.py
@@ -77,9 +77,7 @@
         state = jnp.exp2(total * rate) * state + ends_ref[base : base + SUB, :]
 
 
-def gated_kernel(
-    delta_ref, u_ref, z_ref, bc_ref, a_ref, skip_ref, start_ref, out_ref, d_t, w_t, bc_t, y_t, a_t,
-):
+def local_kernel(delta_ref, u_ref, bc_ref, a_ref, y_ref, sum_ref, c_ref, d_t, w_t, b_t, a_t):
     rows, channels = delta_ref.shape
     groups = channels // LANES
     states = a_ref.shape[0]
@@ -94,30 +92,60 @@
         groups,
         lambda g: delta_ref[:, lanes(g)] * u_ref[:, lanes(g)].astype(jnp.float32),
     )
-    fill_coefficients(bc_t, bc_ref[...], rows, 2 * states)
+    fill_coefficients(b_t, bc_ref[:states, :], rows, states)
+    fill_coefficients(c_ref, bc_ref[states:, :], rows, states)
     fill_transposed(a_t, states, groups, lambda g: a_ref[:, lanes(g)])
     rate = [a_t[n * groups : (n + 1) * groups, :] * NEG_LOG2E for n in range(states)]
 
-    start = [start_ref[n * groups : (n + 1) * groups, :] for n in range(states)]
-
-    def step(t, state):
-        d = d_t[pl.ds(pl.multiple_of(t * groups, groups), groups), :]
-        w = w_t[pl.ds(pl.multiple_of(t * groups, groups), groups), :]
+    def step(t, carry):
+        total, state = carry
+        at = pl.ds(pl.multiple_of(t * groups, groups), groups)
+        d = d_t[at, :]
+        w = w_t[at, :]
         new = []
         parts = [None] * 4
         for n in range(states):
-            b = bc_t[pl.ds(t * 2 * states + n, groups, stride=0), :]
-            c = bc_t[pl.ds(t * 2 * states + states + n, groups, stride=0), :]
+            b = b_t[pl.ds(t * states + n, groups, stride=0), :]
+            c = c_ref[pl.ds(t * states + n, groups, stride=0), :]
             s = jnp.exp2(d * rate[n]) * state[n] + w * b
             new.append(s)
             term = s * c
             parts[n % 4] = term if parts[n % 4] is None else parts[n % 4] + term
-        y_t[pl.ds(pl.multiple_of(t * groups, groups), groups), :] = (parts[0] + parts[1]) + (
-            parts[2] + parts[3]
-        )
-        return tuple(new)
-
-    lax.fori_loop(0, rows, step, tuple(start), unroll=4)
+        y_ref[at, :] = (parts[0] + parts[1]) + (parts[2] + parts[3])
+        total = total + d
+        sum_ref[at, :] = total
+        return total, tuple(new)
+
+    zero = jnp.zeros((groups, LANES), jnp.float32)
+    lax.fori_loop(0, rows, step, (zero, (zero,) * states), unroll=4)
+
+
+def gated_kernel(
+    u_ref, z_ref, a_ref, skip_ref, start_ref, y_ref, sum_ref, c_ref, out_ref, y_t, a_t
+):
+    rows, channels = u_ref.shape
+    groups = channels // LANES
+    states = a_ref.shape[0]
+
+    def lanes(g):
+        return slice(g * LANES, (g + 1) * LANES)
+
+    fill_transposed(a_t, states, groups, lambda g: a_ref[:, lanes(g)])
+    rate = [a_t[n * groups : (n + 1) * groups, :] * NEG_LOG2E for n in range(states)]
+    start = [start_ref[n * groups : (n + 1) * groups, :] for n in range(states)]
+
+    def step(t, carry):
+        at = pl.ds(pl.multiple_of(t * groups, groups), groups)
+        total = sum_ref[at, :]
+        parts = [None] * 4
+        for n in range(states):
+            c = c_ref[pl.ds(t * states + n, groups, stride=0), :]
+            term = jnp.exp2(total * rate[n]) * start[n] * c
+            parts[n % 4] = term if parts[n % 4] is None else parts[n % 4] + term
+        y_t[at, :] = y_ref[at, :] + ((parts[0] + parts[1]) + (parts[2] + parts[3]))
+        return carry
+
+    lax.fori_loop(0, rows, step, 0, unroll=4)
 
     for g in range(groups):
         y = y_t[pl.ds(g, rows, stride=groups), :]
@@ -171,6 +199,21 @@
         scratch_shapes=[flat, flat, pltpu.VMEM((rows * states, LANES), jnp.float32), rates],
         name="end_state",
     )(delta, u_in, bc_proj, a_rate)
+    tokens = jax.ShapeDtypeStruct((rows * groups, LANES), jnp.float32)
+    spread = pltpu.VMEM((rows * states, LANES), jnp.float32)
+    local = pl.pallas_call(
+        local_kernel,
+        out_shape=(tokens, tokens, jax.ShapeDtypeStruct((rows * states, LANES), jnp.float32)),
+        in_specs=[whole()] * 4,
+        out_specs=(whole(),) * 3,
+        scratch_shapes=[flat, flat, spread, rates],
+        cost_estimate=pl.CostEstimate(
+            flops=6 * rows * channels * states,
+            bytes_accessed=4 * rows * (4 * channels + states * LANES),
+            transcendentals=rows * channels * states,
+        ),
+        name="local",
+    )(delta, u_in, bc_proj, a_rate)
     ends = lax.all_to_all(ends, "ctx", split_axis=0, concat_axis=0, tiled=True)
     entering = pl.pallas_call(
         carry_kernel,
@@ -184,20 +227,18 @@
     gated = pl.pallas_call(
         gated_kernel,
         out_shape=jax.ShapeDtypeStruct((rows, channels), jnp.bfloat16),
-        in_specs=[whole()] * 7,
-        out_specs=whole(),
-        scratch_shapes=[
-            flat, flat, pltpu.VMEM((rows * 2 * states, LANES), jnp.float32), flat, rates
-        ],
+        in_specs=[whole()] * 8,
+        out_specs=whole(),
+        scratch_shapes=[flat, rates],
         name="gated",
-    )(delta, u_in, z_in, bc_proj, a_rate, d_skip.reshape(1, channels), entering)
+    )(u_in, z_in, a_rate, d_skip.reshape(1, channels), entering, *local)
 
     ring = [(i, (i + 2 - 4 * (i % 2)) % count) for i in range(count)]
     trade = [(i, i ^ 1) for i in range(count)]
-    local = [gated, lax.ppermute(gated, "ctx", trade)]
+    chip_blocks = [gated, lax.ppermute(gated, "ctx", trade)]
     arrived = []
     for unit in range(count // 2 - 1):
-        source = (local + arrived)[unit]
+        source = (chip_blocks + arrived)[unit]
         arrived.append(lax.ppermute(source, "ctx", ring))
     traded = [lax.ppermute(value, "ctx", trade) for value in arrived]
     terms = pl.pallas_call(
@@ -206,7 +247,7 @@
         in_specs=[smem] + [whole()] * (count + 1),
         out_specs=whole(),
         name="project",
-    )(me, *local, *arrived, *traded, w_out)
+    )(me, *chip_blocks, *arrived, *traded, w_out)
 
     received = lax.all_to_all(
         terms.reshape(count, rows, width), "exp", split_axis=0, concat_axis=0

time: 120 us -> 118 us (0.983)
  blocking collectives: 45.7 us -> 34.3 us
  starting transfers between devices: 33.8 us -> 38.6 us
  Pallas kernels: 18.2 us -> 22.2 us
    all_to_all x1 -> x0, blocking collectives: 11.4 us -> none  [body(): lax.all_to_all(entering, 'ctx', split_axis=0, concat_axis=0, tiled=True)]
    pallas_call x0 -> x1, Pallas kernels: none -> 5.81 us  [body(): pl.pallas_call(local_kernel, out_shape=(tokens, tokens, jax.ShapeDtypeStr...]
    all_to_all x0 -> x1, starting transfers between devices: none -> 3.38 us  [body(): lax.all_to_all(entering, 'ctx', split_axis=0, concat_axis=0, tiled=True)]
    ppermute x7, starting transfers between devices: 9.49 us -> 12.8 us  [body(): arrived.append(lax.ppermute(source, 'ctx', ring))]
    pallas_call x1, Pallas kernels: 6.32 us -> 4.48 us  [body(): pl.pallas_call(gated_kernel, out_shape=jax.ShapeDtypeStruct((rows, channe...]
    all_to_all x0 -> x1, waiting for transfers between devices: none -> 1.48 us  [body(): lax.all_to_all(entering, 'ctx', split_axis=0, concat_axis=0, tiled=True)]
    ppermute x7, waiting for transfers between devices: 9.78 us -> 8.38 us  [body(): arrived.append(lax.ppermute(source, 'ctx', ring))]
    ppermute x7, starting transfers between devices: 13.6 us -> 12.4 us  [body(): traded = [lax.ppermute(value, 'ctx', trade) for value in arrived]]
  transfers between devices with their start and end apart: 16 -> 17, of which waited for: 5 -> 6; matrix products, arithmetic and copies ran while one was open for 0% -> 0% of each run, Pallas kernels for 0% -> 5%
where the time goes in v4:
time: 118 us
  starting transfers between devices  38.6 us (33%)
  blocking collectives  34.3 us (29%)
  Pallas kernels  22.2 us (19%)
  waiting for transfers between devices  19.5 us (17%)
  local copies, waits for them, and re-layouts  2.11 us (2%)
    all_to_all x1, blocking collectives, body(): lax.all_to_all(terms.reshape(count, rows, width), 'exp', split_axis=0, co...  34.3 us
    ppermute x7, starting transfers between devices, body(): arrived.append(lax.ppermute(source, 'ctx', ring))  12.8 us
    ppermute x7, starting transfers between devices, body(): traded = [lax.ppermute(value, 'ctx', trade) for value in arrived]  12.4 us
    all_to_all x1, starting transfers between devices, body(): ends = lax.all_to_all(ends, 'ctx', split_axis=0, concat_axis=0, tiled=True)  9.98 us
    all_to_all x1, waiting for transfers between devices, body(): ends = lax.all_to_all(ends, 'ctx', split_axis=0, concat_axis=0, tiled=True)  9.17 us
    ppermute x7, waiting for transfers between devices, body(): arrived.append(lax.ppermute(source, 'ctx', ring))  8.38 us
    pallas_call x1, Pallas kernels, body(): pl.pallas_call(functools.partial(project_kernel, count), out_shape=jax.Sh...  6.23 us
    pallas_call x1, Pallas kernels, body(): pl.pallas_call(local_kernel, out_shape=(tokens, tokens, jax.ShapeDtypeStr...  5.81 us
  transfers between devices with their start and end apart: 17, of which 6 were waited for; matrix products, arithmetic and copies ran while one was open for 0% of the time, Pallas kernels for 5%

profile of v4, /device:TPU:1, one launch (start us, length us, event | category | flops | bytes accessed | tf_op | source)
XLA Modules:
  0.0 117.8 jit_solution(15555933704715593609)
XLA Ops:
  0.0 4.1 %end_state.1 = f32[256,128]{1,0:T(8,128)} custom-call(f32[128,1024]{1,0:T(8,128)} %delta_ref.3, bf16[128,1024]{1,0:T(8,128)(2,1)} %u_ref.5, f32[32,128]{1,0:T(8,128)} %bc_ref.3, f32[16,1024]{1,0:T(8,128)} %a_ref.7), custom_call_target="tpu_custom_call" | custom-call | tf_op jit(solution)/shard_map/end_state/pallas_call | solution.py:194
  4.1 10.0 %all-to-all-start = ((f32[16,16,128]{2,1,0:T(8,128)}), f32[16,16,128]{2,1,0:T(8,128)S(1)}, u32[]{:S(2)}, u32[]{:S(2)}) async-start(f32[16,16,128]{2,1,0:T(8,128)} %bitcast.8), calls=%async_computation | async-start | bytes 262144 | tf_op jit(solution)/shard_map/all_to_all | solution.py:217
  14.1 9.2 %all-to-all-done = f32[16,16,128]{2,1,0:T(8,128)S(1)} async-done(((f32[16,16,128]{2,1,0:T(8,128)}), f32[16,16,128]{2,1,0:T(8,128)S(1)}, u32[]{:S(2)}, u32[]{:S(2)}) %all-to-all-start) | async-done | bytes 131104 | tf_op jit(solution)/shard_map/all_to_all | solution.py:217
  23.9 1.6 %carry.1 = f32[128,128]{1,0:T(8,128)} custom-call(s32[1]{0:T(128)} %bitcast.me_ref, f32[256,128]{1,0:T(8,128)} %bitcast.9, f32[16,1024]{1,0:T(8,128)} %a_ref.7), custom_call_target="tpu_custom_call" | custom-call | tf_op jit(solution)/shard_map/carry/pallas_call | solution.py:218
  25.5 3.4 %all-to-all-start.1 = ((f32[16,8,128]{2,1,0:T(8,128)}), f32[16,8,128]{2,1,0:T(8,128)S(1)}, u32[]{:S(2)}, u32[]{:S(2)}) async-start(f32[16,8,128]{2,1,0:T(8,128)} %bitcast.11), calls=%async_computation.1 | async-start | bytes 131072 | tf_op jit(solution)/shard_map/all_to_all | solution.py:226
  28.9 5.8 %local.1 = (f32[1024,128]{1,0:T(8,128)}, f32[1024,128]{1,0:T(8,128)}, f32[2048,128]{1,0:T(8,128)}) custom-call(f32[128,1024]{1,0:T(8,128)} %delta_ref.3, bf16[128,1024]{1,0:T(8,128)(2,1)} %u_ref.5, f32[32,128]{1,0:T(8,128)} %bc_ref.3, f32[16,1024]{1,0:T(8,128)} %a_ref.7), custom_call_target="tpu_custom_call" | custom-call | flops 12582912 | bytes 3145728 | tf_op jit(solution)/shard_map/local/pallas_call | solution.py:204
  34.7 1.5 %all-to-all-done.1 = f32[16,8,128]{2,1,0:T(8,128)S(1)} async-done(((f32[16,8,128]{2,1,0:T(8,128)}), f32[16,8,128]{2,1,0:T(8,128)S(1)}, u32[]{:S(2)}, u32[]{:S(2)}) %all-to-all-start.1) | async-done | bytes 65568 | tf_op jit(solution)/shard_map/all_to_all | solution.py:226
  36.8 4.5 %gated.1.refs_0_ = bf16[128,1024]{1,0:T(8,128)(2,1)} custom-call(bf16[128,1024]{1,0:T(8,128)(2,1)} %u_ref.5, bf16[128,1024]{1,0:T(8,128)(2,1)} %z_ref.1, f32[16,1024]{1,0:T(8,128)} %a_ref.7, f32[1,1024]{1,0:T(1,128)} %bitcast.12, f32[128,128]{1,0:T(8,128)} %bitcast.10, f32[1024,128]{1,0:T(8,128)} %get-tuple-element.8.y_ref, ...), custom_call_target="tpu_custom_call" | custom-call | tf_op jit(solution)/shard_map/gated/pallas_call | solution.py:227
  41.3 0.8 collective-permute-start.1
  42.1 4.9 %collective-permute-done.1.refs_2_ = bf16[128,1024]{1,0:T(8,128)(2,1)S(1)} collective-permute-done((bf16[128,1024]{1,0:T(8,128)(2,1)}, bf16[128,1024]{1,0:T(8,128)(2,1)S(1)}, u32[]{:S(2)}, u32[]{:S(2)}) %collective-permute-start.1) | collective-permute-done | bytes 262176 | tf_op jit(solution)/shard_map/ppermute | solution.py:242
  47.0 1.7 %collective-permute-start.3 = (bf16[128,1024]{1,0:T(8,128)(2,1)S(1)}, bf16[128,1024]{1,0:T(8,128)(2,1)S(1)}, u32[]{:S(2)}, u32[]{:S(2)}) collective-permute-start(bf16[128,1024]{1,0:T(8,128)(2,1)S(1)} %collective-permute-done.1.refs_2_), channel_id=1, source_target_pairs={{0,32},{16,240},{32,64},{48,16},{64,96},{80,48},{96,128},{112,80},... | collective-permute-start | bytes 786440 | tf_op jit(solution)/shard_map/ppermute | solution.py:242
  49.0 3.3 %collective-permute-done.3.refs_4_ = bf16[128,1024]{1,0:T(8,128)(2,1)S(1)} collective-permute-done((bf16[128,1024]{1,0:T(8,128)(2,1)S(1)}, bf16[128,1024]{1,0:T(8,128)(2,1)S(1)}, u32[]{:S(2)}, u32[]{:S(2)}) %collective-permute-start.3) | collective-permute-done | bytes 262176 | tf_op jit(solution)/shard_map/ppermute | solution.py:242
  52.3 2.9 %collective-permute-start.5 = (bf16[128,1024]{1,0:T(8,128)(2,1)S(1)}, bf16[128,1024]{1,0:T(8,128)(2,1)S(1)}, u32[]{:S(2)}, u32[]{:S(2)}) collective-permute-start(bf16[128,1024]{1,0:T(8,128)(2,1)S(1)} %collective-permute-done.3.refs_4_), channel_id=1, source_target_pairs={{0,32},{16,240},{32,64},{48,16},{64,96},{80,48},{96,128},{112,80},... | collective-permute-start | bytes 786440 | tf_op jit(solution)/shard_map/ppermute | solution.py:242
  55.4 2.6 %collective-permute-start.4 = (bf16[128,1024]{1,0:T(8,128)(2,1)S(1)}, bf16[128,1024]{1,0:T(8,128)(2,1)S(1)}, u32[]{:S(2)}, u32[]{:S(2)}) collective-permute-start(bf16[128,1024]{1,0:T(8,128)(2,1)S(1)} %collective-permute-done.2.refs_3_), channel_id=1, source_target_pairs={{0,32},{16,240},{32,64},{48,16},{64,96},{80,48},{96,128},{112,80},... | collective-permute-start | bytes 786440 | tf_op jit(solution)/shard_map/ppermute | solution.py:242
  58.0 1.8 %collective-permute-start.8 = (bf16[128,1024]{1,0:T(8,128)(2,1)S(1)}, bf16[128,1024]{1,0:T(8,128)(2,1)S(1)}, u32[]{:S(2)}, u32[]{:S(2)}) collective-permute-start(bf16[128,1024]{1,0:T(8,128)(2,1)S(1)} %collective-permute-done.1.refs_2_), channel_id=1, source_target_pairs={{0,16},{16,0},{32,48},{48,32},{64,80},{80,64},{96,112},{112,96},{1... | collective-permute-start | bytes 786440 | tf_op jit(solution)/shard_map/ppermute | solution.py:243
  59.9 2.9 %collective-permute-start.7 = (bf16[128,1024]{1,0:T(8,128)(2,1)S(1)}, bf16[128,1024]{1,0:T(8,128)(2,1)S(1)}, u32[]{:S(2)}, u32[]{:S(2)}) collective-permute-start(bf16[128,1024]{1,0:T(8,128)(2,1)S(1)} %collective-permute-done.5.refs_6_), channel_id=1, source_target_pairs={{0,32},{16,240},{32,64},{48,16},{64,96},{80,48},{96,128},{112,80},... | collective-permute-start | bytes 786440 | tf_op jit(solution)/shard_map/ppermute | solution.py:242
  62.8 1.6 %collective-permute-start.6 = (bf16[128,1024]{1,0:T(8,128)(2,1)S(1)}, bf16[128,1024]{1,0:T(8,128)(2,1)S(1)}, u32[]{:S(2)}, u32[]{:S(2)}) collective-permute-start(bf16[128,1024]{1,0:T(8,128)(2,1)S(1)} %collective-permute-done.4.refs_5_), channel_id=1, source_target_pairs={{0,32},{16,240},{32,64},{48,16},{64,96},{80,48},{96,128},{112,80},... | collective-permute-start | bytes 786440 | tf_op jit(solution)/shard_map/ppermute | solution.py:242
  64.4 2.9 %collective-permute-start.9 = (bf16[128,1024]{1,0:T(8,128)(2,1)S(1)}, bf16[128,1024]{1,0:T(8,128)(2,1)S(1)}, u32[]{:S(2)}, u32[]{:S(2)}) collective-permute-start(bf16[128,1024]{1,0:T(8,128)(2,1)S(1)} %collective-permute-done.2.refs_3_), channel_id=1, source_target_pairs={{0,16},{16,0},{32,48},{48,32},{64,80},{80,64},{96,112},{112,96},{1... | collective-permute-start | bytes 786440 | tf_op jit(solution)/shard_map/ppermute | solution.py:243
  67.9 4.2 %collective-permute-start.14 = (bf16[128,1024]{1,0:T(8,128)(2,1)S(1)}, bf16[128,1024]{1,0:T(8,128)(2,1)S(1)}, u32[]{:S(2)}, u32[]{:S(2)}) collective-permute-start(bf16[128,1024]{1,0:T(8,128)(2,1)S(1)} %collective-permute-done.7.refs_8_), channel_id=1, source_target_pairs={{0,16},{16,0},{32,48},{48,32},{64,80},{80,64},{96,112},{112,96},{1... | collective-permute-start | bytes 786440 | tf_op jit(solution)/shard_map/ppermute | solution.py:243
  72.1 2.8 %collective-permute-start.13 = (bf16[128,1024]{1,0:T(8,128)(2,1)S(1)}, bf16[128,1024]{1,0:T(8,128)(2,1)}, u32[]{:S(2)}, u32[]{:S(2)}) collective-permute-start(bf16[128,1024]{1,0:T(8,128)(2,1)S(1)} %collective-permute-done.6.refs_7_), channel_id=1, source_target_pairs={{0,16},{16,0},{32,48},{48,32},{64,80},{80,64},{96,112},{112,96},{1... | collective-permute-start | bytes 786440 | tf_op jit(solution)/shard_map/ppermute | solution.py:243
  75.0 0.8 copy-done.15
  76.3 6.2 %project.1 = bf16[2048,512]{1,0:T(8,128)(2,1)} custom-call(s32[1]{0:T(128)} %bitcast.me_ref, bf16[128,1024]{1,0:T(8,128)(2,1)} %gated.1.refs_0_, bf16[128,1024]{1,0:T(8,128)(2,1)} %copy-done.3, bf16[128,1024]{1,0:T(8,128)(2,1)} %copy-done.2, bf16[128,1024]{1,0:T(8,128)(2,1)} %copy-done.5, bf16[128,1024]{1,0:T(8,128)(2,1)} %copy-done.4, ...), custom_call_target="tpu_custom_call" | custom-call | tf_op jit(solution)/shard_map/project/pallas_call | solution.py:244
  82.5 34.3 %all_to_all.27 = bf16[16,128,512]{2,1,0:T(8,128)(2,1)S(1)} all-to-all(bf16[16,128,512]{2,1,0:T(8,128)(2,1)} %bitcast.7), channel_id=1, replica_groups=mesh['ctx'=16,'exp'=16] {'exp'}, dimensions={0} | all-to-all | bytes 4194304 | tf_op jit(solution)/shard_map/all_to_all | solution.py:252
  116.9 1.0 reduce_sum.12
  (49 shorter events, 2.9 us)
Async XLA Ops:
  4.1 19.1 %all-to-all-start = ((f32[16,16,128]{2,1,0:T(8,128)}), f32[16,16,128]{2,1,0:T(8,128)S(1)}, u32[]{:S(2)}, u32[]{:S(2)}) async-start(f32[16,16,128]{2,1,0:T(8,128)} %bitcast.8), calls=%async_computation | async-start | bytes 262144 | tf_op jit(solution)/shard_map/all_to_all | solution.py:217
  25.5 10.7 %all-to-all-start.1 = ((f32[16,8,128]{2,1,0:T(8,128)}), f32[16,8,128]{2,1,0:T(8,128)S(1)}, u32[]{:S(2)}, u32[]{:S(2)}) async-start(f32[16,8,128]{2,1,0:T(8,128)} %bitcast.11), calls=%async_computation.1 | async-start | bytes 131072 | tf_op jit(solution)/shard_map/all_to_all | solution.py:226
  41.3 5.7 %collective-permute-start.1 = (bf16[128,1024]{1,0:T(8,128)(2,1)}, bf16[128,1024]{1,0:T(8,128)(2,1)S(1)}, u32[]{:S(2)}, u32[]{:S(2)}) collective-permute-start(bf16[128,1024]{1,0:T(8,128)(2,1)} %gated.1.refs_0_), channel_id=1, source_target_pairs={{0,32},{16,240},{32,64},{48,16},{64,96},{80,48},{96,128},{112,80},... | collective-permute-start | bytes 786440 | tf_op jit(solution)/shard_map/ppermute | solution.py:242
  42.1 6.6 %collective-permute-start = (bf16[128,1024]{1,0:T(8,128)(2,1)}, bf16[128,1024]{1,0:T(8,128)(2,1)S(1)}, u32[]{:S(2)}, u32[]{:S(2)}) collective-permute-start(bf16[128,1024]{1,0:T(8,128)(2,1)} %gated.1.refs_0_), channel_id=1, source_target_pairs={{0,16},{16,0},{32,48},{48,32},{64,80},{80,64},{96,112},{112,96},{1... | collective-permute-start | bytes 786440 | tf_op jit(solution)/shard_map/ppermute | solution.py:238
  47.0 29.2 %copy-start.2 = (bf16[128,1024]{1,0:T(8,128)(2,1)}, bf16[128,1024]{1,0:T(8,128)(2,1)S(1)}, u32[]{:S(2)}) copy-start(bf16[128,1024]{1,0:T(8,128)(2,1)S(1)} %collective-permute-done.1.refs_2_) | copy-start | bytes 786436
  47.0 5.2 %collective-permute-start.3 = (bf16[128,1024]{1,0:T(8,128)(2,1)S(1)}, bf16[128,1024]{1,0:T(8,128)(2,1)S(1)}, u32[]{:S(2)}, u32[]{:S(2)}) collective-permute-start(bf16[128,1024]{1,0:T(8,128)(2,1)S(1)} %collective-permute-done.1.refs_2_), channel_id=1, source_target_pairs={{0,32},{16,240},{32,64},{48,16},{64,96},{80,48},{96,128},{112,80},... | collective-permute-start | bytes 786440 | tf_op jit(solution)/shard_map/ppermute | solution.py:242
  48.7 27.5 %copy-start.3 = (bf16[128,1024]{1,0:T(8,128)(2,1)}, bf16[128,1024]{1,0:T(8,128)(2,1)S(1)}, u32[]{:S(2)}) copy-start(bf16[128,1024]{1,0:T(8,128)(2,1)S(1)} %collective-permute-done.refs_1_) | copy-start | bytes 786436
  48.7 6.6 %collective-permute-start.2 = (bf16[128,1024]{1,0:T(8,128)(2,1)S(1)}, bf16[128,1024]{1,0:T(8,128)(2,1)S(1)}, u32[]{:S(2)}, u32[]{:S(2)}) collective-permute-start(bf16[128,1024]{1,0:T(8,128)(2,1)S(1)} %collective-permute-done.refs_1_), channel_id=1, source_target_pairs={{0,32},{16,240},{32,64},{48,16},{64,96},{80,48},{96,128},{112,80},... | collective-permute-start | bytes 786440 | tf_op jit(solution)/shard_map/ppermute | solution.py:242
  52.3 24.0 %copy-start.4 = (bf16[128,1024]{1,0:T(8,128)(2,1)}, bf16[128,1024]{1,0:T(8,128)(2,1)S(1)}, u32[]{:S(2)}) copy-start(bf16[128,1024]{1,0:T(8,128)(2,1)S(1)} %collective-permute-done.3.refs_4_) | copy-start | bytes 786436
  52.3 7.6 %collective-permute-start.5 = (bf16[128,1024]{1,0:T(8,128)(2,1)S(1)}, bf16[128,1024]{1,0:T(8,128)(2,1)S(1)}, u32[]{:S(2)}, u32[]{:S(2)}) collective-permute-start(bf16[128,1024]{1,0:T(8,128)(2,1)S(1)} %collective-permute-done.3.refs_4_), channel_id=1, source_target_pairs={{0,32},{16,240},{32,64},{48,16},{64,96},{80,48},{96,128},{112,80},... | collective-permute-start | bytes 786440 | tf_op jit(solution)/shard_map/ppermute | solution.py:242
  55.4 20.9 %copy-start.5 = (bf16[128,1024]{1,0:T(8,128)(2,1)}, bf16[128,1024]{1,0:T(8,128)(2,1)S(1)}, u32[]{:S(2)}) copy-start(bf16[128,1024]{1,0:T(8,128)(2,1)S(1)} %collective-permute-done.2.refs_3_) | copy-start | bytes 786436
  55.4 7.4 %collective-permute-start.4 = (bf16[128,1024]{1,0:T(8,128)(2,1)S(1)}, bf16[128,1024]{1,0:T(8,128)(2,1)S(1)}, u32[]{:S(2)}, u32[]{:S(2)}) collective-permute-start(bf16[128,1024]{1,0:T(8,128)(2,1)S(1)} %collective-permute-done.2.refs_3_), channel_id=1, source_target_pairs={{0,32},{16,240},{32,64},{48,16},{64,96},{80,48},{96,128},{112,80},... | collective-permute-start | bytes 786440 | tf_op jit(solution)/shard_map/ppermute | solution.py:242
  58.0 9.4 %collective-permute-start.8 = (bf16[128,1024]{1,0:T(8,128)(2,1)S(1)}, bf16[128,1024]{1,0:T(8,128)(2,1)S(1)}, u32[]{:S(2)}, u32[]{:S(2)}) collective-permute-start(bf16[128,1024]{1,0:T(8,128)(2,1)S(1)} %collective-permute-done.1.refs_2_), channel_id=1, source_target_pairs={{0,16},{16,0},{32,48},{48,32},{64,80},{80,64},{96,112},{112,96},{1... | collective-permute-start | bytes 786440 | tf_op jit(solution)/shard_map/ppermute | solution.py:243
  59.8 7.7 %collective-permute-start.10 = (bf16[128,1024]{1,0:T(8,128)(2,1)S(1)}, bf16[128,1024]{1,0:T(8,128)(2,1)S(1)}, u32[]{:S(2)}, u32[]{:S(2)}) collective-permute-start(bf16[128,1024]{1,0:T(8,128)(2,1)S(1)} %collective-permute-done.3.refs_4_), channel_id=1, source_target_pairs={{0,16},{16,0},{32,48},{48,32},{64,80},{80,64},{96,112},{112,96},{1... | collective-permute-start | bytes 786440 | tf_op jit(solution)/shard_map/ppermute | solution.py:243
  59.9 16.4 %copy-start.6 = (bf16[128,1024]{1,0:T(8,128)(2,1)}, bf16[128,1024]{1,0:T(8,128)(2,1)S(1)}, u32[]{:S(2)}) copy-start(bf16[128,1024]{1,0:T(8,128)(2,1)S(1)} %collective-permute-done.5.refs_6_) | copy-start | bytes 786436
  59.9 8.0 %collective-permute-start.7 = (bf16[128,1024]{1,0:T(8,128)(2,1)S(1)}, bf16[128,1024]{1,0:T(8,128)(2,1)S(1)}, u32[]{:S(2)}, u32[]{:S(2)}) collective-permute-start(bf16[128,1024]{1,0:T(8,128)(2,1)S(1)} %collective-permute-done.5.refs_6_), channel_id=1, source_target_pairs={{0,32},{16,240},{32,64},{48,16},{64,96},{80,48},{96,128},{112,80},... | collective-permute-start | bytes 786440 | tf_op jit(solution)/shard_map/ppermute | solution.py:242
  62.8 13.4 %copy-start.7 = (bf16[128,1024]{1,0:T(8,128)(2,1)}, bf16[128,1024]{1,0:T(8,128)(2,1)S(1)}, u32[]{:S(2)}) copy-start(bf16[128,1024]{1,0:T(8,128)(2,1)S(1)} %collective-permute-done.4.refs_5_) | copy-start | bytes 786436
  62.8 9.3 %collective-permute-start.6 = (bf16[128,1024]{1,0:T(8,128)(2,1)S(1)}, bf16[128,1024]{1,0:T(8,128)(2,1)S(1)}, u32[]{:S(2)}, u32[]{:S(2)}) collective-permute-start(bf16[128,1024]{1,0:T(8,128)(2,1)S(1)} %collective-permute-done.4.refs_5_), channel_id=1, source_target_pairs={{0,32},{16,240},{32,64},{48,16},{64,96},{80,48},{96,128},{112,80},... | collective-permute-start | bytes 786440 | tf_op jit(solution)/shard_map/ppermute | solution.py:242
  64.4 10.5 %collective-permute-start.9 = (bf16[128,1024]{1,0:T(8,128)(2,1)S(1)}, bf16[128,1024]{1,0:T(8,128)(2,1)S(1)}, u32[]{:S(2)}, u32[]{:S(2)}) collective-permute-start(bf16[128,1024]{1,0:T(8,128)(2,1)S(1)} %collective-permute-done.2.refs_3_), channel_id=1, source_target_pairs={{0,16},{16,0},{32,48},{48,32},{64,80},{80,64},{96,112},{112,96},{1... | collective-permute-start | bytes 786440 | tf_op jit(solution)/shard_map/ppermute | solution.py:243
  67.3 8.9 %copy-start.8 = (bf16[128,1024]{1,0:T(8,128)(2,1)}, bf16[128,1024]{1,0:T(8,128)(2,1)S(1)}, u32[]{:S(2)}) copy-start(bf16[128,1024]{1,0:T(8,128)(2,1)S(1)} %collective-permute-done.8.refs_9_) | copy-start | bytes 786436
  67.3 7.6 %collective-permute-start.12 = (bf16[128,1024]{1,0:T(8,128)(2,1)S(1)}, bf16[128,1024]{1,0:T(8,128)(2,1)S(1)}, u32[]{:S(2)}, u32[]{:S(2)}) collective-permute-start(bf16[128,1024]{1,0:T(8,128)(2,1)S(1)} %collective-permute-done.5.refs_6_), channel_id=1, source_target_pairs={{0,16},{16,0},{32,48},{48,32},{64,80},{80,64},{96,112},{112,96},{1... | collective-permute-start | bytes 786440 | tf_op jit(solution)/shard_map/ppermute | solution.py:243
  67.5 7.5 %collective-permute-start.11 = (bf16[128,1024]{1,0:T(8,128)(2,1)S(1)}, bf16[128,1024]{1,0:T(8,128)(2,1)S(1)}, u32[]{:S(2)}, u32[]{:S(2)}) collective-permute-start(bf16[128,1024]{1,0:T(8,128)(2,1)S(1)} %collective-permute-done.4.refs_5_), channel_id=1, source_target_pairs={{0,16},{16,0},{32,48},{48,32},{64,80},{80,64},{96,112},{112,96},{1... | collective-permute-start | bytes 786440 | tf_op jit(solution)/shard_map/ppermute | solution.py:243
  67.9 7.1 %collective-permute-start.14 = (bf16[128,1024]{1,0:T(8,128)(2,1)S(1)}, bf16[128,1024]{1,0:T(8,128)(2,1)S(1)}, u32[]{:S(2)}, u32[]{:S(2)}) collective-permute-start(bf16[128,1024]{1,0:T(8,128)(2,1)S(1)} %collective-permute-done.7.refs_8_), channel_id=1, source_target_pairs={{0,16},{16,0},{32,48},{48,32},{64,80},{80,64},{96,112},{112,96},{1... | collective-permute-start | bytes 786440 | tf_op jit(solution)/shard_map/ppermute | solution.py:243
  72.1 4.1 %collective-permute-start.13 = (bf16[128,1024]{1,0:T(8,128)(2,1)S(1)}, bf16[128,1024]{1,0:T(8,128)(2,1)}, u32[]{:S(2)}, u32[]{:S(2)}) collective-permute-start(bf16[128,1024]{1,0:T(8,128)(2,1)S(1)} %collective-permute-done.6.refs_7_), channel_id=1, source_target_pairs={{0,16},{16,0},{32,48},{48,32},{64,80},{80,64},{96,112},{112,96},{1... | collective-permute-start | bytes 786440 | tf_op jit(solution)/shard_map/ppermute | solution.py:243
  (9 other events, 27.5 us)

commit v5 on v4

--- a/solution.py
+++ b/solution.py
@@ -155,25 +155,31 @@
         out_ref[:, lanes(g)] = (mixed * (z / (1.0 + jnp.exp(-z)))).astype(jnp.bfloat16)
 
 
-def project_kernel(count, me_ref, *refs):
-    blocks, w_ref, out_ref = refs[:count], refs[count], refs[count + 1]
+def project_kernel(places, me_ref, w_ref, *refs):
+    units = len(places)
+    blocks, out_ref, joined, result, sems = refs[:units], *refs[-4:]
     rows = blocks[0].shape[0]
+    count = out_ref.shape[0] // rows
     me = me_ref[0]
     core = lax.rem(me, 2)
-    chip = me - core
     way = 2 - 4 * core
-    units = (count - 2) // 2
-    homes = [chip + core, chip + 1 - core]
-    for side in (-1, 1):
-        for unit in range(units):
-            same = (unit % 2 == 0) == (side == -1)
-            parity = core if same else 1 - core
-            homes.append(chip + side * way * (unit // 2 + 1) + parity)
-    for block, home in zip(blocks, homes):
+    for i, block in enumerate(blocks):
+        joined[i * rows : (i + 1) * rows, :] = block[...]
+    result[...] = jnp.dot(
+        joined[...], w_ref[...], preferred_element_type=jnp.float32
+    ).astype(jnp.bfloat16)
+    copies = []
+    for i, (step, same) in enumerate(places):
+        home = me - core + step * way + (core if same else 1 - core)
         at = pl.multiple_of(lax.rem(home + 2 * count, count) * rows, rows)
-        out_ref[pl.ds(at, rows), :] = jnp.dot(
-            block[...], w_ref[...], preferred_element_type=jnp.float32
-        ).astype(jnp.bfloat16)
+        copies.append(
+            pltpu.make_async_copy(
+                result.at[pl.ds(i * rows, rows), :], out_ref.at[pl.ds(at, rows), :], sems.at[i]
+            )
+        )
+        copies[-1].start()
+    for copy in copies:
+        copy.wait()
 
 
 def whole():
@@ -235,19 +241,52 @@
 
     ring = [(i, (i + 2 - 4 * (i % 2)) % count) for i in range(count)]
     trade = [(i, i ^ 1) for i in range(count)]
-    chip_blocks = [gated, lax.ppermute(gated, "ctx", trade)]
-    arrived = []
+    swapped = lax.ppermute(gated, "ctx", trade)
+    gated, swapped = lax.optimization_barrier((gated, swapped))
+    sources = [gated, swapped]
     for unit in range(count // 2 - 1):
-        source = (chip_blocks + arrived)[unit]
-        arrived.append(lax.ppermute(source, "ctx", ring))
-    traded = [lax.ppermute(value, "ctx", trade) for value in arrived]
-    terms = pl.pallas_call(
-        functools.partial(project_kernel, count),
-        out_shape=jax.ShapeDtypeStruct((rows * count, width), jnp.bfloat16),
-        in_specs=[smem] + [whole()] * (count + 1),
-        out_specs=whole(),
-        name="project",
-    )(me, *chip_blocks, *arrived, *traded, w_out)
+        sources.append(lax.ppermute(sources[unit], "ctx", ring))
+    arrived = sources[2:]
+    early = len(arrived) - 3
+
+    def place_of(unit, side):
+        return side * (unit // 2 + 1), (unit % 2 == 0) == (side == -1)
+
+    def project(blocks, places, done):
+        tall = len(places) * rows
+        return pl.pallas_call(
+            functools.partial(project_kernel, tuple(places)),
+            out_shape=jax.ShapeDtypeStruct((rows * count, width), jnp.bfloat16),
+            in_specs=[smem]
+            + [whole()] * (len(places) + 1)
+            + [pl.BlockSpec(memory_space=pl.ANY)] * len(done),
+            out_specs=pl.BlockSpec(memory_space=pl.ANY),
+            scratch_shapes=[
+                pltpu.VMEM((tall, channels), jnp.bfloat16),
+                pltpu.VMEM((tall, width), jnp.bfloat16),
+                pltpu.SemaphoreType.DMA((len(places),)),
+            ],
+            input_output_aliases={len(places) + 2: 0} if done else {},
+            cost_estimate=pl.CostEstimate(
+                flops=2 * tall * channels * width,
+                bytes_accessed=2 * tall * (channels + width),
+                transcendentals=0,
+            ),
+            name="project",
+        )(me, w_out, *blocks, *done)
+
+    blocks, places = [gated, swapped], [(0, True), (0, False)]
+    for unit in range(early):
+        blocks += [arrived[unit], lax.ppermute(arrived[unit], "ctx", trade)]
+        places += [place_of(unit, -1), place_of(unit, 1)]
+    terms = project(blocks, places, [])
+    last, terms = lax.optimization_barrier((arrived[-1], terms))
+    blocks, places = [], []
+    for unit in range(early, len(arrived)):
+        value = last if unit == len(arrived) - 1 else arrived[unit]
+        blocks += [value, lax.ppermute(value, "ctx", trade)]
+        places += [place_of(unit, -1), place_of(unit, 1)]
+    terms = project(blocks, places, [terms])
 
     received = lax.all_to_all(
         terms.reshape(count, rows, width), "exp", split_axis=0, concat_axis=0

time: 118 us -> 116 us (0.983)
  starting transfers between devices: 38.6 us -> 34.7 us
  Pallas kernels: 22.2 us -> 24.3 us
    ppermute x15, starting transfers between devices: 25.2 us -> 21.3 us  [the longest x7 13.5 us: body(): sources.append(lax.ppermute(sources[unit], 'ctx', ring))]
    pallas_call x1 -> x2, Pallas kernels: 6.23 us -> 8.28 us  [project(): pl.pallas_call(functools.partial(project_kernel, tuple(places)), out_shap...]
  transfers between devices with their start and end apart: 17 -> 17, of which waited for: 6 -> 7; matrix products, arithmetic and copies ran while one was open for 0% -> 0% of each run, Pallas kernels for 5% -> 9%
where the time goes in v5:
time: 116 us
  starting transfers between devices  34.7 us (30%)
  blocking collectives  34.5 us (30%)
  Pallas kernels  24.3 us (21%)
  waiting for transfers between devices  18.7 us (16%)
  local copies, waits for them, and re-layouts  2.67 us (2%)
    all_to_all x1, blocking collectives, body(): lax.all_to_all(terms.reshape(count, rows, width), 'exp', split_axis=0, co...  34.5 us
    ppermute x7, starting transfers between devices, body(): sources.append(lax.ppermute(sources[unit], 'ctx', ring))  13.5 us
    all_to_all x1, starting transfers between devices, body(): ends = lax.all_to_all(ends, 'ctx', split_axis=0, concat_axis=0, tiled=True)  9.98 us
    all_to_all x1, waiting for transfers between devices, body(): ends = lax.all_to_all(ends, 'ctx', split_axis=0, concat_axis=0, tiled=True)  9.17 us
    pallas_call x2, Pallas kernels, project(): pl.pallas_call(functools.partial(project_kernel, tuple(places)), out_shap...  8.28 us
    pallas_call x1, Pallas kernels, body(): pl.pallas_call(local_kernel, out_shape=(tokens, tokens, jax.ShapeDtypeStr...  5.81 us
    ppermute x7, waiting for transfers between devices, body(): sources.append(lax.ppermute(sources[unit], 'ctx', ring))  5.1 us
    ppermute x3, starting transfers between devices, body(): blocks += [value, lax.ppermute(value, 'ctx', trade)]  4.66 us
  transfers between devices with their start and end apart: 17, of which 7 were waited for; matrix products, arithmetic and copies ran while one was open for 0% of the time, Pallas kernels for 9%

profile of v5, /device:TPU:1, one launch (start us, length us, event | category | flops | bytes accessed | tf_op | source)
XLA Modules:
  0.0 116.0 jit_solution(1276230476632502416)
XLA Ops:
  0.0 4.1 %end_state.1 = f32[256,128]{1,0:T(8,128)} custom-call(f32[128,1024]{1,0:T(8,128)} %delta_ref.3, bf16[128,1024]{1,0:T(8,128)(2,1)} %u_ref.5, f32[32,128]{1,0:T(8,128)} %bc_ref.3, f32[16,1024]{1,0:T(8,128)} %a_ref.7), custom_call_target="tpu_custom_call" | custom-call | tf_op jit(solution)/shard_map/end_state/pallas_call | solution.py:200
  4.1 10.0 %all-to-all-start = ((f32[16,16,128]{2,1,0:T(8,128)}), f32[16,16,128]{2,1,0:T(8,128)S(1)}, u32[]{:S(2)}, u32[]{:S(2)}) async-start(f32[16,16,128]{2,1,0:T(8,128)} %bitcast.8), calls=%async_computation | async-start | bytes 262144 | tf_op jit(solution)/shard_map/all_to_all | solution.py:223
  14.1 9.2 %all-to-all-done = f32[16,16,128]{2,1,0:T(8,128)S(1)} async-done(((f32[16,16,128]{2,1,0:T(8,128)}), f32[16,16,128]{2,1,0:T(8,128)S(1)}, u32[]{:S(2)}, u32[]{:S(2)}) %all-to-all-start) | async-done | bytes 131104 | tf_op jit(solution)/shard_map/all_to_all | solution.py:223
  23.9 1.6 %carry.1 = f32[128,128]{1,0:T(8,128)} custom-call(s32[1]{0:T(128)} %bitcast.me_ref, f32[256,128]{1,0:T(8,128)} %bitcast.9, f32[16,1024]{1,0:T(8,128)} %a_ref.7), custom_call_target="tpu_custom_call" | custom-call | tf_op jit(solution)/shard_map/carry/pallas_call | solution.py:224
  25.5 3.4 %all-to-all-start.1 = ((f32[16,8,128]{2,1,0:T(8,128)}), f32[16,8,128]{2,1,0:T(8,128)S(1)}, u32[]{:S(2)}, u32[]{:S(2)}) async-start(f32[16,8,128]{2,1,0:T(8,128)} %bitcast.11), calls=%async_computation.1 | async-start | bytes 131072 | tf_op jit(solution)/shard_map/all_to_all | solution.py:232
  28.9 5.8 %local.1 = (f32[1024,128]{1,0:T(8,128)}, f32[1024,128]{1,0:T(8,128)}, f32[2048,128]{1,0:T(8,128)}) custom-call(f32[128,1024]{1,0:T(8,128)} %delta_ref.3, bf16[128,1024]{1,0:T(8,128)(2,1)} %u_ref.5, f32[32,128]{1,0:T(8,128)} %bc_ref.3, f32[16,1024]{1,0:T(8,128)} %a_ref.7), custom_call_target="tpu_custom_call" | custom-call | flops 12582912 | bytes 3145728 | tf_op jit(solution)/shard_map/local/pallas_call | solution.py:210
  34.7 1.5 %all-to-all-done.1 = f32[16,8,128]{2,1,0:T(8,128)S(1)} async-done(((f32[16,8,128]{2,1,0:T(8,128)}), f32[16,8,128]{2,1,0:T(8,128)S(1)}, u32[]{:S(2)}, u32[]{:S(2)}) %all-to-all-start.1) | async-done | bytes 65568 | tf_op jit(solution)/shard_map/all_to_all | solution.py:232
  36.8 4.5 %gated.1.refs_0_ = bf16[128,1024]{1,0:T(8,128)(2,1)} custom-call(bf16[128,1024]{1,0:T(8,128)(2,1)} %u_ref.5, bf16[128,1024]{1,0:T(8,128)(2,1)} %z_ref.1, f32[16,1024]{1,0:T(8,128)} %a_ref.7, f32[1,1024]{1,0:T(1,128)} %bitcast.12, f32[128,128]{1,0:T(8,128)} %bitcast.10, f32[1024,128]{1,0:T(8,128)} %get-tuple-element.12.y_ref, ...), custom_call_target="tpu_custom_call" | custom-call | tf_op jit(solution)/shard_map/gated/pallas_call | solution.py:233
  41.5 1.5 %collective-permute-done.refs_1_ = bf16[128,1024]{1,0:T(8,128)(2,1)S(1)} collective-permute-done((bf16[128,1024]{1,0:T(8,128)(2,1)}, bf16[128,1024]{1,0:T(8,128)(2,1)S(1)}, u32[]{:S(2)}, u32[]{:S(2)}) %collective-permute-start) | collective-permute-done | bytes 262176 | tf_op jit(solution)/shard_map/ppermute | solution.py:244
  43.8 1.2 %collective-permute-start.5 = (bf16[128,1024]{1,0:T(8,128)(2,1)S(1)}, bf16[128,1024]{1,0:T(8,128)(2,1)S(1)}, u32[]{:S(2)}, u32[]{:S(2)}) collective-permute-start(bf16[128,1024]{1,0:T(8,128)(2,1)S(1)} %collective-permute-done.refs_1_), channel_id=1, source_target_pairs={{0,32},{16,240},{32,64},{48,16},{64,96},{80,48},{96,128},{112,80},... | collective-permute-start | bytes 786440 | tf_op jit(solution)/shard_map/ppermute | solution.py:248
  45.0 3.8 %collective-permute-done.1.refs_2_ = bf16[128,1024]{1,0:T(8,128)(2,1)S(1)} collective-permute-done((bf16[128,1024]{1,0:T(8,128)(2,1)}, bf16[128,1024]{1,0:T(8,128)(2,1)S(1)}, u32[]{:S(2)}, u32[]{:S(2)}) %collective-permute-start.1) | collective-permute-done | bytes 262176 | tf_op jit(solution)/shard_map/ppermute | solution.py:248
  48.8 1.7 %collective-permute-start.2 = (bf16[128,1024]{1,0:T(8,128)(2,1)S(1)}, bf16[128,1024]{1,0:T(8,128)(2,1)S(1)}, u32[]{:S(2)}, u32[]{:S(2)}) collective-permute-start(bf16[128,1024]{1,0:T(8,128)(2,1)S(1)} %collective-permute-done.1.refs_2_), channel_id=1, source_target_pairs={{0,32},{16,240},{32,64},{48,16},{64,96},{80,48},{96,128},{112,80},... | collective-permute-start | bytes 786440 | tf_op jit(solution)/shard_map/ppermute | solution.py:248
  50.5 1.1 collective-permute-done.5.refs_4_
  51.6 1.7 %collective-permute-start.6 = (bf16[128,1024]{1,0:T(8,128)(2,1)S(1)}, bf16[128,1024]{1,0:T(8,128)(2,1)S(1)}, u32[]{:S(2)}, u32[]{:S(2)}) collective-permute-start(bf16[128,1024]{1,0:T(8,128)(2,1)S(1)} %collective-permute-done.5.refs_4_), channel_id=1, source_target_pairs={{0,32},{16,240},{32,64},{48,16},{64,96},{80,48},{96,128},{112,80},... | collective-permute-start | bytes 786440 | tf_op jit(solution)/shard_map/ppermute | solution.py:248
  54.1 2.8 %collective-permute-start.3 = (bf16[128,1024]{1,0:T(8,128)(2,1)S(1)}, bf16[128,1024]{1,0:T(8,128)(2,1)S(1)}, u32[]{:S(2)}, u32[]{:S(2)}) collective-permute-start(bf16[128,1024]{1,0:T(8,128)(2,1)S(1)} %collective-permute-done.2.refs_6_), channel_id=1, source_target_pairs={{0,32},{16,240},{32,64},{48,16},{64,96},{80,48},{96,128},{112,80},... | collective-permute-start | bytes 786440 | tf_op jit(solution)/shard_map/ppermute | solution.py:248
  56.9 1.8 %collective-permute-start.11 = (bf16[128,1024]{1,0:T(8,128)(2,1)S(1)}, bf16[128,1024]{1,0:T(8,128)(2,1)S(1)}, u32[]{:S(2)}, u32[]{:S(2)}) collective-permute-start(bf16[128,1024]{1,0:T(8,128)(2,1)S(1)} %collective-permute-done.5.refs_4_), channel_id=1, source_target_pairs={{0,16},{16,0},{32,48},{48,32},{64,80},{80,64},{96,112},{112,96},{1... | collective-permute-start | bytes 786440 | tf_op jit(solution)/shard_map/ppermute | solution.py:280
  58.7 3.0 %collective-permute-start.7 = (bf16[128,1024]{1,0:T(8,128)(2,1)S(1)}, bf16[128,1024]{1,0:T(8,128)(2,1)S(1)}, u32[]{:S(2)}, u32[]{:S(2)}) collective-permute-start(bf16[128,1024]{1,0:T(8,128)(2,1)S(1)} %collective-permute-done.6.refs_8_), channel_id=1, source_target_pairs={{0,32},{16,240},{32,64},{48,16},{64,96},{80,48},{96,128},{112,80},... | collective-permute-start | bytes 786440 | tf_op jit(solution)/shard_map/ppermute | solution.py:248
  62.2 2.4 %collective-permute-start.9 = (bf16[128,1024]{1,0:T(8,128)(2,1)S(1)}, bf16[128,1024]{1,0:T(8,128)(2,1)S(1)}, u32[]{:S(2)}, u32[]{:S(2)}) collective-permute-start(bf16[128,1024]{1,0:T(8,128)(2,1)S(1)} %collective-permute-done.3.refs_0_), channel_id=1, source_target_pairs={{0,32},{16,240},{32,64},{48,16},{64,96},{80,48},{96,128},{112,80},... | collective-permute-start | bytes 786440 | tf_op jit(solution)/shard_map/ppermute | solution.py:248
  64.6 1.8 %collective-permute-start.4 = (bf16[128,1024]{1,0:T(8,128)(2,1)S(1)}, bf16[128,1024]{1,0:T(8,128)(2,1)S(1)}, u32[]{:S(2)}, u32[]{:S(2)}) collective-permute-start(bf16[128,1024]{1,0:T(8,128)(2,1)S(1)} %collective-permute-done.3.refs_0_), channel_id=1, source_target_pairs={{0,16},{16,0},{32,48},{48,32},{64,80},{80,64},{96,112},{112,96},{1... | collective-permute-start | bytes 786440 | tf_op jit(solution)/shard_map/ppermute | solution.py:287
  66.4 2.7 %collective-permute-start.8 = (bf16[128,1024]{1,0:T(8,128)(2,1)S(1)}, bf16[128,1024]{1,0:T(8,128)(2,1)S(1)}, u32[]{:S(2)}, u32[]{:S(2)}) collective-permute-start(bf16[128,1024]{1,0:T(8,128)(2,1)S(1)} %collective-permute-done.7.refs_2_), channel_id=1, source_target_pairs={{0,16},{16,0},{32,48},{48,32},{64,80},{80,64},{96,112},{112,96},{1... | collective-permute-start | bytes 786440 | tf_op jit(solution)/shard_map/ppermute | solution.py:287
  69.8 4.7 %project.2.refs_6_ = bf16[2048,512]{1,0:T(8,128)(2,1)} custom-call(s32[1]{0:T(128)} %bitcast.me_ref, bf16[1024,512]{1,0:T(8,128)(2,1)} %w_ref.3, bf16[128,1024]{1,0:T(8,128)(2,1)} %gated.1.refs_0_, bf16[128,1024]{1,0:T(8,128)(2,1)} %copy-done.1, bf16[128,1024]{1,0:T(8,128)(2,1)} %copy-done.2, bf16[128,1024]{1,0:T(8,128)(2,1)} %copy-done.8, ...), custom_call_target="tpu_custom_call" | custom-call | flops 1342177280 | bytes 3932160 | tf_op jit(solution)/shard_map/project/pallas_call | solution.py:257
  74.7 1.4 %collective-permute-done.14.refs_5_ = bf16[128,1024]{1,0:T(8,128)(2,1)S(1)} collective-permute-done((bf16[128,1024]{1,0:T(8,128)(2,1)S(1)}, bf16[128,1024]{1,0:T(8,128)(2,1)S(1)}, u32[]{:S(2)}, u32[]{:S(2)}) %collective-permute-start.14) | collective-permute-done | bytes 262176 | tf_op jit(solution)/shard_map/ppermute | solution.py:287
  76.8 3.6 %project.3 = bf16[2048,512]{1,0:T(8,128)(2,1)} custom-call(s32[1]{0:T(128)} %bitcast.me_ref, bf16[1024,512]{1,0:T(8,128)(2,1)} %w_ref.3, bf16[128,1024]{1,0:T(8,128)(2,1)} %copy-done.4, bf16[128,1024]{1,0:T(8,128)(2,1)} %copy-done.11, bf16[128,1024]{1,0:T(8,128)(2,1)} %copy-done.6, bf16[128,1024]{1,0:T(8,128)(2,1)} %copy-done.13, ...), custom_call_target="tpu_custom_call", output_to_operand_aliasing={{}: (8, {})} | custom-call | flops 805306368 | bytes 2359296 | tf_op jit(solution)/shard_map/project/pallas_call | solution.py:257
  80.5 34.5 %all_to_all.27 = bf16[16,128,512]{2,1,0:T(8,128)(2,1)S(1)} all-to-all(bf16[16,128,512]{2,1,0:T(8,128)(2,1)} %bitcast.7), channel_id=1, replica_groups=mesh['ctx'=16,'exp'=16] {'exp'}, dimensions={0} | all-to-all | bytes 4194304 | tf_op jit(solution)/shard_map/all_to_all | solution.py:291
  (50 shorter events, 6.2 us)
Async XLA Ops:
  4.1 19.1 %all-to-all-start = ((f32[16,16,128]{2,1,0:T(8,128)}), f32[16,16,128]{2,1,0:T(8,128)S(1)}, u32[]{:S(2)}, u32[]{:S(2)}) async-start(f32[16,16,128]{2,1,0:T(8,128)} %bitcast.8), calls=%async_computation | async-start | bytes 262144 | tf_op jit(solution)/shard_map/all_to_all | solution.py:223
  25.5 10.7 %all-to-all-start.1 = ((f32[16,8,128]{2,1,0:T(8,128)}), f32[16,8,128]{2,1,0:T(8,128)S(1)}, u32[]{:S(2)}, u32[]{:S(2)}) async-start(f32[16,8,128]{2,1,0:T(8,128)} %bitcast.11), calls=%async_computation.1 | async-start | bytes 131072 | tf_op jit(solution)/shard_map/all_to_all | solution.py:232
  41.3 1.7 %collective-permute-start = (bf16[128,1024]{1,0:T(8,128)(2,1)}, bf16[128,1024]{1,0:T(8,128)(2,1)S(1)}, u32[]{:S(2)}, u32[]{:S(2)}) collective-permute-start(bf16[128,1024]{1,0:T(8,128)(2,1)} %gated.1.refs_0_), channel_id=1, source_target_pairs={{0,16},{16,0},{32,48},{48,32},{64,80},{80,64},{96,112},{112,96},{1... | collective-permute-start | bytes 786440 | tf_op jit(solution)/shard_map/ppermute | solution.py:244
  43.0 26.1 %copy-start.1 = (bf16[128,1024]{1,0:T(8,128)(2,1)}, bf16[128,1024]{1,0:T(8,128)(2,1)S(1)}, u32[]{:S(2)}) copy-start(bf16[128,1024]{1,0:T(8,128)(2,1)S(1)} %collective-permute-done.refs_1_) | copy-start | bytes 786436
  43.0 5.7 %collective-permute-start.1 = (bf16[128,1024]{1,0:T(8,128)(2,1)}, bf16[128,1024]{1,0:T(8,128)(2,1)S(1)}, u32[]{:S(2)}, u32[]{:S(2)}) collective-permute-start(bf16[128,1024]{1,0:T(8,128)(2,1)} %gated.1.refs_0_), channel_id=1, source_target_pairs={{0,32},{16,240},{32,64},{48,16},{64,96},{80,48},{96,128},{112,80},... | collective-permute-start | bytes 786440 | tf_op jit(solution)/shard_map/ppermute | solution.py:248
  43.8 7.8 %collective-permute-start.5 = (bf16[128,1024]{1,0:T(8,128)(2,1)S(1)}, bf16[128,1024]{1,0:T(8,128)(2,1)S(1)}, u32[]{:S(2)}, u32[]{:S(2)}) collective-permute-start(bf16[128,1024]{1,0:T(8,128)(2,1)S(1)} %collective-permute-done.refs_1_), channel_id=1, source_target_pairs={{0,32},{16,240},{32,64},{48,16},{64,96},{80,48},{96,128},{112,80},... | collective-permute-start | bytes 786440 | tf_op jit(solution)/shard_map/ppermute | solution.py:248
  48.8 20.3 %copy-start.2 = (bf16[128,1024]{1,0:T(8,128)(2,1)}, bf16[128,1024]{1,0:T(8,128)(2,1)S(1)}, u32[]{:S(2)}) copy-start(bf16[128,1024]{1,0:T(8,128)(2,1)S(1)} %collective-permute-done.1.refs_2_) | copy-start | bytes 786436
  48.8 5.3 %collective-permute-start.2 = (bf16[128,1024]{1,0:T(8,128)(2,1)S(1)}, bf16[128,1024]{1,0:T(8,128)(2,1)S(1)}, u32[]{:S(2)}, u32[]{:S(2)}) collective-permute-start(bf16[128,1024]{1,0:T(8,128)(2,1)S(1)} %collective-permute-done.1.refs_2_), channel_id=1, source_target_pairs={{0,32},{16,240},{32,64},{48,16},{64,96},{80,48},{96,128},{112,80},... | collective-permute-start | bytes 786440 | tf_op jit(solution)/shard_map/ppermute | solution.py:248
  51.6 17.5 %copy-start.3 = (bf16[128,1024]{1,0:T(8,128)(2,1)}, bf16[128,1024]{1,0:T(8,128)(2,1)S(1)}, u32[]{:S(2)}) copy-start(bf16[128,1024]{1,0:T(8,128)(2,1)S(1)} %collective-permute-done.5.refs_4_) | copy-start | bytes 786436
  51.6 7.1 %collective-permute-start.6 = (bf16[128,1024]{1,0:T(8,128)(2,1)S(1)}, bf16[128,1024]{1,0:T(8,128)(2,1)S(1)}, u32[]{:S(2)}, u32[]{:S(2)}) collective-permute-start(bf16[128,1024]{1,0:T(8,128)(2,1)S(1)} %collective-permute-done.5.refs_4_), channel_id=1, source_target_pairs={{0,32},{16,240},{32,64},{48,16},{64,96},{80,48},{96,128},{112,80},... | collective-permute-start | bytes 786440 | tf_op jit(solution)/shard_map/ppermute | solution.py:248
  53.3 8.4 %collective-permute-start.10 = (bf16[128,1024]{1,0:T(8,128)(2,1)S(1)}, bf16[128,1024]{1,0:T(8,128)(2,1)S(1)}, u32[]{:S(2)}, u32[]{:S(2)}) collective-permute-start(bf16[128,1024]{1,0:T(8,128)(2,1)S(1)} %collective-permute-done.1.refs_2_), channel_id=1, source_target_pairs={{0,16},{16,0},{32,48},{48,32},{64,80},{80,64},{96,112},{112,96},{1... | collective-permute-start | bytes 786440 | tf_op jit(solution)/shard_map/ppermute | solution.py:280
  54.1 15.0 %copy-start.5 = (bf16[128,1024]{1,0:T(8,128)(2,1)}, bf16[128,1024]{1,0:T(8,128)(2,1)S(1)}, u32[]{:S(2)}) copy-start(bf16[128,1024]{1,0:T(8,128)(2,1)S(1)} %collective-permute-done.2.refs_6_) | copy-start | bytes 786436
  54.1 8.1 %collective-permute-start.3 = (bf16[128,1024]{1,0:T(8,128)(2,1)S(1)}, bf16[128,1024]{1,0:T(8,128)(2,1)S(1)}, u32[]{:S(2)}, u32[]{:S(2)}) collective-permute-start(bf16[128,1024]{1,0:T(8,128)(2,1)S(1)} %collective-permute-done.2.refs_6_), channel_id=1, source_target_pairs={{0,32},{16,240},{32,64},{48,16},{64,96},{80,48},{96,128},{112,80},... | collective-permute-start | bytes 786440 | tf_op jit(solution)/shard_map/ppermute | solution.py:248
  56.9 7.7 %collective-permute-start.11 = (bf16[128,1024]{1,0:T(8,128)(2,1)S(1)}, bf16[128,1024]{1,0:T(8,128)(2,1)S(1)}, u32[]{:S(2)}, u32[]{:S(2)}) collective-permute-start(bf16[128,1024]{1,0:T(8,128)(2,1)S(1)} %collective-permute-done.5.refs_4_), channel_id=1, source_target_pairs={{0,16},{16,0},{32,48},{48,32},{64,80},{80,64},{96,112},{112,96},{1... | collective-permute-start | bytes 786440 | tf_op jit(solution)/shard_map/ppermute | solution.py:280
  58.7 10.4 %copy-start.7 = (bf16[128,1024]{1,0:T(8,128)(2,1)}, bf16[128,1024]{1,0:T(8,128)(2,1)S(1)}, u32[]{:S(2)}) copy-start(bf16[128,1024]{1,0:T(8,128)(2,1)S(1)} %collective-permute-done.6.refs_8_) | copy-start | bytes 786436
  58.7 7.7 %collective-permute-start.7 = (bf16[128,1024]{1,0:T(8,128)(2,1)S(1)}, bf16[128,1024]{1,0:T(8,128)(2,1)S(1)}, u32[]{:S(2)}, u32[]{:S(2)}) collective-permute-start(bf16[128,1024]{1,0:T(8,128)(2,1)S(1)} %collective-permute-done.6.refs_8_), channel_id=1, source_target_pairs={{0,32},{16,240},{32,64},{48,16},{64,96},{80,48},{96,128},{112,80},... | collective-permute-start | bytes 786440 | tf_op jit(solution)/shard_map/ppermute | solution.py:248
  61.6 7.4 %collective-permute-start.12 = (bf16[128,1024]{1,0:T(8,128)(2,1)S(1)}, bf16[128,1024]{1,0:T(8,128)(2,1)S(1)}, u32[]{:S(2)}, u32[]{:S(2)}) collective-permute-start(bf16[128,1024]{1,0:T(8,128)(2,1)S(1)} %collective-permute-done.2.refs_6_), channel_id=1, source_target_pairs={{0,16},{16,0},{32,48},{48,32},{64,80},{80,64},{96,112},{112,96},{1... | collective-permute-start | bytes 786440 | tf_op jit(solution)/shard_map/ppermute | solution.py:280
  61.7 7.4 %collective-permute-start.13 = (bf16[128,1024]{1,0:T(8,128)(2,1)S(1)}, bf16[128,1024]{1,0:T(8,128)(2,1)}, u32[]{:S(2)}, u32[]{:S(2)}) collective-permute-start(bf16[128,1024]{1,0:T(8,128)(2,1)S(1)} %collective-permute-done.6.refs_8_), channel_id=1, source_target_pairs={{0,16},{16,0},{32,48},{48,32},{64,80},{80,64},{96,112},{112,96},{1... | collective-permute-start | bytes 786440 | tf_op jit(solution)/shard_map/ppermute | solution.py:280
  62.2 12.3 %copy-start.4 = (bf16[128,1024]{1,0:T(8,128)(2,1)}, bf16[128,1024]{1,0:T(8,128)(2,1)S(1)}, u32[]{:S(2)}) copy-start(bf16[128,1024]{1,0:T(8,128)(2,1)S(1)} %collective-permute-done.3.refs_0_) | copy-start | bytes 786436
  62.2 12.3 %collective-permute-start.9 = (bf16[128,1024]{1,0:T(8,128)(2,1)S(1)}, bf16[128,1024]{1,0:T(8,128)(2,1)S(1)}, u32[]{:S(2)}, u32[]{:S(2)}) collective-permute-start(bf16[128,1024]{1,0:T(8,128)(2,1)S(1)} %collective-permute-done.3.refs_0_), channel_id=1, source_target_pairs={{0,32},{16,240},{32,64},{48,16},{64,96},{80,48},{96,128},{112,80},... | collective-permute-start | bytes 786440 | tf_op jit(solution)/shard_map/ppermute | solution.py:248
  64.6 10.1 %collective-permute-start.4 = (bf16[128,1024]{1,0:T(8,128)(2,1)S(1)}, bf16[128,1024]{1,0:T(8,128)(2,1)S(1)}, u32[]{:S(2)}, u32[]{:S(2)}) collective-permute-start(bf16[128,1024]{1,0:T(8,128)(2,1)S(1)} %collective-permute-done.3.refs_0_), channel_id=1, source_target_pairs={{0,16},{16,0},{32,48},{48,32},{64,80},{80,64},{96,112},{112,96},{1... | collective-permute-start | bytes 786440 | tf_op jit(solution)/shard_map/ppermute | solution.py:287
  66.4 8.1 %copy-start.6 = (bf16[128,1024]{1,0:T(8,128)(2,1)}, bf16[128,1024]{1,0:T(8,128)(2,1)S(1)}, u32[]{:S(2)}) copy-start(bf16[128,1024]{1,0:T(8,128)(2,1)S(1)} %collective-permute-done.7.refs_2_) | copy-start | bytes 786436
  66.4 8.3 %collective-permute-start.8 = (bf16[128,1024]{1,0:T(8,128)(2,1)S(1)}, bf16[128,1024]{1,0:T(8,128)(2,1)S(1)}, u32[]{:S(2)}, u32[]{:S(2)}) collective-permute-start(bf16[128,1024]{1,0:T(8,128)(2,1)S(1)} %collective-permute-done.7.refs_2_), channel_id=1, source_target_pairs={{0,16},{16,0},{32,48},{48,32},{64,80},{80,64},{96,112},{112,96},{1... | collective-permute-start | bytes 786440 | tf_op jit(solution)/shard_map/ppermute | solution.py:287
  74.5 1.6 %collective-permute-start.14 = (bf16[128,1024]{1,0:T(8,128)(2,1)S(1)}, bf16[128,1024]{1,0:T(8,128)(2,1)S(1)}, u32[]{:S(2)}, u32[]{:S(2)}) collective-permute-start(bf16[128,1024]{1,0:T(8,128)(2,1)S(1)} %collective-permute-done.9.refs_4_), channel_id=1, source_target_pairs={{0,16},{16,0},{32,48},{48,32},{64,80},{80,64},{96,112},{112,96},{1... | collective-permute-start | bytes 786440 | tf_op jit(solution)/shard_map/ppermute | solution.py:287
  (9 other events, 19.4 us)

commit v6 on v5

--- a/solution.py
+++ b/solution.py
@@ -56,7 +56,7 @@
         return total + d, tuple(new)
 
     zero = jnp.zeros((groups, LANES), jnp.float32)
-    total, state = lax.fori_loop(0, rows, step, (zero, (zero,) * states), unroll=4)
+    total, state = lax.fori_loop(0, rows, step, (zero, (zero,) * states), unroll=8)
     for n in range(states):
         base = 2 * n * groups
         out_ref[base : base + groups, :] = state[n]
@@ -145,7 +145,7 @@
         y_t[at, :] = y_ref[at, :] + ((parts[0] + parts[1]) + (parts[2] + parts[3]))
         return carry
 
-    lax.fori_loop(0, rows, step, 0, unroll=4)
+    lax.fori_loop(0, rows, step, 0, unroll=8)
 
     for g in range(groups):
         y = y_t[pl.ds(g, rows, stride=groups), :]
@@ -163,21 +163,24 @@
     me = me_ref[0]
     core = lax.rem(me, 2)
     way = 2 - 4 * core
-    for i, block in enumerate(blocks):
-        joined[i * rows : (i + 1) * rows, :] = block[...]
-    result[...] = jnp.dot(
-        joined[...], w_ref[...], preferred_element_type=jnp.float32
-    ).astype(jnp.bfloat16)
     copies = []
-    for i, (step, same) in enumerate(places):
-        home = me - core + step * way + (core if same else 1 - core)
-        at = pl.multiple_of(lax.rem(home + 2 * count, count) * rows, rows)
-        copies.append(
-            pltpu.make_async_copy(
-                result.at[pl.ds(i * rows, rows), :], out_ref.at[pl.ds(at, rows), :], sems.at[i]
+    for first in range(0, units, 2):
+        piece = slice(first * rows, (first + 2) * rows)
+        joined[first * rows : (first + 1) * rows, :] = blocks[first][...]
+        joined[(first + 1) * rows : (first + 2) * rows, :] = blocks[first + 1][...]
+        result[piece, :] = jnp.dot(
+            joined[piece, :], w_ref[...], preferred_element_type=jnp.float32
+        ).astype(jnp.bfloat16)
+        for i in (first, first + 1):
+            step, same = places[i]
+            home = me - core + step * way + (core if same else 1 - core)
+            at = pl.multiple_of(lax.rem(home + 2 * count, count) * rows, rows)
+            copies.append(
+                pltpu.make_async_copy(
+                    result.at[pl.ds(i * rows, rows), :], out_ref.at[pl.ds(at, rows), :], sems.at[i]
+                )
             )
-        )
-        copies[-1].start()
+            copies[-1].start()
     for copy in copies:
         copy.wait()
 

time: 116 us -> 116 us (level)
  no operation moved by 1% of the time
where the time goes in v6:
time: 116 us; the launch traced here: 115 us
  starting transfers between devices  34.7 us (30%)
  blocking collectives  34.7 us (30%)
  Pallas kernels  23.4 us (20%)
  waiting for transfers between devices  18.7 us (16%)
  local copies, waits for them, and re-layouts  2.67 us (2%)
    all_to_all x1, blocking collectives, body(): lax.all_to_all(terms.reshape(count, rows, width), 'exp', split_axis=0, co...  34.7 us
    ppermute x7, starting transfers between devices, body(): sources.append(lax.ppermute(sources[unit], 'ctx', ring))  13.5 us
    all_to_all x1, starting transfers between devices, body(): ends = lax.all_to_all(ends, 'ctx', split_axis=0, concat_axis=0, tiled=True)  9.98 us
    all_to_all x1, waiting for transfers between devices, body(): ends = lax.all_to_all(ends, 'ctx', split_axis=0, concat_axis=0, tiled=True)  9.17 us
    pallas_call x2, Pallas kernels, project(): pl.pallas_call(functools.partial(project_kernel, tuple(places)), out_shap...  7.7 us
    pallas_call x1, Pallas kernels, body(): pl.pallas_call(local_kernel, out_shape=(tokens, tokens, jax.ShapeDtypeStr...  5.81 us
    ppermute x7, waiting for transfers between devices, body(): sources.append(lax.ppermute(sources[unit], 'ctx', ring))  5.1 us
    ppermute x3, starting transfers between devices, body(): blocks += [value, lax.ppermute(value, 'ctx', trade)]  4.65 us
  transfers between devices with their start and end apart: 17, of which 7 were waited for; matrix products, arithmetic and copies ran while one was open for 0% of the time, Pallas kernels for 9%

profile of v6, /device:TPU:1, one launch (start us, length us, event | category | flops | bytes accessed | tf_op | source)
XLA Modules:
  0.0 115.3 jit_solution(15151488151464318384)
XLA Ops:
  0.0 4.0 %end_state.1 = f32[256,128]{1,0:T(8,128)} custom-call(f32[128,1024]{1,0:T(8,128)} %delta_ref.3, bf16[128,1024]{1,0:T(8,128)(2,1)} %u_ref.5, f32[32,128]{1,0:T(8,128)} %bc_ref.3, f32[16,1024]{1,0:T(8,128)} %a_ref.7), custom_call_target="tpu_custom_call" | custom-call | tf_op jit(solution)/shard_map/end_state/pallas_call | solution.py:203
  4.0 10.0 %all-to-all-start = ((f32[16,16,128]{2,1,0:T(8,128)}), f32[16,16,128]{2,1,0:T(8,128)S(1)}, u32[]{:S(2)}, u32[]{:S(2)}) async-start(f32[16,16,128]{2,1,0:T(8,128)} %bitcast.8), calls=%async_computation | async-start | bytes 262144 | tf_op jit(solution)/shard_map/all_to_all | solution.py:226
  14.0 9.2 %all-to-all-done = f32[16,16,128]{2,1,0:T(8,128)S(1)} async-done(((f32[16,16,128]{2,1,0:T(8,128)}), f32[16,16,128]{2,1,0:T(8,128)S(1)}, u32[]{:S(2)}, u32[]{:S(2)}) %all-to-all-start) | async-done | bytes 131104 | tf_op jit(solution)/shard_map/all_to_all | solution.py:226
  23.8 1.6 %carry.1 = f32[128,128]{1,0:T(8,128)} custom-call(s32[1]{0:T(128)} %bitcast.me_ref, f32[256,128]{1,0:T(8,128)} %bitcast.9, f32[16,1024]{1,0:T(8,128)} %a_ref.7), custom_call_target="tpu_custom_call" | custom-call | tf_op jit(solution)/shard_map/carry/pallas_call | solution.py:227
  25.4 3.4 %all-to-all-start.1 = ((f32[16,8,128]{2,1,0:T(8,128)}), f32[16,8,128]{2,1,0:T(8,128)S(1)}, u32[]{:S(2)}, u32[]{:S(2)}) async-start(f32[16,8,128]{2,1,0:T(8,128)} %bitcast.11), calls=%async_computation.1 | async-start | bytes 131072 | tf_op jit(solution)/shard_map/all_to_all | solution.py:235
  28.8 5.8 %local.1 = (f32[1024,128]{1,0:T(8,128)}, f32[1024,128]{1,0:T(8,128)}, f32[2048,128]{1,0:T(8,128)}) custom-call(f32[128,1024]{1,0:T(8,128)} %delta_ref.3, bf16[128,1024]{1,0:T(8,128)(2,1)} %u_ref.5, f32[32,128]{1,0:T(8,128)} %bc_ref.3, f32[16,1024]{1,0:T(8,128)} %a_ref.7), custom_call_target="tpu_custom_call" | custom-call | flops 12582912 | bytes 3145728 | tf_op jit(solution)/shard_map/local/pallas_call | solution.py:213
  34.6 1.5 %all-to-all-done.1 = f32[16,8,128]{2,1,0:T(8,128)S(1)} async-done(((f32[16,8,128]{2,1,0:T(8,128)}), f32[16,8,128]{2,1,0:T(8,128)S(1)}, u32[]{:S(2)}, u32[]{:S(2)}) %all-to-all-start.1) | async-done | bytes 65568 | tf_op jit(solution)/shard_map/all_to_all | solution.py:235
  36.7 4.3 %gated.1.refs_0_ = bf16[128,1024]{1,0:T(8,128)(2,1)} custom-call(bf16[128,1024]{1,0:T(8,128)(2,1)} %u_ref.5, bf16[128,1024]{1,0:T(8,128)(2,1)} %z_ref.1, f32[16,1024]{1,0:T(8,128)} %a_ref.7, f32[1,1024]{1,0:T(1,128)} %bitcast.12, f32[128,128]{1,0:T(8,128)} %bitcast.10, f32[1024,128]{1,0:T(8,128)} %get-tuple-element.12.y_ref, ...), custom_call_target="tpu_custom_call" | custom-call | tf_op jit(solution)/shard_map/gated/pallas_call | solution.py:236
  41.3 1.5 %collective-permute-done.refs_1_ = bf16[128,1024]{1,0:T(8,128)(2,1)S(1)} collective-permute-done((bf16[128,1024]{1,0:T(8,128)(2,1)}, bf16[128,1024]{1,0:T(8,128)(2,1)S(1)}, u32[]{:S(2)}, u32[]{:S(2)}) %collective-permute-start) | collective-permute-done | bytes 262176 | tf_op jit(solution)/shard_map/ppermute | solution.py:247
  43.5 1.2 %collective-permute-start.5 = (bf16[128,1024]{1,0:T(8,128)(2,1)S(1)}, bf16[128,1024]{1,0:T(8,128)(2,1)S(1)}, u32[]{:S(2)}, u32[]{:S(2)}) collective-permute-start(bf16[128,1024]{1,0:T(8,128)(2,1)S(1)} %collective-permute-done.refs_1_), channel_id=1, source_target_pairs={{0,32},{16,240},{32,64},{48,16},{64,96},{80,48},{96,128},{112,80},... | collective-permute-start | bytes 786440 | tf_op jit(solution)/shard_map/ppermute | solution.py:251
  44.7 3.8 %collective-permute-done.1.refs_2_ = bf16[128,1024]{1,0:T(8,128)(2,1)S(1)} collective-permute-done((bf16[128,1024]{1,0:T(8,128)(2,1)}, bf16[128,1024]{1,0:T(8,128)(2,1)S(1)}, u32[]{:S(2)}, u32[]{:S(2)}) %collective-permute-start.1) | collective-permute-done | bytes 262176 | tf_op jit(solution)/shard_map/ppermute | solution.py:251
  48.5 1.7 %collective-permute-start.2 = (bf16[128,1024]{1,0:T(8,128)(2,1)S(1)}, bf16[128,1024]{1,0:T(8,128)(2,1)S(1)}, u32[]{:S(2)}, u32[]{:S(2)}) collective-permute-start(bf16[128,1024]{1,0:T(8,128)(2,1)S(1)} %collective-permute-done.1.refs_2_), channel_id=1, source_target_pairs={{0,32},{16,240},{32,64},{48,16},{64,96},{80,48},{96,128},{112,80},... | collective-permute-start | bytes 786440 | tf_op jit(solution)/shard_map/ppermute | solution.py:251
  50.2 1.1 collective-permute-done.5.refs_4_
  51.3 1.7 %collective-permute-start.6 = (bf16[128,1024]{1,0:T(8,128)(2,1)S(1)}, bf16[128,1024]{1,0:T(8,128)(2,1)S(1)}, u32[]{:S(2)}, u32[]{:S(2)}) collective-permute-start(bf16[128,1024]{1,0:T(8,128)(2,1)S(1)} %collective-permute-done.5.refs_4_), channel_id=1, source_target_pairs={{0,32},{16,240},{32,64},{48,16},{64,96},{80,48},{96,128},{112,80},... | collective-permute-start | bytes 786440 | tf_op jit(solution)/shard_map/ppermute | solution.py:251
  53.8 2.8 %collective-permute-start.3 = (bf16[128,1024]{1,0:T(8,128)(2,1)S(1)}, bf16[128,1024]{1,0:T(8,128)(2,1)S(1)}, u32[]{:S(2)}, u32[]{:S(2)}) collective-permute-start(bf16[128,1024]{1,0:T(8,128)(2,1)S(1)} %collective-permute-done.2.refs_6_), channel_id=1, source_target_pairs={{0,32},{16,240},{32,64},{48,16},{64,96},{80,48},{96,128},{112,80},... | collective-permute-start | bytes 786440 | tf_op jit(solution)/shard_map/ppermute | solution.py:251
  56.6 1.8 %collective-permute-start.11 = (bf16[128,1024]{1,0:T(8,128)(2,1)S(1)}, bf16[128,1024]{1,0:T(8,128)(2,1)S(1)}, u32[]{:S(2)}, u32[]{:S(2)}) collective-permute-start(bf16[128,1024]{1,0:T(8,128)(2,1)S(1)} %collective-permute-done.5.refs_4_), channel_id=1, source_target_pairs={{0,16},{16,0},{32,48},{48,32},{64,80},{80,64},{96,112},{112,96},{1... | collective-permute-start | bytes 786440 | tf_op jit(solution)/shard_map/ppermute | solution.py:283
  58.4 3.0 %collective-permute-start.7 = (bf16[128,1024]{1,0:T(8,128)(2,1)S(1)}, bf16[128,1024]{1,0:T(8,128)(2,1)S(1)}, u32[]{:S(2)}, u32[]{:S(2)}) collective-permute-start(bf16[128,1024]{1,0:T(8,128)(2,1)S(1)} %collective-permute-done.6.refs_8_), channel_id=1, source_target_pairs={{0,32},{16,240},{32,64},{48,16},{64,96},{80,48},{96,128},{112,80},... | collective-permute-start | bytes 786440 | tf_op jit(solution)/shard_map/ppermute | solution.py:251
  61.9 2.4 %collective-permute-start.9 = (bf16[128,1024]{1,0:T(8,128)(2,1)S(1)}, bf16[128,1024]{1,0:T(8,128)(2,1)S(1)}, u32[]{:S(2)}, u32[]{:S(2)}) collective-permute-start(bf16[128,1024]{1,0:T(8,128)(2,1)S(1)} %collective-permute-done.3.refs_0_), channel_id=1, source_target_pairs={{0,32},{16,240},{32,64},{48,16},{64,96},{80,48},{96,128},{112,80},... | collective-permute-start | bytes 786440 | tf_op jit(solution)/shard_map/ppermute | solution.py:251
  64.3 1.8 %collective-permute-start.4 = (bf16[128,1024]{1,0:T(8,128)(2,1)S(1)}, bf16[128,1024]{1,0:T(8,128)(2,1)S(1)}, u32[]{:S(2)}, u32[]{:S(2)}) collective-permute-start(bf16[128,1024]{1,0:T(8,128)(2,1)S(1)} %collective-permute-done.3.refs_0_), channel_id=1, source_target_pairs={{0,16},{16,0},{32,48},{48,32},{64,80},{80,64},{96,112},{112,96},{1... | collective-permute-start | bytes 786440 | tf_op jit(solution)/shard_map/ppermute | solution.py:290
  66.1 2.7 %collective-permute-start.8 = (bf16[128,1024]{1,0:T(8,128)(2,1)S(1)}, bf16[128,1024]{1,0:T(8,128)(2,1)S(1)}, u32[]{:S(2)}, u32[]{:S(2)}) collective-permute-start(bf16[128,1024]{1,0:T(8,128)(2,1)S(1)} %collective-permute-done.7.refs_2_), channel_id=1, source_target_pairs={{0,16},{16,0},{32,48},{48,32},{64,80},{80,64},{96,112},{112,96},{1... | collective-permute-start | bytes 786440 | tf_op jit(solution)/shard_map/ppermute | solution.py:290
  69.5 4.3 %project.2.refs_6_ = bf16[2048,512]{1,0:T(8,128)(2,1)} custom-call(s32[1]{0:T(128)} %bitcast.me_ref, bf16[1024,512]{1,0:T(8,128)(2,1)} %w_ref.3, bf16[128,1024]{1,0:T(8,128)(2,1)} %gated.1.refs_0_, bf16[128,1024]{1,0:T(8,128)(2,1)} %copy-done.1, bf16[128,1024]{1,0:T(8,128)(2,1)} %copy-done.2, bf16[128,1024]{1,0:T(8,128)(2,1)} %copy-done.8, ...), custom_call_target="tpu_custom_call" | custom-call | flops 1342177280 | bytes 3932160 | tf_op jit(solution)/shard_map/project/pallas_call | solution.py:260
  74.0 1.5 %collective-permute-done.14.refs_5_ = bf16[128,1024]{1,0:T(8,128)(2,1)S(1)} collective-permute-done((bf16[128,1024]{1,0:T(8,128)(2,1)S(1)}, bf16[128,1024]{1,0:T(8,128)(2,1)S(1)}, u32[]{:S(2)}, u32[]{:S(2)}) %collective-permute-start.14) | collective-permute-done | bytes 262176 | tf_op jit(solution)/shard_map/ppermute | solution.py:290
  76.2 3.4 %project.3 = bf16[2048,512]{1,0:T(8,128)(2,1)} custom-call(s32[1]{0:T(128)} %bitcast.me_ref, bf16[1024,512]{1,0:T(8,128)(2,1)} %w_ref.3, bf16[128,1024]{1,0:T(8,128)(2,1)} %copy-done.4, bf16[128,1024]{1,0:T(8,128)(2,1)} %copy-done.11, bf16[128,1024]{1,0:T(8,128)(2,1)} %copy-done.6, bf16[128,1024]{1,0:T(8,128)(2,1)} %copy-done.13, ...), custom_call_target="tpu_custom_call", output_to_operand_aliasing={{}: (8, {})} | custom-call | flops 805306368 | bytes 2359296 | tf_op jit(solution)/shard_map/project/pallas_call | solution.py:260
  79.6 34.7 %all_to_all.27 = bf16[16,128,512]{2,1,0:T(8,128)(2,1)S(1)} all-to-all(bf16[16,128,512]{2,1,0:T(8,128)(2,1)} %bitcast.7), channel_id=1, replica_groups=mesh['ctx'=16,'exp'=16] {'exp'}, dimensions={0} | all-to-all | bytes 4194304 | tf_op jit(solution)/shard_map/all_to_all | solution.py:294
  (50 shorter events, 6.2 us)
Async XLA Ops:
  4.0 19.1 %all-to-all-start = ((f32[16,16,128]{2,1,0:T(8,128)}), f32[16,16,128]{2,1,0:T(8,128)S(1)}, u32[]{:S(2)}, u32[]{:S(2)}) async-start(f32[16,16,128]{2,1,0:T(8,128)} %bitcast.8), calls=%async_computation | async-start | bytes 262144 | tf_op jit(solution)/shard_map/all_to_all | solution.py:226
  25.4 10.7 %all-to-all-start.1 = ((f32[16,8,128]{2,1,0:T(8,128)}), f32[16,8,128]{2,1,0:T(8,128)S(1)}, u32[]{:S(2)}, u32[]{:S(2)}) async-start(f32[16,8,128]{2,1,0:T(8,128)} %bitcast.11), calls=%async_computation.1 | async-start | bytes 131072 | tf_op jit(solution)/shard_map/all_to_all | solution.py:235
  41.0 1.7 %collective-permute-start = (bf16[128,1024]{1,0:T(8,128)(2,1)}, bf16[128,1024]{1,0:T(8,128)(2,1)S(1)}, u32[]{:S(2)}, u32[]{:S(2)}) collective-permute-start(bf16[128,1024]{1,0:T(8,128)(2,1)} %gated.1.refs_0_), channel_id=1, source_target_pairs={{0,16},{16,0},{32,48},{48,32},{64,80},{80,64},{96,112},{112,96},{1... | collective-permute-start | bytes 786440 | tf_op jit(solution)/shard_map/ppermute | solution.py:247
  42.8 26.1 %copy-start.1 = (bf16[128,1024]{1,0:T(8,128)(2,1)}, bf16[128,1024]{1,0:T(8,128)(2,1)S(1)}, u32[]{:S(2)}) copy-start(bf16[128,1024]{1,0:T(8,128)(2,1)S(1)} %collective-permute-done.refs_1_) | copy-start | bytes 786436
  42.8 5.7 %collective-permute-start.1 = (bf16[128,1024]{1,0:T(8,128)(2,1)}, bf16[128,1024]{1,0:T(8,128)(2,1)S(1)}, u32[]{:S(2)}, u32[]{:S(2)}) collective-permute-start(bf16[128,1024]{1,0:T(8,128)(2,1)} %gated.1.refs_0_), channel_id=1, source_target_pairs={{0,32},{16,240},{32,64},{48,16},{64,96},{80,48},{96,128},{112,80},... | collective-permute-start | bytes 786440 | tf_op jit(solution)/shard_map/ppermute | solution.py:251
  43.5 7.8 %collective-permute-start.5 = (bf16[128,1024]{1,0:T(8,128)(2,1)S(1)}, bf16[128,1024]{1,0:T(8,128)(2,1)S(1)}, u32[]{:S(2)}, u32[]{:S(2)}) collective-permute-start(bf16[128,1024]{1,0:T(8,128)(2,1)S(1)} %collective-permute-done.refs_1_), channel_id=1, source_target_pairs={{0,32},{16,240},{32,64},{48,16},{64,96},{80,48},{96,128},{112,80},... | collective-permute-start | bytes 786440 | tf_op jit(solution)/shard_map/ppermute | solution.py:251
  48.5 20.3 %copy-start.2 = (bf16[128,1024]{1,0:T(8,128)(2,1)}, bf16[128,1024]{1,0:T(8,128)(2,1)S(1)}, u32[]{:S(2)}) copy-start(bf16[128,1024]{1,0:T(8,128)(2,1)S(1)} %collective-permute-done.1.refs_2_) | copy-start | bytes 786436
  48.5 5.3 %collective-permute-start.2 = (bf16[128,1024]{1,0:T(8,128)(2,1)S(1)}, bf16[128,1024]{1,0:T(8,128)(2,1)S(1)}, u32[]{:S(2)}, u32[]{:S(2)}) collective-permute-start(bf16[128,1024]{1,0:T(8,128)(2,1)S(1)} %collective-permute-done.1.refs_2_), channel_id=1, source_target_pairs={{0,32},{16,240},{32,64},{48,16},{64,96},{80,48},{96,128},{112,80},... | collective-permute-start | bytes 786440 | tf_op jit(solution)/shard_map/ppermute | solution.py:251
  51.3 17.5 %copy-start.3 = (bf16[128,1024]{1,0:T(8,128)(2,1)}, bf16[128,1024]{1,0:T(8,128)(2,1)S(1)}, u32[]{:S(2)}) copy-start(bf16[128,1024]{1,0:T(8,128)(2,1)S(1)} %collective-permute-done.5.refs_4_) | copy-start | bytes 786436
  51.3 7.1 %collective-permute-start.6 = (bf16[128,1024]{1,0:T(8,128)(2,1)S(1)}, bf16[128,1024]{1,0:T(8,128)(2,1)S(1)}, u32[]{:S(2)}, u32[]{:S(2)}) collective-permute-start(bf16[128,1024]{1,0:T(8,128)(2,1)S(1)} %collective-permute-done.5.refs_4_), channel_id=1, source_target_pairs={{0,32},{16,240},{32,64},{48,16},{64,96},{80,48},{96,128},{112,80},... | collective-permute-start | bytes 786440 | tf_op jit(solution)/shard_map/ppermute | solution.py:251
  53.0 8.4 %collective-permute-start.10 = (bf16[128,1024]{1,0:T(8,128)(2,1)S(1)}, bf16[128,1024]{1,0:T(8,128)(2,1)S(1)}, u32[]{:S(2)}, u32[]{:S(2)}) collective-permute-start(bf16[128,1024]{1,0:T(8,128)(2,1)S(1)} %collective-permute-done.1.refs_2_), channel_id=1, source_target_pairs={{0,16},{16,0},{32,48},{48,32},{64,80},{80,64},{96,112},{112,96},{1... | collective-permute-start | bytes 786440 | tf_op jit(solution)/shard_map/ppermute | solution.py:283
  53.8 15.0 %copy-start.5 = (bf16[128,1024]{1,0:T(8,128)(2,1)}, bf16[128,1024]{1,0:T(8,128)(2,1)S(1)}, u32[]{:S(2)}) copy-start(bf16[128,1024]{1,0:T(8,128)(2,1)S(1)} %collective-permute-done.2.refs_6_) | copy-start | bytes 786436
  53.8 8.1 %collective-permute-start.3 = (bf16[128,1024]{1,0:T(8,128)(2,1)S(1)}, bf16[128,1024]{1,0:T(8,128)(2,1)S(1)}, u32[]{:S(2)}, u32[]{:S(2)}) collective-permute-start(bf16[128,1024]{1,0:T(8,128)(2,1)S(1)} %collective-permute-done.2.refs_6_), channel_id=1, source_target_pairs={{0,32},{16,240},{32,64},{48,16},{64,96},{80,48},{96,128},{112,80},... | collective-permute-start | bytes 786440 | tf_op jit(solution)/shard_map/ppermute | solution.py:251
  56.6 7.7 %collective-permute-start.11 = (bf16[128,1024]{1,0:T(8,128)(2,1)S(1)}, bf16[128,1024]{1,0:T(8,128)(2,1)S(1)}, u32[]{:S(2)}, u32[]{:S(2)}) collective-permute-start(bf16[128,1024]{1,0:T(8,128)(2,1)S(1)} %collective-permute-done.5.refs_4_), channel_id=1, source_target_pairs={{0,16},{16,0},{32,48},{48,32},{64,80},{80,64},{96,112},{112,96},{1... | collective-permute-start | bytes 786440 | tf_op jit(solution)/shard_map/ppermute | solution.py:283
  58.4 10.4 %copy-start.7 = (bf16[128,1024]{1,0:T(8,128)(2,1)}, bf16[128,1024]{1,0:T(8,128)(2,1)S(1)}, u32[]{:S(2)}) copy-start(bf16[128,1024]{1,0:T(8,128)(2,1)S(1)} %collective-permute-done.6.refs_8_) | copy-start | bytes 786436
  58.4 7.7 %collective-permute-start.7 = (bf16[128,1024]{1,0:T(8,128)(2,1)S(1)}, bf16[128,1024]{1,0:T(8,128)(2,1)S(1)}, u32[]{:S(2)}, u32[]{:S(2)}) collective-permute-start(bf16[128,1024]{1,0:T(8,128)(2,1)S(1)} %collective-permute-done.6.refs_8_), channel_id=1, source_target_pairs={{0,32},{16,240},{32,64},{48,16},{64,96},{80,48},{96,128},{112,80},... | collective-permute-start | bytes 786440 | tf_op jit(solution)/shard_map/ppermute | solution.py:251
  61.4 7.4 %collective-permute-start.12 = (bf16[128,1024]{1,0:T(8,128)(2,1)S(1)}, bf16[128,1024]{1,0:T(8,128)(2,1)S(1)}, u32[]{:S(2)}, u32[]{:S(2)}) collective-permute-start(bf16[128,1024]{1,0:T(8,128)(2,1)S(1)} %collective-permute-done.2.refs_6_), channel_id=1, source_target_pairs={{0,16},{16,0},{32,48},{48,32},{64,80},{80,64},{96,112},{112,96},{1... | collective-permute-start | bytes 786440 | tf_op jit(solution)/shard_map/ppermute | solution.py:283
  61.4 7.4 %collective-permute-start.13 = (bf16[128,1024]{1,0:T(8,128)(2,1)S(1)}, bf16[128,1024]{1,0:T(8,128)(2,1)}, u32[]{:S(2)}, u32[]{:S(2)}) collective-permute-start(bf16[128,1024]{1,0:T(8,128)(2,1)S(1)} %collective-permute-done.6.refs_8_), channel_id=1, source_target_pairs={{0,16},{16,0},{32,48},{48,32},{64,80},{80,64},{96,112},{112,96},{1... | collective-permute-start | bytes 786440 | tf_op jit(solution)/shard_map/ppermute | solution.py:283
  61.9 12.0 %copy-start.4 = (bf16[128,1024]{1,0:T(8,128)(2,1)}, bf16[128,1024]{1,0:T(8,128)(2,1)S(1)}, u32[]{:S(2)}) copy-start(bf16[128,1024]{1,0:T(8,128)(2,1)S(1)} %collective-permute-done.3.refs_0_) | copy-start | bytes 786436
  61.9 12.0 %collective-permute-start.9 = (bf16[128,1024]{1,0:T(8,128)(2,1)S(1)}, bf16[128,1024]{1,0:T(8,128)(2,1)S(1)}, u32[]{:S(2)}, u32[]{:S(2)}) collective-permute-start(bf16[128,1024]{1,0:T(8,128)(2,1)S(1)} %collective-permute-done.3.refs_0_), channel_id=1, source_target_pairs={{0,32},{16,240},{32,64},{48,16},{64,96},{80,48},{96,128},{112,80},... | collective-permute-start | bytes 786440 | tf_op jit(solution)/shard_map/ppermute | solution.py:251
  64.3 9.7 %collective-permute-start.4 = (bf16[128,1024]{1,0:T(8,128)(2,1)S(1)}, bf16[128,1024]{1,0:T(8,128)(2,1)S(1)}, u32[]{:S(2)}, u32[]{:S(2)}) collective-permute-start(bf16[128,1024]{1,0:T(8,128)(2,1)S(1)} %collective-permute-done.3.refs_0_), channel_id=1, source_target_pairs={{0,16},{16,0},{32,48},{48,32},{64,80},{80,64},{96,112},{112,96},{1... | collective-permute-start | bytes 786440 | tf_op jit(solution)/shard_map/ppermute | solution.py:290
  66.1 7.8 %copy-start.6 = (bf16[128,1024]{1,0:T(8,128)(2,1)}, bf16[128,1024]{1,0:T(8,128)(2,1)S(1)}, u32[]{:S(2)}) copy-start(bf16[128,1024]{1,0:T(8,128)(2,1)S(1)} %collective-permute-done.7.refs_2_) | copy-start | bytes 786436
  66.1 7.9 %collective-permute-start.8 = (bf16[128,1024]{1,0:T(8,128)(2,1)S(1)}, bf16[128,1024]{1,0:T(8,128)(2,1)S(1)}, u32[]{:S(2)}, u32[]{:S(2)}) collective-permute-start(bf16[128,1024]{1,0:T(8,128)(2,1)S(1)} %collective-permute-done.7.refs_2_), channel_id=1, source_target_pairs={{0,16},{16,0},{32,48},{48,32},{64,80},{80,64},{96,112},{112,96},{1... | collective-permute-start | bytes 786440 | tf_op jit(solution)/shard_map/ppermute | solution.py:290
  73.9 1.6 %collective-permute-start.14 = (bf16[128,1024]{1,0:T(8,128)(2,1)S(1)}, bf16[128,1024]{1,0:T(8,128)(2,1)S(1)}, u32[]{:S(2)}, u32[]{:S(2)}) collective-permute-start(bf16[128,1024]{1,0:T(8,128)(2,1)S(1)} %collective-permute-done.9.refs_4_), channel_id=1, source_target_pairs={{0,16},{16,0},{32,48},{48,32},{64,80},{80,64},{96,112},{112,96},{1... | collective-permute-start | bytes 786440 | tf_op jit(solution)/shard_map/ppermute | solution.py:290
  (9 other events, 19.4 us)

commit v7 on v6

--- a/solution.py
+++ b/solution.py
@@ -282,13 +282,15 @@
     for unit in range(early):
         blocks += [arrived[unit], lax.ppermute(arrived[unit], "ctx", trade)]
         places += [place_of(unit, -1), place_of(unit, 1)]
+    blocks += arrived[early:-1]
+    places += [place_of(unit, -1) for unit in range(early, len(arrived) - 1)]
     terms = project(blocks, places, [])
     last, terms = lax.optimization_barrier((arrived[-1], terms))
-    blocks, places = [], []
+    blocks, places = [last], [place_of(len(arrived) - 1, -1)]
     for unit in range(early, len(arrived)):
         value = last if unit == len(arrived) - 1 else arrived[unit]
-        blocks += [value, lax.ppermute(value, "ctx", trade)]
-        places += [place_of(unit, -1), place_of(unit, 1)]
+        blocks.append(lax.ppermute(value, "ctx", trade))
+        places.append(place_of(unit, 1))
     terms = project(blocks, places, [terms])
 
     received = lax.all_to_all(

time: 116 us -> 115 us (level)
  no operation moved by 1% of the time
where the time goes in v7:
time: 115 us
  starting transfers between devices  34.7 us (30%)
  blocking collectives  34.5 us (30%)
  Pallas kernels  23.4 us (20%)
  waiting for transfers between devices  18.7 us (16%)
  local copies, waits for them, and re-layouts  2.63 us (2%)
    all_to_all x1, blocking collectives, body(): lax.all_to_all(terms.reshape(count, rows, width), 'exp', split_axis=0, co...  34.5 us
    ppermute x7, starting transfers between devices, body(): sources.append(lax.ppermute(sources[unit], 'ctx', ring))  13.5 us
    all_to_all x1, starting transfers between devices, body(): ends = lax.all_to_all(ends, 'ctx', split_axis=0, concat_axis=0, tiled=True)  9.98 us
    all_to_all x1, waiting for transfers between devices, body(): ends = lax.all_to_all(ends, 'ctx', split_axis=0, concat_axis=0, tiled=True)  9.17 us
    pallas_call x2, Pallas kernels, project(): pl.pallas_call(functools.partial(project_kernel, tuple(places)), out_shap...  7.69 us
    pallas_call x1, Pallas kernels, body(): pl.pallas_call(local_kernel, out_shape=(tokens, tokens, jax.ShapeDtypeStr...  5.81 us
    ppermute x7, waiting for transfers between devices, body(): sources.append(lax.ppermute(sources[unit], 'ctx', ring))  5.1 us
    ppermute x3, starting transfers between devices, body(): blocks.append(lax.ppermute(value, 'ctx', trade))  4.7 us
  transfers between devices with their start and end apart: 17, of which 7 were waited for; matrix products, arithmetic and copies ran while one was open for 0% of the time, Pallas kernels for 9%

profile of v7, /device:TPU:1, one launch (start us, length us, event | category | flops | bytes accessed | tf_op | source)
XLA Modules:
  0.0 115.1 jit_solution(4258843276449789900)
XLA Ops:
  0.0 4.0 %end_state.1 = f32[256,128]{1,0:T(8,128)} custom-call(f32[128,1024]{1,0:T(8,128)} %delta_ref.3, bf16[128,1024]{1,0:T(8,128)(2,1)} %u_ref.5, f32[32,128]{1,0:T(8,128)} %bc_ref.3, f32[16,1024]{1,0:T(8,128)} %a_ref.7), custom_call_target="tpu_custom_call" | custom-call | tf_op jit(solution)/shard_map/end_state/pallas_call | solution.py:203
  4.0 10.0 %all-to-all-start = ((f32[16,16,128]{2,1,0:T(8,128)}), f32[16,16,128]{2,1,0:T(8,128)S(1)}, u32[]{:S(2)}, u32[]{:S(2)}) async-start(f32[16,16,128]{2,1,0:T(8,128)} %bitcast.8), calls=%async_computation | async-start | bytes 262144 | tf_op jit(solution)/shard_map/all_to_all | solution.py:226
  14.0 9.2 %all-to-all-done = f32[16,16,128]{2,1,0:T(8,128)S(1)} async-done(((f32[16,16,128]{2,1,0:T(8,128)}), f32[16,16,128]{2,1,0:T(8,128)S(1)}, u32[]{:S(2)}, u32[]{:S(2)}) %all-to-all-start) | async-done | bytes 131104 | tf_op jit(solution)/shard_map/all_to_all | solution.py:226
  23.8 1.6 %carry.1 = f32[128,128]{1,0:T(8,128)} custom-call(s32[1]{0:T(128)} %bitcast.me_ref, f32[256,128]{1,0:T(8,128)} %bitcast.9, f32[16,1024]{1,0:T(8,128)} %a_ref.7), custom_call_target="tpu_custom_call" | custom-call | tf_op jit(solution)/shard_map/carry/pallas_call | solution.py:227
  25.4 3.4 %all-to-all-start.1 = ((f32[16,8,128]{2,1,0:T(8,128)}), f32[16,8,128]{2,1,0:T(8,128)S(1)}, u32[]{:S(2)}, u32[]{:S(2)}) async-start(f32[16,8,128]{2,1,0:T(8,128)} %bitcast.11), calls=%async_computation.1 | async-start | bytes 131072 | tf_op jit(solution)/shard_map/all_to_all | solution.py:235
  28.8 5.8 %local.1 = (f32[1024,128]{1,0:T(8,128)}, f32[1024,128]{1,0:T(8,128)}, f32[2048,128]{1,0:T(8,128)}) custom-call(f32[128,1024]{1,0:T(8,128)} %delta_ref.3, bf16[128,1024]{1,0:T(8,128)(2,1)} %u_ref.5, f32[32,128]{1,0:T(8,128)} %bc_ref.3, f32[16,1024]{1,0:T(8,128)} %a_ref.7), custom_call_target="tpu_custom_call" | custom-call | flops 12582912 | bytes 3145728 | tf_op jit(solution)/shard_map/local/pallas_call | solution.py:213
  34.6 1.5 %all-to-all-done.1 = f32[16,8,128]{2,1,0:T(8,128)S(1)} async-done(((f32[16,8,128]{2,1,0:T(8,128)}), f32[16,8,128]{2,1,0:T(8,128)S(1)}, u32[]{:S(2)}, u32[]{:S(2)}) %all-to-all-start.1) | async-done | bytes 65568 | tf_op jit(solution)/shard_map/all_to_all | solution.py:235
  36.7 4.3 %gated.1.refs_0_ = bf16[128,1024]{1,0:T(8,128)(2,1)} custom-call(bf16[128,1024]{1,0:T(8,128)(2,1)} %u_ref.5, bf16[128,1024]{1,0:T(8,128)(2,1)} %z_ref.1, f32[16,1024]{1,0:T(8,128)} %a_ref.7, f32[1,1024]{1,0:T(1,128)} %bitcast.12, f32[128,128]{1,0:T(8,128)} %bitcast.10, f32[1024,128]{1,0:T(8,128)} %get-tuple-element.12.y_ref, ...), custom_call_target="tpu_custom_call" | custom-call | tf_op jit(solution)/shard_map/gated/pallas_call | solution.py:236
  41.3 1.5 %collective-permute-done.refs_1_ = bf16[128,1024]{1,0:T(8,128)(2,1)S(1)} collective-permute-done((bf16[128,1024]{1,0:T(8,128)(2,1)}, bf16[128,1024]{1,0:T(8,128)(2,1)S(1)}, u32[]{:S(2)}, u32[]{:S(2)}) %collective-permute-start) | collective-permute-done | bytes 262176 | tf_op jit(solution)/shard_map/ppermute | solution.py:247
  43.5 1.2 %collective-permute-start.6 = (bf16[128,1024]{1,0:T(8,128)(2,1)S(1)}, bf16[128,1024]{1,0:T(8,128)(2,1)S(1)}, u32[]{:S(2)}, u32[]{:S(2)}) collective-permute-start(bf16[128,1024]{1,0:T(8,128)(2,1)S(1)} %collective-permute-done.refs_1_), channel_id=1, source_target_pairs={{0,32},{16,240},{32,64},{48,16},{64,96},{80,48},{96,128},{112,80},... | collective-permute-start | bytes 786440 | tf_op jit(solution)/shard_map/ppermute | solution.py:251
  44.7 3.8 %collective-permute-done.1.refs_2_ = bf16[128,1024]{1,0:T(8,128)(2,1)S(1)} collective-permute-done((bf16[128,1024]{1,0:T(8,128)(2,1)}, bf16[128,1024]{1,0:T(8,128)(2,1)S(1)}, u32[]{:S(2)}, u32[]{:S(2)}) %collective-permute-start.1) | collective-permute-done | bytes 262176 | tf_op jit(solution)/shard_map/ppermute | solution.py:251
  48.5 1.7 %collective-permute-start.2 = (bf16[128,1024]{1,0:T(8,128)(2,1)S(1)}, bf16[128,1024]{1,0:T(8,128)(2,1)S(1)}, u32[]{:S(2)}, u32[]{:S(2)}) collective-permute-start(bf16[128,1024]{1,0:T(8,128)(2,1)S(1)} %collective-permute-done.1.refs_2_), channel_id=1, source_target_pairs={{0,32},{16,240},{32,64},{48,16},{64,96},{80,48},{96,128},{112,80},... | collective-permute-start | bytes 786440 | tf_op jit(solution)/shard_map/ppermute | solution.py:251
  50.2 1.1 collective-permute-done.6.refs_4_
  51.3 1.7 %collective-permute-start.9 = (bf16[128,1024]{1,0:T(8,128)(2,1)S(1)}, bf16[128,1024]{1,0:T(8,128)(2,1)S(1)}, u32[]{:S(2)}, u32[]{:S(2)}) collective-permute-start(bf16[128,1024]{1,0:T(8,128)(2,1)S(1)} %collective-permute-done.6.refs_4_), channel_id=1, source_target_pairs={{0,32},{16,240},{32,64},{48,16},{64,96},{80,48},{96,128},{112,80},... | collective-permute-start | bytes 786440 | tf_op jit(solution)/shard_map/ppermute | solution.py:251
  53.8 2.8 %collective-permute-start.3 = (bf16[128,1024]{1,0:T(8,128)(2,1)S(1)}, bf16[128,1024]{1,0:T(8,128)(2,1)S(1)}, u32[]{:S(2)}, u32[]{:S(2)}) collective-permute-start(bf16[128,1024]{1,0:T(8,128)(2,1)S(1)} %collective-permute-done.2.refs_6_), channel_id=1, source_target_pairs={{0,32},{16,240},{32,64},{48,16},{64,96},{80,48},{96,128},{112,80},... | collective-permute-start | bytes 786440 | tf_op jit(solution)/shard_map/ppermute | solution.py:251
  56.6 1.8 %collective-permute-start.7 = (bf16[128,1024]{1,0:T(8,128)(2,1)S(1)}, bf16[128,1024]{1,0:T(8,128)(2,1)S(1)}, u32[]{:S(2)}, u32[]{:S(2)}) collective-permute-start(bf16[128,1024]{1,0:T(8,128)(2,1)S(1)} %collective-permute-done.6.refs_4_), channel_id=1, source_target_pairs={{0,16},{16,0},{32,48},{48,32},{64,80},{80,64},{96,112},{112,96},{1... | collective-permute-start | bytes 786440 | tf_op jit(solution)/shard_map/ppermute | solution.py:283
  58.4 3.0 %collective-permute-start.11 = (bf16[128,1024]{1,0:T(8,128)(2,1)S(1)}, bf16[128,1024]{1,0:T(8,128)(2,1)S(1)}, u32[]{:S(2)}, u32[]{:S(2)}) collective-permute-start(bf16[128,1024]{1,0:T(8,128)(2,1)S(1)} %collective-permute-done.9.refs_8_), channel_id=1, source_target_pairs={{0,32},{16,240},{32,64},{48,16},{64,96},{80,48},{96,128},{112,80},... | collective-permute-start | bytes 786440 | tf_op jit(solution)/shard_map/ppermute | solution.py:251
  61.9 2.4 %collective-permute-start.4 = (bf16[128,1024]{1,0:T(8,128)(2,1)S(1)}, bf16[128,1024]{1,0:T(8,128)(2,1)S(1)}, u32[]{:S(2)}, u32[]{:S(2)}) collective-permute-start(bf16[128,1024]{1,0:T(8,128)(2,1)S(1)} %collective-permute-done.3.refs_10_), channel_id=1, source_target_pairs={{0,32},{16,240},{32,64},{48,16},{64,96},{80,48},{96,128},{112,80},... | collective-permute-start | bytes 786440 | tf_op jit(solution)/shard_map/ppermute | solution.py:251
  64.3 1.8 %collective-permute-start.12 = (bf16[128,1024]{1,0:T(8,128)(2,1)S(1)}, bf16[128,1024]{1,0:T(8,128)(2,1)S(1)}, u32[]{:S(2)}, u32[]{:S(2)}) collective-permute-start(bf16[128,1024]{1,0:T(8,128)(2,1)S(1)} %collective-permute-done.3.refs_10_), channel_id=1, source_target_pairs={{0,16},{16,0},{32,48},{48,32},{64,80},{80,64},{96,112},{112,96},{1... | collective-permute-start | bytes 786440 | tf_op jit(solution)/shard_map/ppermute | solution.py:292
  66.1 2.7 %collective-permute-start.13 = (bf16[128,1024]{1,0:T(8,128)(2,1)S(1)}, bf16[128,1024]{1,0:T(8,128)(2,1)S(1)}, u32[]{:S(2)}, u32[]{:S(2)}) collective-permute-start(bf16[128,1024]{1,0:T(8,128)(2,1)S(1)} %collective-permute-done.11.refs_11_), channel_id=1, source_target_pairs={{0,16},{16,0},{32,48},{48,32},{64,80},{80,64},{96,112},{112,96},{1... | collective-permute-start | bytes 786440 | tf_op jit(solution)/shard_map/ppermute | solution.py:292
  69.5 4.8 %project.2.refs_4_ = bf16[2048,512]{1,0:T(8,128)(2,1)} custom-call(s32[1]{0:T(128)} %bitcast.me_ref, bf16[1024,512]{1,0:T(8,128)(2,1)} %w_ref.3, bf16[128,1024]{1,0:T(8,128)(2,1)} %gated.1.refs_0_, bf16[128,1024]{1,0:T(8,128)(2,1)} %copy-done.1, bf16[128,1024]{1,0:T(8,128)(2,1)} %copy-done.2, bf16[128,1024]{1,0:T(8,128)(2,1)} %copy-done.7, ...), custom_call_target="tpu_custom_call" | custom-call | flops 1610612736 | bytes 4718592 | tf_op jit(solution)/shard_map/project/pallas_call | solution.py:260
  74.5 1.4 %collective-permute-done.14.refs_3_ = bf16[128,1024]{1,0:T(8,128)(2,1)S(1)} collective-permute-done((bf16[128,1024]{1,0:T(8,128)(2,1)S(1)}, bf16[128,1024]{1,0:T(8,128)(2,1)S(1)}, u32[]{:S(2)}, u32[]{:S(2)}) %collective-permute-start.14) | collective-permute-done | bytes 262176 | tf_op jit(solution)/shard_map/ppermute | solution.py:292
  76.6 2.9 %project.3 = bf16[2048,512]{1,0:T(8,128)(2,1)} custom-call(s32[1]{0:T(128)} %bitcast.me_ref, bf16[1024,512]{1,0:T(8,128)(2,1)} %w_ref.3, bf16[128,1024]{1,0:T(8,128)(2,1)} %copy-done.10, bf16[128,1024]{1,0:T(8,128)(2,1)} %copy-done.11, bf16[128,1024]{1,0:T(8,128)(2,1)} %copy-done.13, bf16[128,1024]{1,0:T(8,128)(2,1)} %copy-done.14, ...), custom_call_target="tpu_custom_call", output_to_operand_aliasing={{}: (6, {})} | custom-call | flops 536870912 | bytes 1572864 | tf_op jit(solution)/shard_map/project/pallas_call | solution.py:260
  79.6 34.5 %all_to_all.27 = bf16[16,128,512]{2,1,0:T(8,128)(2,1)S(1)} all-to-all(bf16[16,128,512]{2,1,0:T(8,128)(2,1)} %bitcast.7), channel_id=1, replica_groups=mesh['ctx'=16,'exp'=16] {'exp'}, dimensions={0} | all-to-all | bytes 4194304 | tf_op jit(solution)/shard_map/all_to_all | solution.py:296
  (50 shorter events, 6.2 us)
Async XLA Ops:
  4.0 19.1 %all-to-all-start = ((f32[16,16,128]{2,1,0:T(8,128)}), f32[16,16,128]{2,1,0:T(8,128)S(1)}, u32[]{:S(2)}, u32[]{:S(2)}) async-start(f32[16,16,128]{2,1,0:T(8,128)} %bitcast.8), calls=%async_computation | async-start | bytes 262144 | tf_op jit(solution)/shard_map/all_to_all | solution.py:226
  25.4 10.7 %all-to-all-start.1 = ((f32[16,8,128]{2,1,0:T(8,128)}), f32[16,8,128]{2,1,0:T(8,128)S(1)}, u32[]{:S(2)}, u32[]{:S(2)}) async-start(f32[16,8,128]{2,1,0:T(8,128)} %bitcast.11), calls=%async_computation.1 | async-start | bytes 131072 | tf_op jit(solution)/shard_map/all_to_all | solution.py:235
  41.0 1.7 %collective-permute-start = (bf16[128,1024]{1,0:T(8,128)(2,1)}, bf16[128,1024]{1,0:T(8,128)(2,1)S(1)}, u32[]{:S(2)}, u32[]{:S(2)}) collective-permute-start(bf16[128,1024]{1,0:T(8,128)(2,1)} %gated.1.refs_0_), channel_id=1, source_target_pairs={{0,16},{16,0},{32,48},{48,32},{64,80},{80,64},{96,112},{112,96},{1... | collective-permute-start | bytes 786440 | tf_op jit(solution)/shard_map/ppermute | solution.py:247
  42.8 26.1 %copy-start.1 = (bf16[128,1024]{1,0:T(8,128)(2,1)}, bf16[128,1024]{1,0:T(8,128)(2,1)S(1)}, u32[]{:S(2)}) copy-start(bf16[128,1024]{1,0:T(8,128)(2,1)S(1)} %collective-permute-done.refs_1_) | copy-start | bytes 786436
  42.8 5.7 %collective-permute-start.1 = (bf16[128,1024]{1,0:T(8,128)(2,1)}, bf16[128,1024]{1,0:T(8,128)(2,1)S(1)}, u32[]{:S(2)}, u32[]{:S(2)}) collective-permute-start(bf16[128,1024]{1,0:T(8,128)(2,1)} %gated.1.refs_0_), channel_id=1, source_target_pairs={{0,32},{16,240},{32,64},{48,16},{64,96},{80,48},{96,128},{112,80},... | collective-permute-start | bytes 786440 | tf_op jit(solution)/shard_map/ppermute | solution.py:251
  43.5 7.8 %collective-permute-start.6 = (bf16[128,1024]{1,0:T(8,128)(2,1)S(1)}, bf16[128,1024]{1,0:T(8,128)(2,1)S(1)}, u32[]{:S(2)}, u32[]{:S(2)}) collective-permute-start(bf16[128,1024]{1,0:T(8,128)(2,1)S(1)} %collective-permute-done.refs_1_), channel_id=1, source_target_pairs={{0,32},{16,240},{32,64},{48,16},{64,96},{80,48},{96,128},{112,80},... | collective-permute-start | bytes 786440 | tf_op jit(solution)/shard_map/ppermute | solution.py:251
  48.5 20.3 %copy-start.2 = (bf16[128,1024]{1,0:T(8,128)(2,1)}, bf16[128,1024]{1,0:T(8,128)(2,1)S(1)}, u32[]{:S(2)}) copy-start(bf16[128,1024]{1,0:T(8,128)(2,1)S(1)} %collective-permute-done.1.refs_2_) | copy-start | bytes 786436
  48.5 5.3 %collective-permute-start.2 = (bf16[128,1024]{1,0:T(8,128)(2,1)S(1)}, bf16[128,1024]{1,0:T(8,128)(2,1)S(1)}, u32[]{:S(2)}, u32[]{:S(2)}) collective-permute-start(bf16[128,1024]{1,0:T(8,128)(2,1)S(1)} %collective-permute-done.1.refs_2_), channel_id=1, source_target_pairs={{0,32},{16,240},{32,64},{48,16},{64,96},{80,48},{96,128},{112,80},... | collective-permute-start | bytes 786440 | tf_op jit(solution)/shard_map/ppermute | solution.py:251
  51.3 17.5 %copy-start.3 = (bf16[128,1024]{1,0:T(8,128)(2,1)}, bf16[128,1024]{1,0:T(8,128)(2,1)S(1)}, u32[]{:S(2)}) copy-start(bf16[128,1024]{1,0:T(8,128)(2,1)S(1)} %collective-permute-done.6.refs_4_) | copy-start | bytes 786436
  51.3 7.1 %collective-permute-start.9 = (bf16[128,1024]{1,0:T(8,128)(2,1)S(1)}, bf16[128,1024]{1,0:T(8,128)(2,1)S(1)}, u32[]{:S(2)}, u32[]{:S(2)}) collective-permute-start(bf16[128,1024]{1,0:T(8,128)(2,1)S(1)} %collective-permute-done.6.refs_4_), channel_id=1, source_target_pairs={{0,32},{16,240},{32,64},{48,16},{64,96},{80,48},{96,128},{112,80},... | collective-permute-start | bytes 786440 | tf_op jit(solution)/shard_map/ppermute | solution.py:251
  53.0 8.4 %collective-permute-start.5 = (bf16[128,1024]{1,0:T(8,128)(2,1)S(1)}, bf16[128,1024]{1,0:T(8,128)(2,1)S(1)}, u32[]{:S(2)}, u32[]{:S(2)}) collective-permute-start(bf16[128,1024]{1,0:T(8,128)(2,1)S(1)} %collective-permute-done.1.refs_2_), channel_id=1, source_target_pairs={{0,16},{16,0},{32,48},{48,32},{64,80},{80,64},{96,112},{112,96},{1... | collective-permute-start | bytes 786440 | tf_op jit(solution)/shard_map/ppermute | solution.py:283
  53.8 15.0 %copy-start.4 = (bf16[128,1024]{1,0:T(8,128)(2,1)}, bf16[128,1024]{1,0:T(8,128)(2,1)S(1)}, u32[]{:S(2)}) copy-start(bf16[128,1024]{1,0:T(8,128)(2,1)S(1)} %collective-permute-done.2.refs_6_) | copy-start | bytes 786436
  53.8 8.1 %collective-permute-start.3 = (bf16[128,1024]{1,0:T(8,128)(2,1)S(1)}, bf16[128,1024]{1,0:T(8,128)(2,1)S(1)}, u32[]{:S(2)}, u32[]{:S(2)}) collective-permute-start(bf16[128,1024]{1,0:T(8,128)(2,1)S(1)} %collective-permute-done.2.refs_6_), channel_id=1, source_target_pairs={{0,32},{16,240},{32,64},{48,16},{64,96},{80,48},{96,128},{112,80},... | collective-permute-start | bytes 786440 | tf_op jit(solution)/shard_map/ppermute | solution.py:251
  56.6 7.7 %collective-permute-start.7 = (bf16[128,1024]{1,0:T(8,128)(2,1)S(1)}, bf16[128,1024]{1,0:T(8,128)(2,1)S(1)}, u32[]{:S(2)}, u32[]{:S(2)}) collective-permute-start(bf16[128,1024]{1,0:T(8,128)(2,1)S(1)} %collective-permute-done.6.refs_4_), channel_id=1, source_target_pairs={{0,16},{16,0},{32,48},{48,32},{64,80},{80,64},{96,112},{112,96},{1... | collective-permute-start | bytes 786440 | tf_op jit(solution)/shard_map/ppermute | solution.py:283
  58.4 10.4 %copy-start.6 = (bf16[128,1024]{1,0:T(8,128)(2,1)}, bf16[128,1024]{1,0:T(8,128)(2,1)S(1)}, u32[]{:S(2)}) copy-start(bf16[128,1024]{1,0:T(8,128)(2,1)S(1)} %collective-permute-done.9.refs_8_) | copy-start | bytes 786436
  58.4 7.7 %collective-permute-start.11 = (bf16[128,1024]{1,0:T(8,128)(2,1)S(1)}, bf16[128,1024]{1,0:T(8,128)(2,1)S(1)}, u32[]{:S(2)}, u32[]{:S(2)}) collective-permute-start(bf16[128,1024]{1,0:T(8,128)(2,1)S(1)} %collective-permute-done.9.refs_8_), channel_id=1, source_target_pairs={{0,32},{16,240},{32,64},{48,16},{64,96},{80,48},{96,128},{112,80},... | collective-permute-start | bytes 786440 | tf_op jit(solution)/shard_map/ppermute | solution.py:251
  61.4 7.4 %collective-permute-start.10 = (bf16[128,1024]{1,0:T(8,128)(2,1)S(1)}, bf16[128,1024]{1,0:T(8,128)(2,1)S(1)}, u32[]{:S(2)}, u32[]{:S(2)}) collective-permute-start(bf16[128,1024]{1,0:T(8,128)(2,1)S(1)} %collective-permute-done.9.refs_8_), channel_id=1, source_target_pairs={{0,16},{16,0},{32,48},{48,32},{64,80},{80,64},{96,112},{112,96},{1... | collective-permute-start | bytes 786440 | tf_op jit(solution)/shard_map/ppermute | solution.py:283
  61.4 7.5 %copy-start.7 = (bf16[128,1024]{1,0:T(8,128)(2,1)}, bf16[128,1024]{1,0:T(8,128)(2,1)S(1)}, u32[]{:S(2)}) copy-start(bf16[128,1024]{1,0:T(8,128)(2,1)S(1)} %collective-permute-done.5.refs_3_) | copy-start | bytes 786436
  61.4 7.4 %collective-permute-start.8 = (bf16[128,1024]{1,0:T(8,128)(2,1)S(1)}, bf16[128,1024]{1,0:T(8,128)(2,1)}, u32[]{:S(2)}, u32[]{:S(2)}) collective-permute-start(bf16[128,1024]{1,0:T(8,128)(2,1)S(1)} %collective-permute-done.2.refs_6_), channel_id=1, source_target_pairs={{0,16},{16,0},{32,48},{48,32},{64,80},{80,64},{96,112},{112,96},{1... | collective-permute-start | bytes 786440 | tf_op jit(solution)/shard_map/ppermute | solution.py:283
  61.9 7.0 %copy-start.5 = (bf16[128,1024]{1,0:T(8,128)(2,1)}, bf16[128,1024]{1,0:T(8,128)(2,1)S(1)}, u32[]{:S(2)}) copy-start(bf16[128,1024]{1,0:T(8,128)(2,1)S(1)} %collective-permute-done.3.refs_10_) | copy-start | bytes 786436
  61.9 12.4 %collective-permute-start.4 = (bf16[128,1024]{1,0:T(8,128)(2,1)S(1)}, bf16[128,1024]{1,0:T(8,128)(2,1)S(1)}, u32[]{:S(2)}, u32[]{:S(2)}) collective-permute-start(bf16[128,1024]{1,0:T(8,128)(2,1)S(1)} %collective-permute-done.3.refs_10_), channel_id=1, source_target_pairs={{0,32},{16,240},{32,64},{48,16},{64,96},{80,48},{96,128},{112,80},... | collective-permute-start | bytes 786440 | tf_op jit(solution)/shard_map/ppermute | solution.py:251
  64.3 10.2 %collective-permute-start.12 = (bf16[128,1024]{1,0:T(8,128)(2,1)S(1)}, bf16[128,1024]{1,0:T(8,128)(2,1)S(1)}, u32[]{:S(2)}, u32[]{:S(2)}) collective-permute-start(bf16[128,1024]{1,0:T(8,128)(2,1)S(1)} %collective-permute-done.3.refs_10_), channel_id=1, source_target_pairs={{0,16},{16,0},{32,48},{48,32},{64,80},{80,64},{96,112},{112,96},{1... | collective-permute-start | bytes 786440 | tf_op jit(solution)/shard_map/ppermute | solution.py:292
  66.1 8.4 %collective-permute-start.13 = (bf16[128,1024]{1,0:T(8,128)(2,1)S(1)}, bf16[128,1024]{1,0:T(8,128)(2,1)S(1)}, u32[]{:S(2)}, u32[]{:S(2)}) collective-permute-start(bf16[128,1024]{1,0:T(8,128)(2,1)S(1)} %collective-permute-done.11.refs_11_), channel_id=1, source_target_pairs={{0,16},{16,0},{32,48},{48,32},{64,80},{80,64},{96,112},{112,96},{1... | collective-permute-start | bytes 786440 | tf_op jit(solution)/shard_map/ppermute | solution.py:292
  74.3 1.6 %collective-permute-start.14 = (bf16[128,1024]{1,0:T(8,128)(2,1)S(1)}, bf16[128,1024]{1,0:T(8,128)(2,1)S(1)}, u32[]{:S(2)}, u32[]{:S(2)}) collective-permute-start(bf16[128,1024]{1,0:T(8,128)(2,1)S(1)} %collective-permute-done.4.refs_0_), channel_id=1, source_target_pairs={{0,16},{16,0},{32,48},{48,32},{64,80},{80,64},{96,112},{112,96},{1... | collective-permute-start | bytes 786440 | tf_op jit(solution)/shard_map/ppermute | solution.py:292
  (9 other events, 14.6 us)
